TPU v7x, 256 devices: a whole 4x4x8 slice. The times are simulated.
256 devices in a mesh: section: 8 (over y, x_lo), dev: 32 (over x_hi, z, core).
Axes of the slice: x: 4 (x_hi: 2, x_lo: 2; x = x_hi * 2 + x_lo), y: 4, z: 8, core: 2. Of those that a mesh axis runs over, the one named last changes fastest.
Arguments:
- patches: bfloat16 [8, 49152, 1280], P('section', 'dev'), may hold values from -6 to 6
- win_count: int32 [8, 32], P('section'), may hold values from 1 to 24, 256 in all within a row
- dest_perm: int32 [8, 32], P('section'), may hold values from 0 to 31, each once within a row
- win_groups: int32 [8, 32, 24], P('section'), may hold values from 2 to 16
- norm_gain: float32 [1280], replicated, may hold values from 0.5 to 1.5
- qkv_weight: bfloat16 [1280, 3840], P('dev')
- qkv_bias: float32 [3840], replicated, may hold values from -1.5 to 1.5
- proj_weight: bfloat16 [1280, 1280], P('dev'), may hold values from -0.15625 to 0.15625
- proj_bias: float32 [1280], replicated, may hold values from -1.5 to 1.5
- merge_gain: float32 [1280], replicated, may hold values from 0.5 to 1.5
- owner: int32 [8, 4096, 1], P('section', 'dev'), may hold values from 0 to 7; in each aligned block of 128 rows (0 to 127, 128 to 255, ..., all dimensions but the last counted through in order) at most 32 rows name the same one
Outputs:
- dispatched: bfloat16 [8, 8192, 5120], P('section', 'dev')
Inputs may be any that keep to these rules, and one draw needn't show every extreme that they name: `win_count`: within each section's row the counts sum to 8 times the devices of dev, and the largest is 24. `dest_perm`: each section's row is a permutation. `win_groups`: entries of slots past a device's count are not read. Among the 128 rows of one device, at most 32 have the same owner, and some device of every draw reaches 32.
All inputs are finite; a program needn't handle non-finite values.
Results may differ from a plain program's by a relative error of at most 0.0051.
Values may be sent and summed in bfloat16 or wider, within the bound.
No kernel may reach another device: no remote copies, remote signals or barrier semaphores. Data moves between devices by JAX's collectives and lax.ppermute only.
A program may use at most 128 MiB of HBM per device.

v0:
```python
import jax
import jax.numpy as jnp
from jax import lax
from jax.sharding import PartitionSpec as P

D = 1280
HEADS = 16
WIN = 64
DST_WIN = 8
SRC_WIN = 24


def normalize(values, gain):
    return values * lax.rsqrt(jnp.mean(values * values, axis=-1, keepdims=True) + 1e-06) * gain


def contract(inputs, shard):
    whole = lax.all_gather(shard, "dev", axis=0, tiled=True)
    return jnp.dot(inputs, whole, preferred_element_type=jnp.float32)


def encode(windows, groups, norm_gain, qkv_weight, qkv_bias, proj_weight, proj_bias, merge_gain):
    count = windows.shape[0]
    values = windows.reshape(count * WIN, D).astype(jnp.float32)
    normed = normalize(values, norm_gain).astype(jnp.bfloat16)
    triple = (contract(normed, qkv_weight) + qkv_bias).astype(jnp.bfloat16)
    triple = triple.reshape(count, WIN, 3, HEADS, D // HEADS)
    scores = jnp.einsum(
        "bqhe,bkhe->bhqk", triple[:, :, 0], triple[:, :, 1], preferred_element_type=jnp.float32
    )
    scores = scores * (D // HEADS) ** (-0.5)
    living = jnp.arange(WIN, dtype=jnp.int32)[None, :] < 4 * groups[:, None]
    scores = jnp.where(living[:, None, None, :], scores, -1e30)
    highest = jnp.max(scores, axis=-1, keepdims=True)
    powers = jnp.exp(scores - highest)
    probs = (powers / jnp.sum(powers, axis=-1, keepdims=True)).astype(jnp.bfloat16)
    mixed = jnp.einsum(
        "bhqk,bkhe->bqhe", probs, triple[:, :, 2], preferred_element_type=jnp.float32
    )
    mixed = mixed.astype(jnp.bfloat16).reshape(count * WIN, D)
    encoded = values + contract(mixed, proj_weight) + proj_bias
    final = normalize(encoded, merge_gain) * living.reshape(count * WIN, 1).astype(jnp.float32)
    return final.reshape(count * WIN // 4, 4 * D).astype(jnp.bfloat16)


def pack(merged, owners, section_count, capacity):
    sections = jnp.arange(section_count, dtype=jnp.int32)
    hits = (owners[:, None] == sections[None, :]).astype(jnp.int32)
    ranks = jnp.sum((jnp.cumsum(hits, axis=0) - hits) * hits, axis=1)
    places = owners * capacity + ranks
    chosen = places[None, :] == jnp.arange(section_count * capacity, dtype=jnp.int32)[:, None]
    ladder = jnp.arange(merged.shape[0], dtype=jnp.int32)
    indices = jnp.sum(chosen.astype(jnp.int32) * ladder[None, :], axis=1)
    filled = jnp.any(chosen, axis=1)
    return jnp.where(filled[:, None], merged[indices], jnp.zeros((), merged.dtype))


def body(
    patches,
    win_count,
    dest_perm,
    win_groups,
    norm_gain,
    qkv_weight,
    qkv_bias,
    proj_weight,
    proj_bias,
    merge_gain,
    owner,
):
    dev_count = lax.axis_size("dev")
    section_count = lax.axis_size("section")
    position = lax.axis_index("dev")
    windows = patches.reshape(SRC_WIN, WIN, D)
    counts = win_count[0]
    ladder = jnp.arange(dev_count, dtype=jnp.int32)
    before = jnp.sum(jnp.where(ladder[None, :] < ladder[:, None], counts[None, :], 0), axis=1)
    inverse = jnp.sum(
        ladder[:, None] * (dest_perm[0][:, None] == ladder[None, :]).astype(jnp.int32), axis=0
    )
    pair_slots = (SRC_WIN + dev_count - 1) // dev_count
    my_count = counts[position]
    begin_at = before[position]
    residue = jnp.mod(inverse - begin_at, dev_count)
    picked = jnp.arange(pair_slots, dtype=jnp.int32)[None, :] * dev_count + residue[:, None]
    usable = picked < my_count
    outgoing = jnp.where(
        usable[:, :, None, None],
        windows[jnp.minimum(picked, SRC_WIN - 1)],
        jnp.zeros((), windows.dtype),
    )
    outgoing = outgoing.reshape(dev_count * pair_slots * WIN, D)
    arrived = lax.all_to_all(outgoing, "dev", split_axis=0, concat_axis=0, tiled=True).reshape(
        dev_count, pair_slots, WIN, D
    )
    wanted = jnp.arange(DST_WIN, dtype=jnp.int32) * dev_count + inverse[position]
    source = jnp.sum((before[None, :] <= wanted[:, None]).astype(jnp.int32), axis=1) - 1
    within = wanted - before[source]
    balanced = arrived[source, within // dev_count]
    groups = win_groups[0][source, within]
    merged = encode(
        balanced, groups, norm_gain, qkv_weight, qkv_bias, proj_weight, proj_bias, merge_gain
    )
    merged_rows = merged.shape[0]
    capacity = 2 * merged_rows // section_count
    packed = pack(merged, owner[0, :, 0], section_count, capacity)
    delivered = lax.all_to_all(packed, "section", split_axis=0, concat_axis=0, tiled=True)
    return delivered.reshape(1, section_count * capacity, 4 * D)


def solution(mesh):
    return jax.shard_map(
        body,
        mesh=mesh,
        in_specs=(
            P("section", "dev", None),
            P("section", None),
            P("section", None),
            P("section", None, None),
            P(),
            P("dev", None),
            P(),
            P("dev", None),
            P(),
            P(),
            P("section", "dev", None),
        ),
        out_specs=P("section", "dev", None),
        check_vma=False,
    )
```

profile of v0, /device:TPU:4, one launch (start us, length us, event | category | flops | bytes accessed | tf_op | source)
XLA Modules:
  0.0 324.4 jit_solution(17619789578634482331)
XLA Ops:
  7.3 1.2 constant_dynamic-slice_fusion
  8.5 0.8 select_reduce_fusion.2
  9.9 0.7 select_reduce_fusion.3
  11.3 5.3 %gather_fusion = bf16[32,64,1280]{2,1,0:T(8,128)(2,1)} fusion(bf16[24,64,1280]{2,1,0:T(8,128)(2,1)} %bitcast.76, s32[1024]{0:T(1024)S(1)} %pad_clamp_fusion.2), kind=kCustom, calls=%fused_computation | custom fusion | bytes 10485888 | tf_op jit(solution)/shard_map/gather | solution.py:89
  16.6 1.2 fusion.16
  17.8 5.2 %broadcast_select_fusion = bf16[32,64,1280]{2,1,0:T(8,128)(2,1)} fusion(bf16[32,64,1280]{2,1,0:T(8,128)(2,1)} %gather_fusion, pred[32]{0:T(512)(128)(4,1)S(1)} %fusion.16), kind=kLoop, calls=%fused_computation.7 | loop fusion | flops 2621440 | bytes 10485792 | tf_op jit(solution)/shard_map/jit(_where)/select_n | solution.py:87
  23.0 11.8 %all-to-all-start = ((bf16[32,64,1280]{2,1,0:T(8,128)(2,1)}), bf16[32,64,1280]{2,1,0:T(8,128)(2,1)}, u32[]{:S(2)}, u32[]{:S(2)}) async-start(bf16[32,64,1280]{2,1,0:T(8,128)(2,1)} %broadcast_select_fusion), calls=%async_computation | async-start | bytes 10485760 | tf_op jit(solution)/shard_map/all_to_all | solution.py:93
  39.9 139.4 %all-to-all-done = bf16[32,64,1280]{2,1,0:T(8,128)(2,1)} async-done(((bf16[32,64,1280]{2,1,0:T(8,128)(2,1)}), bf16[32,64,1280]{2,1,0:T(8,128)(2,1)}, u32[]{:S(2)}, u32[]{:S(2)}) %all-to-all-start) | async-done | bytes 5242912 | tf_op jit(solution)/shard_map/all_to_all | solution.py:93
  179.3 3.4 %gather_fusion.2 = bf16[8,64,1280]{2,1,0:T(8,128)(2,1)S(1)} fusion(bf16[32,1,64,1280]{3,2,0,1:T(8,128)(2,1)} %bitcast.8, s32[8]{0:T(128)S(1)} %get-tuple-element.9), kind=kCustom, calls=%fused_computation.2 | custom fusion | bytes 2621504 | tf_op jit(solution)/shard_map/gather | solution.py:99
  183.6 10.9 %add_convert_fusion = bf16[512,3840]{1,0:T(8,128)(2,1)} fusion(bf16[512,1280]{1,0:T(8,128)(2,1)S(1)} %fusion.4, bf16[1280,3840]{1,0:T(8,128)(2,1)} %all-gather.3.cloned.1.call-done, f32[3840]{0:T(1024)S(1)} %copy-done.5), kind=kOutput, calls=%fused_computation.6 | convolution fusion | flops 5037096960 | bytes 15088640 | tf_op jit(solution)/shard_map/dot_general | solution.py:19
  194.4 12.9 %reshape.324 = bf16[8,64,3,16,80]{4,3,2,1,0:T(8,128)(2,1)} reshape(bf16[512,3840]{1,0:T(8,128)(2,1)} %add_convert_fusion) | data formatting | bytes 7864320 | tf_op jit(solution)/shard_map/reshape | solution.py:27
  207.3 4.5 %fusion.30 = (bf16[8,64,1,16,80]{4,3,2,1,0:T(8,128)(2,1)S(1)}, bf16[8,64,1,16,80]{4,3,2,1,0:T(8,128)(2,1)S(1)}, bf16[8,64,1,16,80]{4,3,2,1,0:T(8,128)(2,1)S(1)}) fusion(bf16[8,64,3,16,80]{4,3,2,1,0:T(8,128)(2,1)} %reshape.324), kind=kLoop, calls=%fused_computation.86 | loop fusion | bytes 7864320 | tf_op jit(solution)/shard_map/slice | solution.py:38
  211.9 1.2 fusion.6
  213.1 2.3 fusion.31
  215.4 1.2 convert_bitcast_fusion
  216.6 1.4 copy.25
  218.0 3.3 %reshape.325 = bf16[512,1280]{1,0:T(8,128)(2,1)} reshape(bf16[8,64,16,80]{3,2,1,0:T(8,128)(2,1)S(1)} %copy.25) | data formatting | bytes 2621440 | tf_op jit(solution)/shard_map/reshape | solution.py:40
  221.3 45.1 %all-gather.5.cloned.1.call-done = bf16[1280,1280]{1,0:T(8,128)(2,1)} async-done(((bf16[40,1280]{1,0:T(8,128)(2,1)}), bf16[1280,1280]{1,0:T(8,128)(2,1)}) %all-gather.5.cloned.1.call-update) | async-done | bytes 3276816 | tf_op jit(solution)/shard_map/all_gather | solution.py:18
  266.4 4.4 %multiply_reduce_fusion = (f32[512]{0:T(512)S(1)}, f32[512,1280]{1,0:T(8,128)S(1)}) fusion(f32[1280]{0:T(1024)S(1)} %copy-done.6, bf16[512,1280]{1,0:T(8,128)(2,1)} %reshape.325, bf16[1280,1280]{1,0:T(8,128)(2,1)} %all-gather.5.cloned.1.call-done, bf16[512,1280]{1,0:T(8,128)(2,1)S(1)} %bitcast.73), kind=kOutput, calls=%fused_computation.18 | convolution fusion | flops 1680997888 | bytes 8526848 | tf_op jit(solution)/shard_map/dot_general | solution.py:19
  271.2 0.8 convert_element_type.62
  272.0 3.6 %gather_fusion.4 = bf16[256,5120]{1,0:T(8,128)(2,1)} fusion(bf16[128,5120]{1,0:T(8,128)(2,1)S(1)} %convert_element_type.62, s32[1024]{0:T(1024)S(1)} %pad_clamp_fusion), kind=kCustom, calls=%fused_computation.4 | custom fusion | bytes 5243904 | tf_op jit(solution)/shard_map/gather | solution.py:55
  275.6 2.0 broadcast_select_fusion.1
  277.6 38.5 %all_to_all.12 = bf16[8,32,5120]{2,1,0:T(8,128)(2,1)S(1)} all-to-all(bf16[8,32,5120]{2,1,0:T(8,128)(2,1)S(1)} %broadcast_select_fusion.1), channel_id=1, replica_groups=mesh['section'=8,'dev'=32] {'section'}, dimensions={0} | all-to-all | bytes 5242880 | tf_op jit(solution)/shard_map/all_to_all | solution.py:107
  316.1 1.5 copy.39
  (48 shorter events, 8.3 us)
Async XLA Ops:
  6.5 31.7 %copy-start = (s32[1,32,24]{1,2,0:T(8,128)S(1)}, s32[1,32,24]{1,2,0:T(8,128)}, u32[]{:S(2)}) copy-start(s32[1,32,24]{1,2,0:T(8,128)} %param.14) | copy-start | bytes 9220
  6.5 177.0 %all-gather.3.cloned.1.call-start = ((), (), s32[]{:S(2)}) async-start(), calls=%async_computation.2 | async-start | bytes 10137600 | tf_op jit(solution)/shard_map/all_gather | solution.py:18
  22.9 16.1 %copy-start.4 = (s32[1,128,1]{1,2,0:T(1,128)S(1)}, s32[1,128,1]{1,2,0:T(1,128)}, u32[]{:S(2)}) copy-start(s32[1,128,1]{1,2,0:T(1,128)} %param.21) | copy-start | bytes 1540
  23.0 156.4 %all-to-all-start = ((bf16[32,64,1280]{2,1,0:T(8,128)(2,1)}), bf16[32,64,1280]{2,1,0:T(8,128)(2,1)}, u32[]{:S(2)}, u32[]{:S(2)}) async-start(bf16[32,64,1280]{2,1,0:T(8,128)(2,1)} %broadcast_select_fusion), calls=%async_computation | async-start | bytes 10485760 | tf_op jit(solution)/shard_map/all_to_all | solution.py:93
  34.7 231.6 %all-gather.5.cloned.1.call-start = ((), (), s32[]{:S(2)}) async-start(), calls=%async_computation.3 | async-start | bytes 3379200 | tf_op jit(solution)/shard_map/all_gather | solution.py:18
  36.9 146.2 %copy-start.2 = (f32[1280]{0:T(1024)S(1)}, f32[1280]{0:T(1024)}, u32[]{:S(2)}) copy-start(f32[1280]{0:T(1024)} %param.15) | copy-start | bytes 15364
  182.7 0.8 copy-start.5
  218.0 48.4 %copy-start.6 = (f32[1280]{0:T(1024)S(1)}, f32[1280]{0:T(1024)}, u32[]{:S(2)}) copy-start(f32[1280]{0:T(1024)} %param.19) | copy-start | bytes 15364
  266.4 4.4 %copy-start.3 = (f32[1280]{0:T(1024)S(1)}, f32[1280]{0:T(1024)}, u32[]{:S(2)}) copy-start(f32[1280]{0:T(1024)} %param.20) | copy-start | bytes 15364
  316.1 1.5 copy-start.1
Sparse Core Ops, SparseCore 0:
  10.0 172.9 all-gather.2
  185.7 80.5 all-gather.4
where the time goes:
time: 326 us; the launch traced here: 324 us
  waiting for transfers between devices  186 us (57%)
  local copies, waits for them, and re-layouts  40.6 us (12%)
  blocking collectives  38.5 us (12%)
  matrix products  17.7 us (5%)
  other arithmetic  16.2 us (5%)
  between operations  13.6 us (4%)
  starting transfers between devices  11.8 us (4%)
    all_to_all x1, waiting for transfers between devices, body(): lax.all_to_all(outgoing, 'dev', split_axis=0, concat_axis=0, tiled=True)  139 us
    all_gather x2, waiting for transfers between devices, contract(): whole = lax.all_gather(shard, 'dev', axis=0, tiled=True)  45.1 us
    all_to_all x1, blocking collectives, body(): lax.all_to_all(packed, 'section', split_axis=0, concat_axis=0, tiled=True)  38.5 us
    dot_general x2, matrix products, contract(): return jnp.dot(inputs, whole, preferred_element_type=jnp.float32)  15.2 us
    reshape x1, local copies, waits for them, and re-layouts, encode(): triple = triple.reshape(count, WIN, 3, HEADS, D // HEADS)  12.9 us
    all_to_all x1, starting transfers between devices, body(): lax.all_to_all(outgoing, 'dev', split_axis=0, concat_axis=0, tiled=True)  11.8 us
  transfers between devices with their start and end apart: 3, of which 2 were waited for; matrix products, arithmetic and copies ran while one was open for 19% of the time, Pallas kernels for 0%

commit v1 on v0

v1 whole, which is shorter than its diff:
```python
import functools

import jax
import jax.numpy as jnp
from jax import lax
from jax.experimental import pallas as pl
from jax.experimental.pallas import tpu as pltpu
from jax.sharding import Mesh
from jax.sharding import PartitionSpec as P

D = 1280
HEADS = 16
HD = 80
WIN = 64
DST_WIN = 8
SRC_WIN = 24
N_DEV = 32
N_SEC = 8
CAP = 32
ROWS = DST_WIN * WIN
MERGED = ROWS // 4
COLS = 4 * D
CHUNK = 640
HALF = 640
PAIR = 2 * WIN

F32 = jnp.float32
BF16 = jnp.bfloat16


def outgoing_kernel(place, counts, perm, patches, out, sem):
    pos = place[0]

    def add(d, total):
        return total + jnp.where(d < pos, counts[d], 0)

    begin = lax.fori_loop(0, N_DEV, add, jnp.int32(0))
    mine = counts[pos]

    def copy(i):
        slot = perm[jnp.bitwise_and(begin + i, N_DEV - 1)]
        return pltpu.make_async_copy(patches.at[i], out.at[slot], sem.at[i])

    for i in range(SRC_WIN):

        @pl.when(i < mine)
        def _(i=i):
            copy(i).start()

    for i in range(SRC_WIN):

        @pl.when(i < mine)
        def _(i=i):
            copy(i).wait()


def outgoing(place, counts, perm, patches):
    smem = pl.BlockSpec(memory_space=pltpu.SMEM)
    return pl.pallas_call(
        outgoing_kernel,
        out_shape=jax.ShapeDtypeStruct((N_DEV, WIN, D), patches.dtype),
        in_specs=[smem, smem, smem, pl.BlockSpec(memory_space=pl.ANY)],
        out_specs=pl.BlockSpec(memory_space=pl.ANY),
        scratch_shapes=[pltpu.SemaphoreType.DMA((SRC_WIN,))],
        name="outgoing",
    )(place, counts, perm, patches)


def lane_window(head):
    first = head * HD
    low = first // 128 * 128
    high = -(-(first + HD) // 128) * 128
    return first, low, high


def encode_kernel(
    n_pieces,
    place,
    counts,
    perm,
    groups,
    owner_row,
    owner_column,
    norm_gain,
    qkv_bias,
    proj_bias,
    merge_gain,
    arrived,
    *rest,
):
    pieces = rest[:n_pieces]
    out, weights, windows, normed, triple, mixed, encoded, source, live, wsem, xsem = rest[n_pieces:]
    pos = place[0]

    def weight_copy(n):
        row = pl.multiple_of(place[2 + 2 * n] * HALF, HALF)
        return pltpu.make_async_copy(
            pieces[n], weights.at[place[1 + 2 * n], pl.ds(row, HALF)], wsem.at[n]
        )

    def find(r, found):
        return jnp.where(perm[r] == pos, r, found)

    residue = lax.fori_loop(0, N_DEV, find, jnp.int32(0))

    def locate(d, begin):
        count = counts[d]
        within = jnp.bitwise_and(residue - begin, N_DEV - 1)

        @pl.when(within < count)
        def _():
            slot = lax.shift_right_logical(begin + within, 5)
            source[slot] = d
            live[slot] = 4 * groups[d * SRC_WIN + within]

        return begin + count

    lax.fori_loop(0, N_DEV, locate, jnp.int32(0))

    def window_copy(k):
        return pltpu.make_async_copy(
            arrived.at[source[k]], windows.at[pl.ds(k * WIN, WIN)], xsem.at[k]
        )

    for k in range(DST_WIN):
        window_copy(k).start()
    for n in range(n_pieces):
        weight_copy(n).start()
    for k in range(DST_WIN):
        window_copy(k).wait()
        rows = pl.ds(k * WIN, WIN)
        values = windows[rows, :].astype(F32)
        mean = jnp.mean(values * values, axis=-1, keepdims=True)
        normed[rows, :] = (values * lax.rsqrt(mean + 1e-6) * norm_gain[...]).astype(BF16)
    for n in range(n_pieces):
        weight_copy(n).wait()

    for c in range(6):
        cols = pl.ds(c * CHUNK, CHUNK)
        product = jnp.dot(normed[...], weights[c], preferred_element_type=F32)
        triple[c] = (product + qkv_bias[:, cols]).astype(BF16)

    query_at = lax.broadcasted_iota(jnp.int32, (PAIR, PAIR), 0)
    key_at = lax.broadcasted_iota(jnp.int32, (PAIR, PAIR), 1)

    def attend(pair, carry):
        rows = pl.ds(pl.multiple_of(pair * PAIR, PAIR), PAIR)
        first, second = live[2 * pair], live[2 * pair + 1]
        low = (query_at < WIN) & (key_at < first)
        high = (query_at >= WIN) & (key_at >= WIN) & (key_at < WIN + second)
        seen = low | high
        for half in range(2):
            parts = [jnp.zeros((PAIR, 128), F32) for _ in range(CHUNK // 128)]
            for head in range(HEADS // 2):
                begin, lo, hi = lane_window(head)
                lane = lo + lax.broadcasted_iota(jnp.int32, (PAIR, hi - lo), 1)
                inside = (lane >= begin) & (lane < begin + HD)
                zero = jnp.zeros((), BF16)
                q = jnp.where(inside, triple[half, rows, lo:hi], zero)
                k = triple[2 + half, rows, lo:hi]
                v = jnp.where(inside, triple[4 + half, rows, lo:hi], zero)
                scores = lax.dot_general(
                    q, k, (((1,), (1,)), ((), ())), preferred_element_type=F32
                )
                scores = jnp.where(seen, scores * HD ** (-0.5), -1e30)
                highest = jnp.max(scores, axis=-1, keepdims=True)
                powers = jnp.exp(scores - highest)
                probs = (powers / jnp.sum(powers, axis=-1, keepdims=True)).astype(BF16)
                product = jnp.dot(probs, v, preferred_element_type=F32)
                for tile in range(lo // 128, hi // 128):
                    at = tile * 128 - lo
                    parts[tile] = parts[tile] + product[:, at : at + 128]
            for tile in range(CHUNK // 128):
                at = half * CHUNK + tile * 128
                mixed[rows, at : at + 128] = parts[tile].astype(BF16)
        return carry

    lax.fori_loop(0, DST_WIN // 2, attend, 0)

    for half in range(2):
        cols = pl.ds(half * CHUNK, CHUNK)
        product = jnp.dot(mixed[...], weights[6 + half], preferred_element_type=F32)
        encoded[:, cols] = windows[:, cols].astype(F32) + product + proj_bias[:, cols]

    for k in range(DST_WIN):
        rows = pl.ds(k * WIN, WIN)
        values = encoded[rows, :]
        mean = jnp.mean(values * values, axis=-1, keepdims=True)
        alive = lax.broadcasted_iota(jnp.int32, (WIN, 1), 0) < live[k]
        scale = jnp.where(alive, lax.rsqrt(mean + 1e-6), 0.0)
        normed[rows, :] = (values * scale * merge_gain[...]).astype(BF16)

    lane = lax.broadcasted_iota(jnp.int32, (MERGED, ROWS), 1)
    earlier = lax.broadcasted_iota(jnp.int32, (MERGED, ROWS), 0) < lax.shift_right_logical(lane, 2)
    same = owner_column[...] == owner_row[...]
    rank = jnp.sum(jnp.where(same & earlier, 1, 0), axis=0, keepdims=True)
    places = owner_row[...] * CAP + rank
    chosen = lax.broadcasted_iota(jnp.int32, (N_SEC * CAP, ROWS), 0) == places
    turn = jnp.bitwise_and(lax.broadcasted_iota(jnp.int32, (N_SEC * CAP, ROWS), 1), 3)
    for p in range(4):
        pick = jnp.where(chosen & (turn == p), 1.0, 0.0).astype(BF16)
        packed = jnp.dot(pick, normed[...], preferred_element_type=F32)
        out[:, p * D : (p + 1) * D] = packed.astype(BF16)


def encode(place, counts, perm, groups, owner_row, owner_column, gain, qb, pb, mg, arrived, pieces):
    smem = pl.BlockSpec(memory_space=pltpu.SMEM)
    vmem = pl.BlockSpec(memory_space=pltpu.VMEM)
    hbm = pl.BlockSpec(memory_space=pl.ANY)
    n = len(pieces)
    return pl.pallas_call(
        functools.partial(encode_kernel, n),
        out_shape=jax.ShapeDtypeStruct((N_SEC * CAP, COLS), BF16),
        in_specs=[smem] * 4 + [vmem] * 6 + [hbm] * (1 + n),
        out_specs=vmem,
        scratch_shapes=[
            pltpu.VMEM((8, D, CHUNK), BF16),
            pltpu.VMEM((ROWS, D), BF16),
            pltpu.VMEM((ROWS, D), BF16),
            pltpu.VMEM((6, ROWS, CHUNK), BF16),
            pltpu.VMEM((ROWS, D), BF16),
            pltpu.VMEM((ROWS, D), F32),
            pltpu.SMEM((DST_WIN,), jnp.int32),
            pltpu.SMEM((DST_WIN,), jnp.int32),
            pltpu.SemaphoreType.DMA((n,)),
            pltpu.SemaphoreType.DMA((DST_WIN,)),
        ],
        compiler_params=pltpu.CompilerParams(vmem_limit_bytes=48 * 1024 * 1024),
        name="encode",
    )(place, counts, perm, groups, owner_row, owner_column, gain, qb, pb, mg, arrived, *pieces)


def shift(n, k):
    return [(i, (i + k) % n) for i in range(n)]


SWAP = [(0, 1), (1, 0)]
CROSS = [(i, 3 - i) for i in range(4)]


def gather_weights(qkv_weight, proj_weight):
    y, xh = lax.axis_index("y"), lax.axis_index("xh")
    c = lax.axis_index("c")
    send = lax.ppermute
    shard = jnp.concatenate([qkv_weight, proj_weight], axis=1)
    other = send(shard, "c", SWAP)
    slab = jnp.concatenate([jnp.where(c == 0, shard, other), jnp.where(c == 0, other, shard)], axis=0)
    own = lax.dynamic_slice(slab, (0, (2 * y + c) * CHUNK), (80, CHUNK))
    here = lax.all_to_all(jnp.broadcast_to(own[None], (8, 80, CHUNK)), "z", 0, 0, tiled=True)
    here = here.reshape(HALF, CHUNK)
    across = send(here, ("xl", "xh"), CROSS)
    up_h, down_h = send(here, "y", shift(4, 1)), send(here, "y", shift(4, -1))
    up_a, down_a = send(across, "y", shift(4, 1)), send(across, "y", shift(4, -1))
    far_h, far_a = send(up_h, "y", shift(4, 1)), send(down_a, "y", shift(4, -1))
    pieces = [here, across, up_h, down_h, up_a, down_a, far_h, far_a]
    steps = [0, 0, 1, -1, 1, -1, 2, 2]
    halves = [xh, 1 - xh, xh, xh, 1 - xh, 1 - xh, xh, 1 - xh]
    placed = []
    for core in (c, 1 - c):
        for step, half in zip(steps, halves):
            placed += [jnp.mod(y - step, 4) * 2 + core, half]
    return pieces + [send(p, "c", SWAP) for p in pieces], placed


def body(
    patches,
    win_count,
    dest_perm,
    win_groups,
    norm_gain,
    qkv_weight,
    qkv_bias,
    proj_weight,
    proj_bias,
    merge_gain,
    owner,
):
    position = lax.axis_index(("xh", "z", "c"))
    counts, perm = win_count[0], dest_perm[0]
    pieces, placed = gather_weights(qkv_weight, proj_weight)
    place = jnp.stack([position] + placed).astype(jnp.int32)
    going = outgoing(
        position.astype(jnp.int32).reshape(1), counts, perm, patches.reshape(SRC_WIN, WIN, D)
    )
    arrived = lax.all_to_all(going, ("xh", "z", "c"), split_axis=0, concat_axis=0, tiled=True)
    packed = encode(
        place,
        counts,
        perm,
        win_groups.reshape(N_DEV * SRC_WIN),
        jnp.repeat(owner.reshape(1, MERGED), 4, axis=1),
        owner.reshape(MERGED, 1),
        norm_gain.reshape(1, D),
        qkv_bias.reshape(1, 3 * D),
        proj_bias.reshape(1, D),
        merge_gain.reshape(1, D),
        arrived,
        pieces,
    )
    delivered = lax.all_to_all(packed, ("y", "xl"), split_axis=0, concat_axis=0, tiled=True)
    return delivered.reshape(1, N_SEC * CAP, COLS)


def solution(mesh):
    fine = Mesh(mesh.devices.reshape(4, 2, 2, 8, 2), ("y", "xl", "xh", "z", "c"))
    sec, dev = ("y", "xl"), ("xh", "z", "c")
    return jax.shard_map(
        body,
        mesh=fine,
        in_specs=(
            P(sec, dev, None),
            P(sec, None),
            P(sec, None),
            P(sec, None, None),
            P(),
            P(dev, None),
            P(),
            P(dev, None),
            P(),
            P(),
            P(sec, dev, None),
        ),
        out_specs=P(sec, dev, None),
        check_vma=False,
    )
```

time: 326 us -> 332 us (1.018)
  Pallas kernels: 0 us -> 86.5 us
  starting transfers between devices: 11.8 us -> 95.4 us
  waiting for transfers between devices: 186 us -> 105 us
  local copies, waits for them, and re-layouts: 40.6 us -> 5.75 us
  matrix products: 17.7 us -> 0 us
  other arithmetic: 16.2 us -> 0.08 us
  between operations: 13.6 us -> 0.26 us
    all_to_all x1 -> x2, waiting for transfers between devices: 139 us -> 28.6 us  [the longest x1 28.6 us: body(): lax.all_to_all(going, ('xh', 'z', 'c'), split_axis=0, concat_axis=0, tile...]
    pallas_call x0 -> x2, Pallas kernels: none -> 86.5 us  [the longest x1 56.8 us: outgoing(): pl.pallas_call(outgoing_kernel, out_shape=jax.ShapeDtypeStruct((N_DEV, WI...]
    ppermute x0 -> x16, waiting for transfers between devices: none -> 76.4 us  [the longest x1 37.4 us: gather_weights(): across = send(here, ('xl', 'xh'), CROSS)]
    all_to_all x1 -> x2, starting transfers between devices: 11.8 us -> 83.5 us  [the longest x1 75 us: body(): lax.all_to_all(going, ('xh', 'z', 'c'), split_axis=0, concat_axis=0, tile...]
    all_gather x2 -> x0, waiting for transfers between devices: 45.1 us -> none  [contract(): whole = lax.all_gather(shard, 'dev', axis=0, tiled=True)]
    dot_general x4 -> x0, matrix products: 17.7 us -> none  [the longest x2 15.2 us: contract(): return jnp.dot(inputs, whole, preferred_element_type=jnp.float32)]
    reshape x2 -> x6, local copies, waits for them, and re-layouts: 16.2 us -> 0.23 us  [the longest x1 0.11 us: body(): owner.reshape(MERGED, 1)]
    gather x5 -> x0, local copies, waits for them, and re-layouts: 13.5 us -> none  [the longest x1 5.26 us: body(): windows[jnp.minimum(picked, SRC_WIN - 1)]]
  transfers between devices with their start and end apart: 3 -> 18, of which waited for: 2 -> 9; matrix products, arithmetic and copies ran while one was open for 19% -> 0% of each run, Pallas kernels for 0% -> 17%
where the time goes in v1:
time: 332 us; the launch traced here: 329 us
  waiting for transfers between devices  105 us (32%)
  starting transfers between devices  95.4 us (29%)
  Pallas kernels  86.5 us (26%)
  blocking collectives  36.4 us (11%)
  local copies, waits for them, and re-layouts  5.75 us (2%)
    all_to_all x1, starting transfers between devices, body(): lax.all_to_all(going, ('xh', 'z', 'c'), split_axis=0, concat_axis=0, tile...  75 us
    pallas_call x1, Pallas kernels, outgoing(): pl.pallas_call(outgoing_kernel, out_shape=jax.ShapeDtypeStruct((N_DEV, WI...  56.8 us
    ppermute x1, waiting for transfers between devices, gather_weights(): across = send(here, ('xl', 'xh'), CROSS)  37.4 us
    all_to_all x1, blocking collectives, body(): lax.all_to_all(packed, ('y', 'xl'), split_axis=0, concat_axis=0, tiled=True)  36.4 us
    pallas_call x1, Pallas kernels, encode(): pl.pallas_call(functools.partial(encode_kernel, n), out_shape=jax.ShapeDt...  29.7 us
    all_to_all x1, waiting for transfers between devices, body(): lax.all_to_all(going, ('xh', 'z', 'c'), split_axis=0, concat_axis=0, tile...  28.6 us
    ppermute x1, waiting for transfers between devices, gather_weights(): send(up_h, 'y', shift(4, 1))  16.4 us
    ppermute x1, waiting for transfers between devices, gather_weights(): send(across, 'y', shift(4, -1))  16.3 us
  transfers between devices with their start and end apart: 18, of which 9 were waited for; matrix products, arithmetic and copies ran while one was open for 0% of the time, Pallas kernels for 17%

profile of v1, /device:TPU:4, one launch (start us, length us, event | category | flops | bytes accessed | tf_op | source)
XLA Modules:
  0.0 329.3 jit_solution(13862788125192866409)
XLA Ops:
  0.0 1.0 constant_dynamic-update-slice_fusion.1
  1.0 0.9 constant_dynamic-update-slice_fusion
  1.9 1.7 collective-permute-done
  3.7 1.0 broadcast_in_dim.13
  4.7 8.5 %all-to-all-start.1 = ((bf16[8,80,640]{2,1,0:T(8,128)(2,1)}), bf16[8,80,640]{2,1,0:T(8,128)(2,1)S(1)}, u32[]{:S(2)}, u32[]{:S(2)}) async-start(bf16[8,80,640]{2,1,0:T(8,128)(2,1)} %broadcast_in_dim.13), calls=%async_computation.1 | async-start | bytes 1638400 | tf_op jit(solution)/shard_map/all_to_all | solution.py:249
  13.2 56.8 %outgoing.1 = bf16[32,64,1280]{2,1,0:T(8,128)(2,1)} custom-call(s32[1]{0:T(128)} %bitcast.place, s32[32]{0:T(128)} %bitcast.24, s32[32]{0:T(128)} %bitcast.26, bf16[24,64,1280]{2,1,0:T(8,128)(2,1)} %bitcast.30), custom_call_target="tpu_custom_call" | custom-call | tf_op jit(solution)/shard_map/outgoing/pallas_call | solution.py:59
  70.1 75.0 %all-to-all-start = ((bf16[32,64,1280]{2,1,0:T(8,128)(2,1)}), bf16[32,64,1280]{2,1,0:T(8,128)(2,1)}, u32[]{:S(2)}, u32[]{:S(2)}) async-start(bf16[32,64,1280]{2,1,0:T(8,128)(2,1)} %outgoing.1), calls=%async_computation | async-start | bytes 10485760 | tf_op jit(solution)/shard_map/all_to_all | solution.py:285
  145.2 1.7 collective-permute-start.2
  146.9 1.7 collective-permute-start.3
  148.5 37.4 %collective-permute-done.1.rest_1_ = bf16[640,640]{1,0:T(8,128)(2,1)S(1)} collective-permute-done((bf16[640,640]{1,0:T(8,128)(2,1)S(1)}, bf16[640,640]{1,0:T(8,128)(2,1)S(1)}, u32[]{:S(2)}, u32[]{:S(2)}) %collective-permute-start.1) | collective-permute-done | bytes 819232 | tf_op jit(solution)/shard_map/ppermute | solution.py:251
  185.9 2.2 collective-permute-start.5
  188.1 1.4 collective-permute-start.6
  190.0 16.3 %collective-permute-done.5.rest_5_ = bf16[640,640]{1,0:T(8,128)(2,1)} collective-permute-done((bf16[640,640]{1,0:T(8,128)(2,1)S(1)}, bf16[640,640]{1,0:T(8,128)(2,1)}, u32[]{:S(2)}, u32[]{:S(2)}) %collective-permute-start.5) | collective-permute-done | bytes 819232 | tf_op jit(solution)/shard_map/ppermute | solution.py:253
  206.3 3.4 %collective-permute-start.7 = (bf16[640,640]{1,0:T(8,128)(2,1)}, bf16[640,640]{1,0:T(8,128)(2,1)}, u32[]{:S(2)}, u32[]{:S(2)}) collective-permute-start(bf16[640,640]{1,0:T(8,128)(2,1)} %collective-permute-done.5.rest_5_), channel_id=1, source_target_pairs={{0,192},{64,0},{128,64},{192,128},{1,193},{65,1},{129,65},{193,129... | collective-permute-start | bytes 2457608 | tf_op jit(solution)/shard_map/ppermute | solution.py:254
  209.7 0.8 collective-permute-done.4.rest_4_
  210.6 16.4 %collective-permute-done.6.rest_6_ = bf16[640,640]{1,0:T(8,128)(2,1)} collective-permute-done((bf16[640,640]{1,0:T(8,128)(2,1)S(1)}, bf16[640,640]{1,0:T(8,128)(2,1)}, u32[]{:S(2)}, u32[]{:S(2)}) %collective-permute-start.6) | collective-permute-done | bytes 819232 | tf_op jit(solution)/shard_map/ppermute | solution.py:254
  227.9 0.6 copy-done.4
  229.4 1.4 collective-permute-done.12.rest_12_
  230.8 1.2 collective-permute-done.14.rest_14_
  232.0 1.2 collective-permute-done.15.rest_15_
  233.2 28.6 %all-to-all-done.arrived = bf16[32,64,1280]{2,1,0:T(8,128)(2,1)} async-done(((bf16[32,64,1280]{2,1,0:T(8,128)(2,1)}), bf16[32,64,1280]{2,1,0:T(8,128)(2,1)}, u32[]{:S(2)}, u32[]{:S(2)}) %all-to-all-start) | async-done | bytes 5242912 | tf_op jit(solution)/shard_map/all_to_all | solution.py:285
  261.8 29.7 %encode.1 = bf16[256,5120]{1,0:T(8,128)(2,1)} custom-call(s32[33]{0:T(128)S(1)} %stack.69.place, s32[32]{0:T(128)S(1)} %bitcast.25, s32[32]{0:T(128)S(1)} %bitcast.27, s32[768]{0:T(1024)S(1)} %reshape.41.groups, s32[1,512]{1,0:T(1,128)S(1)} %broadcast_in_dim.12.owner_row, s32[128,1]{1,0:T(8,128)S(1)} %copy.14.owner_column, f32[1,1280]{1,0:T(1,128)S(1)} %reshape.44.norm_gain, ...), custom_call_target="tpu_custom_call" | custom-call | tf_op jit(solution)/shard_map/encode/pallas_call | solution.py:211
  291.5 36.4 %all_to_all.19 = bf16[8,32,5120]{2,1,0:T(8,128)(2,1)S(1)} all-to-all(bf16[8,32,5120]{2,1,0:T(8,128)(2,1)} %bitcast.28), channel_id=1, replica_groups=mesh['y'=4,'xl'=2,'xh'=2,'z'=8,'c'=2] {'y','xl'}, dimensions={0} | all-to-all | bytes 5242880 | tf_op jit(solution)/shard_map/all_to_all | solution.py:300
  327.9 1.5 copy.17
  (53 shorter events, 2.5 us)
Async XLA Ops:
  1.9 1.7 collective-permute-start
  4.7 65.4 %all-to-all-start.1 = ((bf16[8,80,640]{2,1,0:T(8,128)(2,1)}), bf16[8,80,640]{2,1,0:T(8,128)(2,1)S(1)}, u32[]{:S(2)}, u32[]{:S(2)}) async-start(bf16[8,80,640]{2,1,0:T(8,128)(2,1)} %broadcast_in_dim.13), calls=%async_computation.1 | async-start | bytes 1638400 | tf_op jit(solution)/shard_map/all_to_all | solution.py:249
  70.0 159.2 %copy-start.7 = (f32[1280]{0:T(1024)S(1)}, f32[1280]{0:T(1024)}, u32[]{:S(2)}) copy-start(f32[1280]{0:T(1024)} %param.15) | copy-start | bytes 15364
  70.0 159.2 %copy-start.5 = (f32[3840]{0:T(1024)S(1)}, f32[3840]{0:T(1024)}, u32[]{:S(2)}) copy-start(f32[3840]{0:T(1024)} %param.17) | copy-start | bytes 46084
  70.0 159.2 %copy-start.8 = (f32[1280]{0:T(1024)S(1)}, f32[1280]{0:T(1024)}, u32[]{:S(2)}) copy-start(f32[1280]{0:T(1024)} %param.19) | copy-start | bytes 15364
  70.0 159.2 %copy-start.9 = (f32[1280]{0:T(1024)S(1)}, f32[1280]{0:T(1024)}, u32[]{:S(2)}) copy-start(f32[1280]{0:T(1024)} %param.20) | copy-start | bytes 15364
  70.0 191.8 %copy-start = (s32[1,32]{1,0:T(1,128)S(1)}, s32[1,32]{1,0:T(1,128)}, u32[]{:S(2)}) copy-start(s32[1,32]{1,0:T(1,128)} %param.12) | copy-start | bytes 388
  70.0 191.8 %copy-start.1 = (s32[1,32]{1,0:T(1,128)S(1)}, s32[1,32]{1,0:T(1,128)}, u32[]{:S(2)}) copy-start(s32[1,32]{1,0:T(1,128)} %param.13) | copy-start | bytes 388
  70.1 191.7 %all-to-all-start = ((bf16[32,64,1280]{2,1,0:T(8,128)(2,1)}), bf16[32,64,1280]{2,1,0:T(8,128)(2,1)}, u32[]{:S(2)}, u32[]{:S(2)}) async-start(bf16[32,64,1280]{2,1,0:T(8,128)(2,1)} %outgoing.1), calls=%async_computation | async-start | bytes 10485760 | tf_op jit(solution)/shard_map/all_to_all | solution.py:285
  145.1 40.8 %collective-permute-start.1 = (bf16[640,640]{1,0:T(8,128)(2,1)S(1)}, bf16[640,640]{1,0:T(8,128)(2,1)S(1)}, u32[]{:S(2)}, u32[]{:S(2)}) collective-permute-start(bf16[640,640]{1,0:T(8,128)(2,1)S(1)} %bitcast.19), channel_id=1, source_target_pairs={{0,48},{16,32},{32,16},{48,0},{1,49},{17,33},{33,17},{49,1},{2,50}... | collective-permute-start | bytes 2457608 | tf_op jit(solution)/shard_map/ppermute | solution.py:251
  145.2 42.9 %collective-permute-start.2 = (bf16[640,640]{1,0:T(8,128)(2,1)S(1)}, bf16[640,640]{1,0:T(8,128)(2,1)S(1)}, u32[]{:S(2)}, u32[]{:S(2)}) collective-permute-start(bf16[640,640]{1,0:T(8,128)(2,1)S(1)} %bitcast.20), channel_id=1, source_target_pairs={{0,64},{64,128},{128,192},{192,0},{1,65},{65,129},{129,193},{193,1... | collective-permute-start | bytes 2457608 | tf_op jit(solution)/shard_map/ppermute | solution.py:252
  146.9 42.6 %collective-permute-start.3 = (bf16[640,640]{1,0:T(8,128)(2,1)S(1)}, bf16[640,640]{1,0:T(8,128)(2,1)S(1)}, u32[]{:S(2)}, u32[]{:S(2)}) collective-permute-start(bf16[640,640]{1,0:T(8,128)(2,1)S(1)} %bitcast.21), channel_id=1, source_target_pairs={{0,192},{64,0},{128,64},{192,128},{1,193},{65,1},{129,65},{193,129... | collective-permute-start | bytes 2457608 | tf_op jit(solution)/shard_map/ppermute | solution.py:252
  148.5 41.0 %collective-permute-start.8 = (bf16[640,640]{1,0:T(8,128)(2,1)S(1)}, bf16[640,640]{1,0:T(8,128)(2,1)S(1)}, u32[]{:S(2)}, u32[]{:S(2)}) collective-permute-start(bf16[640,640]{1,0:T(8,128)(2,1)S(1)} %bitcast.22), channel_id=1, source_target_pairs={{0,1},{1,0},{2,3},{3,2},{4,5},{5,4},{6,7},{7,6},{8,9},{9,8},{10,11... | collective-permute-start | bytes 2457608 | tf_op jit(solution)/shard_map/ppermute | solution.py:262
  185.9 20.4 %collective-permute-start.5 = (bf16[640,640]{1,0:T(8,128)(2,1)S(1)}, bf16[640,640]{1,0:T(8,128)(2,1)}, u32[]{:S(2)}, u32[]{:S(2)}) collective-permute-start(bf16[640,640]{1,0:T(8,128)(2,1)S(1)} %collective-permute-done.1.rest_1_), channel_id=1, source_target_pairs={{0,192},{64,0},{128,64},{192,128},{1,193},{65,1},{129,65},{193,129... | collective-permute-start | bytes 2457608 | tf_op jit(solution)/shard_map/ppermute | solution.py:253
  188.1 22.4 %collective-permute-start.4 = (bf16[640,640]{1,0:T(8,128)(2,1)S(1)}, bf16[640,640]{1,0:T(8,128)(2,1)}, u32[]{:S(2)}, u32[]{:S(2)}) collective-permute-start(bf16[640,640]{1,0:T(8,128)(2,1)S(1)} %collective-permute-done.1.rest_1_), channel_id=1, source_target_pairs={{0,64},{64,128},{128,192},{192,0},{1,65},{65,129},{129,193},{193,1... | collective-permute-start | bytes 2457608 | tf_op jit(solution)/shard_map/ppermute | solution.py:253
  188.1 38.9 %collective-permute-start.6 = (bf16[640,640]{1,0:T(8,128)(2,1)S(1)}, bf16[640,640]{1,0:T(8,128)(2,1)}, u32[]{:S(2)}, u32[]{:S(2)}) collective-permute-start(bf16[640,640]{1,0:T(8,128)(2,1)S(1)} %collective-permute-done.2.rest_2_), channel_id=1, source_target_pairs={{0,64},{64,128},{128,192},{192,0},{1,65},{65,129},{129,193},{193,1... | collective-permute-start | bytes 2457608 | tf_op jit(solution)/shard_map/ppermute | solution.py:254
  189.5 37.5 %collective-permute-start.9 = (bf16[640,640]{1,0:T(8,128)(2,1)S(1)}, bf16[640,640]{1,0:T(8,128)(2,1)S(1)}, u32[]{:S(2)}, u32[]{:S(2)}) collective-permute-start(bf16[640,640]{1,0:T(8,128)(2,1)S(1)} %collective-permute-done.1.rest_1_), channel_id=1, source_target_pairs={{0,1},{1,0},{2,3},{3,2},{4,5},{5,4},{6,7},{7,6},{8,9},{9,8},{10,11... | collective-permute-start | bytes 2457608 | tf_op jit(solution)/shard_map/ppermute | solution.py:262
  189.5 38.0 %collective-permute-start.10 = (bf16[640,640]{1,0:T(8,128)(2,1)S(1)}, bf16[640,640]{1,0:T(8,128)(2,1)S(1)}, u32[]{:S(2)}, u32[]{:S(2)}) collective-permute-start(bf16[640,640]{1,0:T(8,128)(2,1)S(1)} %collective-permute-done.2.rest_2_), channel_id=1, source_target_pairs={{0,1},{1,0},{2,3},{3,2},{4,5},{5,4},{6,7},{7,6},{8,9},{9,8},{10,11... | collective-permute-start | bytes 2457608 | tf_op jit(solution)/shard_map/ppermute | solution.py:262
  206.3 21.6 %collective-permute-start.7 = (bf16[640,640]{1,0:T(8,128)(2,1)}, bf16[640,640]{1,0:T(8,128)(2,1)}, u32[]{:S(2)}, u32[]{:S(2)}) collective-permute-start(bf16[640,640]{1,0:T(8,128)(2,1)} %collective-permute-done.5.rest_5_), channel_id=1, source_target_pairs={{0,192},{64,0},{128,64},{192,128},{1,193},{65,1},{129,65},{193,129... | collective-permute-start | bytes 2457608 | tf_op jit(solution)/shard_map/ppermute | solution.py:254
  210.5 18.8 %collective-permute-start.11 = (bf16[640,640]{1,0:T(8,128)(2,1)S(1)}, bf16[640,640]{1,0:T(8,128)(2,1)}, u32[]{:S(2)}, u32[]{:S(2)}) collective-permute-start(bf16[640,640]{1,0:T(8,128)(2,1)S(1)} %collective-permute-done.3.rest_3_), channel_id=1, source_target_pairs={{0,1},{1,0},{2,3},{3,2},{4,5},{5,4},{6,7},{7,6},{8,9},{9,8},{10,11... | collective-permute-start | bytes 2457608 | tf_op jit(solution)/shard_map/ppermute | solution.py:262
  227.0 3.8 %collective-permute-start.13 = (bf16[640,640]{1,0:T(8,128)(2,1)}, bf16[640,640]{1,0:T(8,128)(2,1)}, u32[]{:S(2)}, u32[]{:S(2)}) collective-permute-start(bf16[640,640]{1,0:T(8,128)(2,1)} %collective-permute-done.5.rest_5_), channel_id=1, source_target_pairs={{0,1},{1,0},{2,3},{3,2},{4,5},{5,4},{6,7},{7,6},{8,9},{9,8},{10,11... | collective-permute-start | bytes 2457608 | tf_op jit(solution)/shard_map/ppermute | solution.py:262
  227.0 3.8 %collective-permute-start.12 = (bf16[640,640]{1,0:T(8,128)(2,1)}, bf16[640,640]{1,0:T(8,128)(2,1)}, u32[]{:S(2)}, u32[]{:S(2)}) collective-permute-start(bf16[640,640]{1,0:T(8,128)(2,1)} %collective-permute-done.4.rest_4_), channel_id=1, source_target_pairs={{0,1},{1,0},{2,3},{3,2},{4,5},{5,4},{6,7},{7,6},{8,9},{9,8},{10,11... | collective-permute-start | bytes 2457608 | tf_op jit(solution)/shard_map/ppermute | solution.py:262
  227.5 4.5 %collective-permute-start.14 = (bf16[640,640]{1,0:T(8,128)(2,1)}, bf16[640,640]{1,0:T(8,128)(2,1)}, u32[]{:S(2)}, u32[]{:S(2)}) collective-permute-start(bf16[640,640]{1,0:T(8,128)(2,1)} %collective-permute-done.6.rest_6_), channel_id=1, source_target_pairs={{0,1},{1,0},{2,3},{3,2},{4,5},{5,4},{6,7},{7,6},{8,9},{9,8},{10,11... | collective-permute-start | bytes 2457608 | tf_op jit(solution)/shard_map/ppermute | solution.py:262
  228.4 4.7 %collective-permute-start.15 = (bf16[640,640]{1,0:T(8,128)(2,1)}, bf16[640,640]{1,0:T(8,128)(2,1)}, u32[]{:S(2)}, u32[]{:S(2)}) collective-permute-start(bf16[640,640]{1,0:T(8,128)(2,1)} %collective-permute-done.7.rest_7_), channel_id=1, source_target_pairs={{0,1},{1,0},{2,3},{3,2},{4,5},{5,4},{6,7},{7,6},{8,9},{9,8},{10,11... | collective-permute-start | bytes 2457608 | tf_op jit(solution)/shard_map/ppermute | solution.py:262
  (5 other events, 357.5 us)

commit v2 on v1

--- a/solution.py
+++ b/solution.py
@@ -28,30 +28,40 @@
 BF16 = jnp.bfloat16
 
 
-def outgoing_kernel(place, counts, perm, patches, out, sem):
+def outgoing_kernel(place, counts, perm, patches, out, staged, in_sem, out_sem):
     pos = place[0]
+    mine = counts[pos]
+
+    def load(i):
+        return pltpu.make_async_copy(patches.at[i], staged.at[i], in_sem.at[i])
+
+    for i in range(SRC_WIN):
+
+        @pl.when(i < mine)
+        def _(i=i):
+            load(i).start()
 
     def add(d, total):
         return total + jnp.where(d < pos, counts[d], 0)
 
     begin = lax.fori_loop(0, N_DEV, add, jnp.int32(0))
-    mine = counts[pos]
-
-    def copy(i):
+
+    def save(i):
         slot = perm[jnp.bitwise_and(begin + i, N_DEV - 1)]
-        return pltpu.make_async_copy(patches.at[i], out.at[slot], sem.at[i])
+        return pltpu.make_async_copy(staged.at[i], out.at[slot], out_sem.at[i])
 
     for i in range(SRC_WIN):
 
         @pl.when(i < mine)
         def _(i=i):
-            copy(i).start()
+            load(i).wait()
+            save(i).start()
 
     for i in range(SRC_WIN):
 
         @pl.when(i < mine)
         def _(i=i):
-            copy(i).wait()
+            save(i).wait()
 
 
 def outgoing(place, counts, perm, patches):
@@ -61,7 +71,12 @@
         out_shape=jax.ShapeDtypeStruct((N_DEV, WIN, D), patches.dtype),
         in_specs=[smem, smem, smem, pl.BlockSpec(memory_space=pl.ANY)],
         out_specs=pl.BlockSpec(memory_space=pl.ANY),
-        scratch_shapes=[pltpu.SemaphoreType.DMA((SRC_WIN,))],
+        scratch_shapes=[
+            pltpu.VMEM((SRC_WIN, WIN, D), patches.dtype),
+            pltpu.SemaphoreType.DMA((SRC_WIN,)),
+            pltpu.SemaphoreType.DMA((SRC_WIN,)),
+        ],
+        compiler_params=pltpu.CompilerParams(vmem_limit_bytes=16 * 1024 * 1024),
         name="outgoing",
     )(place, counts, perm, patches)
 

time: 332 us -> 230 us (0.69)
  starting transfers between devices: 95.4 us -> 26 us
  Pallas kernels: 86.5 us -> 33.2 us
  waiting for transfers between devices: 105 us -> 120 us
  local copies, waits for them, and re-layouts: 5.75 us -> 10.2 us
    all_to_all x1, starting transfers between devices: 75 us -> 5.06 us  [body(): lax.all_to_all(going, ('xh', 'z', 'c'), split_axis=0, concat_axis=0, tile...]
    pallas_call x1, Pallas kernels: 56.8 us -> 3.52 us  [outgoing(): pl.pallas_call(outgoing_kernel, out_shape=jax.ShapeDtypeStruct((N_DEV, WI...]
    all_to_all x1, waiting for transfers between devices: 0.01 us -> 16.1 us  [gather_weights(): lax.all_to_all(jnp.broadcast_to(own[None], (8, 80, CHUNK)), 'z', 0, 0, ti...]
    unnamed x25 -> x29, local copies, waits for them, and re-layouts: 3.36 us -> 7.83 us
  transfers between devices with their start and end apart: 18 -> 18, of which waited for: 9 -> 10; matrix products, arithmetic and copies ran while one was open for 0% -> 0% of each run, Pallas kernels for 17% -> 2%
where the time goes in v2:
time: 230 us; the launch traced here: 228 us
  waiting for transfers between devices  120 us (52%)
  blocking collectives  38.1 us (17%)
  Pallas kernels  33.2 us (14%)
  starting transfers between devices  26 us (11%)
  local copies, waits for them, and re-layouts  10.2 us (4%)
    all_to_all x1, blocking collectives, body(): lax.all_to_all(packed, ('y', 'xl'), split_axis=0, concat_axis=0, tiled=True)  38.1 us
    ppermute x1, waiting for transfers between devices, gather_weights(): across = send(here, ('xl', 'xh'), CROSS)  37.1 us
    pallas_call x1, Pallas kernels, encode(): pl.pallas_call(functools.partial(encode_kernel, n), out_shape=jax.ShapeDt...  29.7 us
    all_to_all x1, waiting for transfers between devices, body(): lax.all_to_all(going, ('xh', 'z', 'c'), split_axis=0, concat_axis=0, tile...  27.8 us
    ppermute x1, waiting for transfers between devices, gather_weights(): send(across, 'y', shift(4, -1))  16.7 us
    ppermute x1, waiting for transfers between devices, gather_weights(): send(up_h, 'y', shift(4, 1))  16.4 us
    all_to_all x1, waiting for transfers between devices, gather_weights(): lax.all_to_all(jnp.broadcast_to(own[None], (8, 80, CHUNK)), 'z', 0, 0, ti...  16.1 us
    all_to_all x1, starting transfers between devices, gather_weights(): lax.all_to_all(jnp.broadcast_to(own[None], (8, 80, CHUNK)), 'z', 0, 0, ti...  8.47 us
  transfers between devices with their start and end apart: 18, of which 10 were waited for; matrix products, arithmetic and copies ran while one was open for 0% of the time, Pallas kernels for 2%

profile of v2, /device:TPU:4, one launch (start us, length us, event | category | flops | bytes accessed | tf_op | source)
XLA Modules:
  0.0 228.3 jit_solution(16149946325937532286)
XLA Ops:
  0.0 1.0 constant_dynamic-update-slice_fusion.1
  1.0 0.9 constant_dynamic-update-slice_fusion
  1.9 1.7 collective-permute-done
  3.8 1.0 broadcast_in_dim.13
  4.7 8.5 %all-to-all-start.1 = ((bf16[8,80,640]{2,1,0:T(8,128)(2,1)}), bf16[8,80,640]{2,1,0:T(8,128)(2,1)S(1)}, u32[]{:S(2)}, u32[]{:S(2)}) async-start(bf16[8,80,640]{2,1,0:T(8,128)(2,1)} %broadcast_in_dim.13), calls=%async_computation.1 | async-start | bytes 1638400 | tf_op jit(solution)/shard_map/all_to_all | solution.py:264
  13.2 2.1 copy-done.1
  15.3 3.5 %outgoing.1 = bf16[32,64,1280]{2,1,0:T(8,128)(2,1)S(1)} custom-call(s32[1]{0:T(128)} %bitcast.place, s32[32]{0:T(128)S(1)} %bitcast.25, s32[32]{0:T(128)S(1)} %bitcast.27, bf16[24,64,1280]{2,1,0:T(8,128)(2,1)S(1)} %bitcast.19), custom_call_target="tpu_custom_call" | custom-call | tf_op jit(solution)/shard_map/outgoing/pallas_call | solution.py:69
  18.9 2.4 %copy-done = bf16[32,64,1280]{2,1,0:T(8,128)(2,1)} copy-done((bf16[32,64,1280]{2,1,0:T(8,128)(2,1)}, bf16[32,64,1280]{2,1,0:T(8,128)(2,1)S(1)}, u32[]{:S(2)}) %copy-start) | copy-done | bytes 5242904
  21.2 16.1 %all-to-all-done.1 = bf16[8,80,640]{2,1,0:T(8,128)(2,1)S(1)} async-done(((bf16[8,80,640]{2,1,0:T(8,128)(2,1)}), bf16[8,80,640]{2,1,0:T(8,128)(2,1)S(1)}, u32[]{:S(2)}, u32[]{:S(2)}) %all-to-all-start.1) | async-done | bytes 819232 | tf_op jit(solution)/shard_map/all_to_all | solution.py:264
  37.3 5.1 %all-to-all-start = ((bf16[32,64,1280]{2,1,0:T(8,128)(2,1)}), bf16[32,64,1280]{2,1,0:T(8,128)(2,1)}, u32[]{:S(2)}, u32[]{:S(2)}) async-start(bf16[32,64,1280]{2,1,0:T(8,128)(2,1)} %copy-done), calls=%async_computation | async-start | bytes 10485760 | tf_op jit(solution)/shard_map/all_to_all | solution.py:300
  42.8 1.6 collective-permute-start.2
  44.4 1.7 collective-permute-start.3
  46.0 37.1 %collective-permute-done.1.rest_1_ = bf16[640,640]{1,0:T(8,128)(2,1)S(1)} collective-permute-done((bf16[640,640]{1,0:T(8,128)(2,1)S(1)}, bf16[640,640]{1,0:T(8,128)(2,1)S(1)}, u32[]{:S(2)}, u32[]{:S(2)}) %collective-permute-start.1) | collective-permute-done | bytes 819232 | tf_op jit(solution)/shard_map/ppermute | solution.py:266
  83.1 3.0 %collective-permute-start.5 = (bf16[640,640]{1,0:T(8,128)(2,1)S(1)}, bf16[640,640]{1,0:T(8,128)(2,1)}, u32[]{:S(2)}, u32[]{:S(2)}) collective-permute-start(bf16[640,640]{1,0:T(8,128)(2,1)S(1)} %collective-permute-done.1.rest_1_), channel_id=1, source_target_pairs={{0,192},{64,0},{128,64},{192,128},{1,193},{65,1},{129,65},{193,129... | collective-permute-start | bytes 2457608 | tf_op jit(solution)/shard_map/ppermute | solution.py:268
  87.3 16.7 %collective-permute-done.5.rest_5_ = bf16[640,640]{1,0:T(8,128)(2,1)} collective-permute-done((bf16[640,640]{1,0:T(8,128)(2,1)S(1)}, bf16[640,640]{1,0:T(8,128)(2,1)}, u32[]{:S(2)}, u32[]{:S(2)}) %collective-permute-start.5) | collective-permute-done | bytes 819232 | tf_op jit(solution)/shard_map/ppermute | solution.py:268
  103.9 3.8 %collective-permute-start.7 = (bf16[640,640]{1,0:T(8,128)(2,1)}, bf16[640,640]{1,0:T(8,128)(2,1)}, u32[]{:S(2)}, u32[]{:S(2)}) collective-permute-start(bf16[640,640]{1,0:T(8,128)(2,1)} %collective-permute-done.5.rest_5_), channel_id=1, source_target_pairs={{0,192},{64,0},{128,64},{192,128},{1,193},{65,1},{129,65},{193,129... | collective-permute-start | bytes 2457608 | tf_op jit(solution)/shard_map/ppermute | solution.py:269
  108.6 16.4 %collective-permute-done.6.rest_6_ = bf16[640,640]{1,0:T(8,128)(2,1)} collective-permute-done((bf16[640,640]{1,0:T(8,128)(2,1)S(1)}, bf16[640,640]{1,0:T(8,128)(2,1)}, u32[]{:S(2)}, u32[]{:S(2)}) %collective-permute-start.6) | collective-permute-done | bytes 819232 | tf_op jit(solution)/shard_map/ppermute | solution.py:269
  127.4 1.4 collective-permute-done.12.rest_12_
  128.9 1.2 collective-permute-done.14.rest_14_
  130.0 1.2 collective-permute-done.15.rest_15_
  131.2 27.8 %all-to-all-done.arrived = bf16[32,64,1280]{2,1,0:T(8,128)(2,1)} async-done(((bf16[32,64,1280]{2,1,0:T(8,128)(2,1)}), bf16[32,64,1280]{2,1,0:T(8,128)(2,1)}, u32[]{:S(2)}, u32[]{:S(2)}) %all-to-all-start) | async-done | bytes 5242912 | tf_op jit(solution)/shard_map/all_to_all | solution.py:300
  159.0 29.7 %encode.1 = bf16[256,5120]{1,0:T(8,128)(2,1)} custom-call(s32[33]{0:T(128)S(1)} %stack.69.place, s32[32]{0:T(128)S(1)} %bitcast.26, s32[32]{0:T(128)S(1)} %bitcast.28, s32[768]{0:T(1024)S(1)} %reshape.41.groups, s32[1,512]{1,0:T(1,128)S(1)} %broadcast_in_dim.12.owner_row, s32[128,1]{1,0:T(8,128)S(1)} %copy.14.owner_column, f32[1,1280]{1,0:T(1,128)S(1)} %reshape.44.norm_gain, ...), custom_call_target="tpu_custom_call" | custom-call | tf_op jit(solution)/shard_map/encode/pallas_call | solution.py:226
  188.7 38.1 %all_to_all.19 = bf16[8,32,5120]{2,1,0:T(8,128)(2,1)S(1)} all-to-all(bf16[8,32,5120]{2,1,0:T(8,128)(2,1)} %bitcast.29), channel_id=1, replica_groups=mesh['y'=4,'xl'=2,'xh'=2,'z'=8,'c'=2] {'y','xl'}, dimensions={0} | all-to-all | bytes 5242880 | tf_op jit(solution)/shard_map/all_to_all | solution.py:315
  226.8 1.5 copy.17
  (57 shorter events, 4.8 us)
Async XLA Ops:
  1.9 1.7 collective-permute-start
  4.7 32.6 %all-to-all-start.1 = ((bf16[8,80,640]{2,1,0:T(8,128)(2,1)}), bf16[8,80,640]{2,1,0:T(8,128)(2,1)S(1)}, u32[]{:S(2)}, u32[]{:S(2)}) async-start(bf16[8,80,640]{2,1,0:T(8,128)(2,1)} %broadcast_in_dim.13), calls=%async_computation.1 | async-start | bytes 1638400 | tf_op jit(solution)/shard_map/all_to_all | solution.py:264
  21.2 105.5 %copy-start.8 = (s32[1,32,24]{1,2,0:T(8,128)S(1)}, s32[1,32,24]{1,2,0:T(8,128)}, u32[]{:S(2)}) copy-start(s32[1,32,24]{1,2,0:T(8,128)} %param.14) | copy-start | bytes 9220
  21.2 105.7 %copy-start.12 = (s32[1,128,1]{1,2,0:T(1,128)S(1)}, s32[1,128,1]{1,2,0:T(1,128)}, u32[]{:S(2)}) copy-start(s32[1,128,1]{1,2,0:T(1,128)} %param.21) | copy-start | bytes 1540
  21.2 106.0 %copy-start.9 = (f32[1280]{0:T(1024)S(1)}, f32[1280]{0:T(1024)}, u32[]{:S(2)}) copy-start(f32[1280]{0:T(1024)} %param.15) | copy-start | bytes 15364
  21.2 106.0 %copy-start.7 = (f32[3840]{0:T(1024)S(1)}, f32[3840]{0:T(1024)}, u32[]{:S(2)}) copy-start(f32[3840]{0:T(1024)} %param.17) | copy-start | bytes 46084
  21.2 106.0 %copy-start.10 = (f32[1280]{0:T(1024)S(1)}, f32[1280]{0:T(1024)}, u32[]{:S(2)}) copy-start(f32[1280]{0:T(1024)} %param.19) | copy-start | bytes 15364
  21.2 106.0 %copy-start.11 = (f32[1280]{0:T(1024)S(1)}, f32[1280]{0:T(1024)}, u32[]{:S(2)}) copy-start(f32[1280]{0:T(1024)} %param.20) | copy-start | bytes 15364
  37.3 121.7 %all-to-all-start = ((bf16[32,64,1280]{2,1,0:T(8,128)(2,1)}), bf16[32,64,1280]{2,1,0:T(8,128)(2,1)}, u32[]{:S(2)}, u32[]{:S(2)}) async-start(bf16[32,64,1280]{2,1,0:T(8,128)(2,1)} %copy-done), calls=%async_computation | async-start | bytes 10485760 | tf_op jit(solution)/shard_map/all_to_all | solution.py:300
  42.4 40.8 %collective-permute-start.1 = (bf16[640,640]{1,0:T(8,128)(2,1)S(1)}, bf16[640,640]{1,0:T(8,128)(2,1)S(1)}, u32[]{:S(2)}, u32[]{:S(2)}) collective-permute-start(bf16[640,640]{1,0:T(8,128)(2,1)S(1)} %bitcast.20), channel_id=1, source_target_pairs={{0,48},{16,32},{32,16},{48,0},{1,49},{17,33},{33,17},{49,1},{2,50}... | collective-permute-start | bytes 2457608 | tf_op jit(solution)/shard_map/ppermute | solution.py:266
  42.8 43.3 %collective-permute-start.2 = (bf16[640,640]{1,0:T(8,128)(2,1)S(1)}, bf16[640,640]{1,0:T(8,128)(2,1)S(1)}, u32[]{:S(2)}, u32[]{:S(2)}) collective-permute-start(bf16[640,640]{1,0:T(8,128)(2,1)S(1)} %bitcast.21), channel_id=1, source_target_pairs={{0,64},{64,128},{128,192},{192,0},{1,65},{65,129},{129,193},{193,1... | collective-permute-start | bytes 2457608 | tf_op jit(solution)/shard_map/ppermute | solution.py:267
  44.4 42.4 %collective-permute-start.3 = (bf16[640,640]{1,0:T(8,128)(2,1)S(1)}, bf16[640,640]{1,0:T(8,128)(2,1)S(1)}, u32[]{:S(2)}, u32[]{:S(2)}) collective-permute-start(bf16[640,640]{1,0:T(8,128)(2,1)S(1)} %bitcast.22), channel_id=1, source_target_pairs={{0,192},{64,0},{128,64},{192,128},{1,193},{65,1},{129,65},{193,129... | collective-permute-start | bytes 2457608 | tf_op jit(solution)/shard_map/ppermute | solution.py:267
  46.0 40.7 %collective-permute-start.8 = (bf16[640,640]{1,0:T(8,128)(2,1)S(1)}, bf16[640,640]{1,0:T(8,128)(2,1)S(1)}, u32[]{:S(2)}, u32[]{:S(2)}) collective-permute-start(bf16[640,640]{1,0:T(8,128)(2,1)S(1)} %bitcast.23), channel_id=1, source_target_pairs={{0,1},{1,0},{2,3},{3,2},{4,5},{5,4},{6,7},{7,6},{8,9},{9,8},{10,11... | collective-permute-start | bytes 2457608 | tf_op jit(solution)/shard_map/ppermute | solution.py:277
  83.1 20.8 %collective-permute-start.5 = (bf16[640,640]{1,0:T(8,128)(2,1)S(1)}, bf16[640,640]{1,0:T(8,128)(2,1)}, u32[]{:S(2)}, u32[]{:S(2)}) collective-permute-start(bf16[640,640]{1,0:T(8,128)(2,1)S(1)} %collective-permute-done.1.rest_1_), channel_id=1, source_target_pairs={{0,192},{64,0},{128,64},{192,128},{1,193},{65,1},{129,65},{193,129... | collective-permute-start | bytes 2457608 | tf_op jit(solution)/shard_map/ppermute | solution.py:268
  86.1 22.4 %collective-permute-start.4 = (bf16[640,640]{1,0:T(8,128)(2,1)S(1)}, bf16[640,640]{1,0:T(8,128)(2,1)}, u32[]{:S(2)}, u32[]{:S(2)}) collective-permute-start(bf16[640,640]{1,0:T(8,128)(2,1)S(1)} %collective-permute-done.1.rest_1_), channel_id=1, source_target_pairs={{0,64},{64,128},{128,192},{192,0},{1,65},{65,129},{129,193},{193,1... | collective-permute-start | bytes 2457608 | tf_op jit(solution)/shard_map/ppermute | solution.py:268
  86.1 38.9 %collective-permute-start.6 = (bf16[640,640]{1,0:T(8,128)(2,1)S(1)}, bf16[640,640]{1,0:T(8,128)(2,1)}, u32[]{:S(2)}, u32[]{:S(2)}) collective-permute-start(bf16[640,640]{1,0:T(8,128)(2,1)S(1)} %collective-permute-done.2.rest_2_), channel_id=1, source_target_pairs={{0,64},{64,128},{128,192},{192,0},{1,65},{65,129},{129,193},{193,1... | collective-permute-start | bytes 2457608 | tf_op jit(solution)/shard_map/ppermute | solution.py:269
  86.7 38.3 %collective-permute-start.9 = (bf16[640,640]{1,0:T(8,128)(2,1)S(1)}, bf16[640,640]{1,0:T(8,128)(2,1)S(1)}, u32[]{:S(2)}, u32[]{:S(2)}) collective-permute-start(bf16[640,640]{1,0:T(8,128)(2,1)S(1)} %collective-permute-done.1.rest_1_), channel_id=1, source_target_pairs={{0,1},{1,0},{2,3},{3,2},{4,5},{5,4},{6,7},{7,6},{8,9},{9,8},{10,11... | collective-permute-start | bytes 2457608 | tf_op jit(solution)/shard_map/ppermute | solution.py:277
  86.8 38.8 %collective-permute-start.10 = (bf16[640,640]{1,0:T(8,128)(2,1)S(1)}, bf16[640,640]{1,0:T(8,128)(2,1)S(1)}, u32[]{:S(2)}, u32[]{:S(2)}) collective-permute-start(bf16[640,640]{1,0:T(8,128)(2,1)S(1)} %collective-permute-done.2.rest_2_), channel_id=1, source_target_pairs={{0,1},{1,0},{2,3},{3,2},{4,5},{5,4},{6,7},{7,6},{8,9},{9,8},{10,11... | collective-permute-start | bytes 2457608 | tf_op jit(solution)/shard_map/ppermute | solution.py:277
  103.9 22.0 %collective-permute-start.7 = (bf16[640,640]{1,0:T(8,128)(2,1)}, bf16[640,640]{1,0:T(8,128)(2,1)}, u32[]{:S(2)}, u32[]{:S(2)}) collective-permute-start(bf16[640,640]{1,0:T(8,128)(2,1)} %collective-permute-done.5.rest_5_), channel_id=1, source_target_pairs={{0,192},{64,0},{128,64},{192,128},{1,193},{65,1},{129,65},{193,129... | collective-permute-start | bytes 2457608 | tf_op jit(solution)/shard_map/ppermute | solution.py:269
  108.6 18.8 %collective-permute-start.11 = (bf16[640,640]{1,0:T(8,128)(2,1)S(1)}, bf16[640,640]{1,0:T(8,128)(2,1)}, u32[]{:S(2)}, u32[]{:S(2)}) collective-permute-start(bf16[640,640]{1,0:T(8,128)(2,1)S(1)} %collective-permute-done.3.rest_3_), channel_id=1, source_target_pairs={{0,1},{1,0},{2,3},{3,2},{4,5},{5,4},{6,7},{7,6},{8,9},{9,8},{10,11... | collective-permute-start | bytes 2457608 | tf_op jit(solution)/shard_map/ppermute | solution.py:277
  125.0 3.8 %collective-permute-start.13 = (bf16[640,640]{1,0:T(8,128)(2,1)}, bf16[640,640]{1,0:T(8,128)(2,1)}, u32[]{:S(2)}, u32[]{:S(2)}) collective-permute-start(bf16[640,640]{1,0:T(8,128)(2,1)} %collective-permute-done.5.rest_5_), channel_id=1, source_target_pairs={{0,1},{1,0},{2,3},{3,2},{4,5},{5,4},{6,7},{7,6},{8,9},{9,8},{10,11... | collective-permute-start | bytes 2457608 | tf_op jit(solution)/shard_map/ppermute | solution.py:277
  125.0 3.8 %collective-permute-start.12 = (bf16[640,640]{1,0:T(8,128)(2,1)}, bf16[640,640]{1,0:T(8,128)(2,1)}, u32[]{:S(2)}, u32[]{:S(2)}) collective-permute-start(bf16[640,640]{1,0:T(8,128)(2,1)} %collective-permute-done.4.rest_4_), channel_id=1, source_target_pairs={{0,1},{1,0},{2,3},{3,2},{4,5},{5,4},{6,7},{7,6},{8,9},{9,8},{10,11... | collective-permute-start | bytes 2457608 | tf_op jit(solution)/shard_map/ppermute | solution.py:277
  125.5 4.5 %collective-permute-start.14 = (bf16[640,640]{1,0:T(8,128)(2,1)}, bf16[640,640]{1,0:T(8,128)(2,1)}, u32[]{:S(2)}, u32[]{:S(2)}) collective-permute-start(bf16[640,640]{1,0:T(8,128)(2,1)} %collective-permute-done.6.rest_6_), channel_id=1, source_target_pairs={{0,1},{1,0},{2,3},{3,2},{4,5},{5,4},{6,7},{7,6},{8,9},{9,8},{10,11... | collective-permute-start | bytes 2457608 | tf_op jit(solution)/shard_map/ppermute | solution.py:277
  126.5 4.7 %collective-permute-start.15 = (bf16[640,640]{1,0:T(8,128)(2,1)}, bf16[640,640]{1,0:T(8,128)(2,1)}, u32[]{:S(2)}, u32[]{:S(2)}) collective-permute-start(bf16[640,640]{1,0:T(8,128)(2,1)} %collective-permute-done.7.rest_7_), channel_id=1, source_target_pairs={{0,1},{1,0},{2,3},{3,2},{4,5},{5,4},{6,7},{7,6},{8,9},{9,8},{10,11... | collective-permute-start | bytes 2457608 | tf_op jit(solution)/shard_map/ppermute | solution.py:277
  (7 other events, 71.5 us)

commit v3 on v2

v3 whole, which is shorter than its diff:
```python
import math

import jax
import jax.numpy as jnp
from jax import lax
from jax.experimental import pallas as pl
from jax.experimental.pallas import tpu as pltpu
from jax.sharding import Mesh
from jax.sharding import PartitionSpec as P

D = 1280
HEADS = 16
HD = 80
WIN = 64
DST_WIN = 8
SRC_WIN = 24
N_DEV = 32
N_SEC = 8
CAP = 32
ROWS = DST_WIN * WIN
MERGED = ROWS // 4
COLS = 4 * D
CHUNK = 640
HALF = 640
EXP2_SCALE = HD ** (-0.5) * math.log2(math.e)
VMEM_LIMIT = 48 * 1024 * 1024

F32 = jnp.float32
BF16 = jnp.bfloat16


def outgoing_kernel(place, counts, perm, patches, out, staged, in_sem, out_sem):
    pos = place[0]
    mine = counts[pos]

    def load(i):
        return pltpu.make_async_copy(patches.at[i], staged.at[i], in_sem.at[i])

    for i in range(SRC_WIN):

        @pl.when(i < mine)
        def _(i=i):
            load(i).start()

    def add(d, total):
        return total + jnp.where(d < pos, counts[d], 0)

    begin = lax.fori_loop(0, N_DEV, add, jnp.int32(0))

    def save(i):
        slot = perm[jnp.bitwise_and(begin + i, N_DEV - 1)]
        return pltpu.make_async_copy(staged.at[i], out.at[slot], out_sem.at[i])

    for i in range(SRC_WIN):

        @pl.when(i < mine)
        def _(i=i):
            load(i).wait()
            save(i).start()

    for i in range(SRC_WIN):

        @pl.when(i < mine)
        def _(i=i):
            save(i).wait()


def outgoing(place, counts, perm, patches):
    smem = pl.BlockSpec(memory_space=pltpu.SMEM)
    return pl.pallas_call(
        outgoing_kernel,
        out_shape=jax.ShapeDtypeStruct((N_DEV, WIN, D), patches.dtype),
        in_specs=[smem, smem, smem, pl.BlockSpec(memory_space=pl.ANY)],
        out_specs=pl.BlockSpec(memory_space=pl.ANY),
        scratch_shapes=[
            pltpu.VMEM((SRC_WIN, WIN, D), patches.dtype),
            pltpu.SemaphoreType.DMA((SRC_WIN,)),
            pltpu.SemaphoreType.DMA((SRC_WIN,)),
        ],
        compiler_params=pltpu.CompilerParams(vmem_limit_bytes=16 * 1024 * 1024),
        name="outgoing",
    )(place, counts, perm, patches)


def encode_kernel(
    place,
    counts,
    perm,
    groups,
    owner_row,
    owner_column,
    norm_gain,
    qkv_bias,
    proj_bias,
    merge_gain,
    arrived,
    *rest,
):
    pieces = rest[:16]
    out, weights, windows, normed, triple, mixed, encoded, final, source, live, wsem, xsem = rest[16:]
    pos, here, side = place[0], place[1], place[2]

    def find(r, found):
        return jnp.where(perm[r] == pos, r, found)

    residue = lax.fori_loop(0, N_DEV, find, jnp.int32(0))

    def locate(d, begin):
        count = counts[d]
        within = jnp.bitwise_and(residue - begin, N_DEV - 1)

        @pl.when(within < count)
        def _():
            slot = lax.shift_right_logical(begin + within, 5)
            source[slot] = d
            live[slot] = 4 * groups[d * SRC_WIN + within]

        return begin + count

    lax.fori_loop(0, N_DEV, locate, jnp.int32(0))

    def window_copy(k):
        return pltpu.make_async_copy(
            arrived.at[source[k]], windows.at[pl.ds(k * WIN, WIN)], xsem.at[k]
        )

    def weight_copy(n, core, across):
        row = jnp.bitwise_xor(here, across) * HALF
        column = jnp.bitwise_xor(side, core) * CHUNK
        to = weights.at[
            place[3 + n],
            pl.ds(pl.multiple_of(row, HALF), HALF),
            pl.ds(pl.multiple_of(column, CHUNK), CHUNK),
        ]
        return pltpu.make_async_copy(pieces[8 * core + 2 * n + across], to, wsem.at[n, core, across])

    for k in range(DST_WIN):
        window_copy(k).start()
    for n in range(4):
        for core in range(2):
            for across in range(2):
                weight_copy(n, core, across).start()
    for k in range(DST_WIN):
        window_copy(k).wait()
        rows = pl.ds(k * WIN, WIN)
        values = windows[rows, :].astype(F32)
        mean = jnp.mean(values * values, axis=-1, keepdims=True)
        normed[rows, :] = (values * lax.rsqrt(mean + 1e-6) * norm_gain[...]).astype(BF16)

    for n in range(4):
        block = place[3 + n]
        for core in range(2):
            for across in range(2):
                weight_copy(n, core, across).wait()

        @pl.when(block < 3)
        def _(block=block):
            product = jnp.dot(normed[...], weights[block], preferred_element_type=F32)
            triple[block] = (product + qkv_bias[block]).astype(BF16)

    def attend(w, carry):
        rows = pl.ds(pl.multiple_of(w * WIN, WIN), WIN)
        dead = lax.broadcasted_iota(jnp.int32, (WIN, 2 * WIN), 0) >= live[w]
        zero = jnp.zeros((), BF16)
        for half in range(2):
            parts = [None] * (CHUNK // 128)
            for pair in range(HEADS // 4):
                begin = pair * 2 * HD
                low = begin // 128 * 128
                lane = low + lax.broadcasted_iota(jnp.int32, (WIN, 256), 1)
                first = (lane >= begin) & (lane < begin + HD)
                second = (lane >= begin + HD) & (lane < begin + 2 * HD)
                at = half * CHUNK + low
                q = triple[0, rows, at : at + 256]
                k = triple[1, rows, at : at + 256]
                v = triple[2, rows, at : at + 256]
                both = jnp.concatenate([jnp.where(first, q, zero), jnp.where(second, q, zero)], axis=0)
                scores = lax.dot_general(
                    k, both, (((1,), (1,)), ((), ())), preferred_element_type=F32
                )
                scores = jnp.where(dead, -1e30, scores)
                highest = jnp.max(scores, axis=0, keepdims=True)
                powers = jnp.exp2((scores - highest) * EXP2_SCALE)
                probs = powers * (1.0 / jnp.sum(powers, axis=0, keepdims=True))
                product = lax.dot_general(
                    probs.astype(BF16), v, (((0,), (0,)), ((), ())), preferred_element_type=F32
                )
                product = jnp.where(first, product[:WIN], jnp.where(second, product[WIN:], 0.0))
                for t in range(2):
                    tile, part = low // 128 + t, product[:, 128 * t : 128 * t + 128]
                    parts[tile] = part if parts[tile] is None else parts[tile] + part
            for tile in range(CHUNK // 128):
                at = half * CHUNK + tile * 128
                mixed[rows, at : at + 128] = parts[tile].astype(BF16)
        return carry

    lax.fori_loop(0, DST_WIN, attend, 0)

    encoded[...] = jnp.dot(mixed[...], weights[3], preferred_element_type=F32)
    for k in range(DST_WIN):
        rows = pl.ds(k * WIN, WIN)
        values = windows[rows, :].astype(F32) + encoded[rows, :] + proj_bias[...]
        mean = jnp.mean(values * values, axis=-1, keepdims=True)
        alive = lax.broadcasted_iota(jnp.int32, (WIN, 1), 0) < live[k]
        scale = jnp.where(alive, lax.rsqrt(mean + 1e-6), 0.0)
        final[rows, :] = (values * scale * merge_gain[...]).astype(BF16)

    lane = lax.broadcasted_iota(jnp.int32, (MERGED, ROWS), 1)
    earlier = lax.broadcasted_iota(jnp.int32, (MERGED, ROWS), 0) < lax.shift_right_logical(lane, 2)
    same = owner_column[...] == owner_row[...]
    rank = jnp.sum(jnp.where(same & earlier, 1, 0), axis=0, keepdims=True)
    places = owner_row[...] * CAP + rank
    chosen = lax.broadcasted_iota(jnp.int32, (N_SEC * CAP, ROWS), 0) == places
    turn = jnp.bitwise_and(lax.broadcasted_iota(jnp.int32, (N_SEC * CAP, ROWS), 1), 3)
    for p in range(4):
        pick = jnp.where(chosen & (turn == p), 1.0, 0.0).astype(BF16)
        packed = jnp.dot(pick, final[...], preferred_element_type=F32)
        out[:, p * D : (p + 1) * D] = packed.astype(BF16)


def encode(place, counts, perm, groups, owner_row, owner_column, gain, qb, pb, mg, arrived, pieces):
    smem = pl.BlockSpec(memory_space=pltpu.SMEM)
    vmem = pl.BlockSpec(memory_space=pltpu.VMEM)
    hbm = pl.BlockSpec(memory_space=pl.ANY)
    return pl.pallas_call(
        encode_kernel,
        out_shape=jax.ShapeDtypeStruct((N_SEC * CAP, COLS), BF16),
        in_specs=[smem] * 4 + [vmem] * 6 + [hbm] * 17,
        out_specs=vmem,
        scratch_shapes=[
            pltpu.VMEM((4, D, D), BF16),
            pltpu.VMEM((ROWS, D), BF16),
            pltpu.VMEM((ROWS, D), BF16),
            pltpu.VMEM((3, ROWS, D), BF16),
            pltpu.VMEM((ROWS, D), BF16),
            pltpu.VMEM((ROWS, D), F32),
            pltpu.VMEM((ROWS, D), BF16),
            pltpu.SMEM((DST_WIN,), jnp.int32),
            pltpu.SMEM((DST_WIN,), jnp.int32),
            pltpu.SemaphoreType.DMA((4, 2, 2)),
            pltpu.SemaphoreType.DMA((DST_WIN,)),
        ],
        compiler_params=pltpu.CompilerParams(vmem_limit_bytes=VMEM_LIMIT),
        name="encode",
    )(place, counts, perm, groups, owner_row, owner_column, gain, qb, pb, mg, arrived, *pieces)


def shift(n, k):
    return [(i, (i + k) % n) for i in range(n)]


SWAP = [(0, 1), (1, 0)]
CROSS = [(i, 3 - i) for i in range(4)]
CROSS3 = [(i, 7 - i) for i in range(8)]


def gather_weights(qkv_weight, proj_weight):
    y, xl, c = lax.axis_index("y"), lax.axis_index("xl"), lax.axis_index("c")
    send = lax.ppermute
    side = jnp.bitwise_xor(xl, c)
    chunk = 2 * y + side
    from_qkv = lax.dynamic_slice(qkv_weight, (0, jnp.minimum(chunk, 5) * CHUNK), (40, CHUNK))
    from_proj = lax.dynamic_slice(proj_weight, (0, jnp.maximum(chunk - 6, 0) * CHUNK), (40, CHUNK))
    own = jnp.where(chunk < 6, from_qkv, from_proj)
    column = lax.all_to_all(jnp.broadcast_to(own[None], (8, 40, CHUNK)), "z", 0, 0, tiled=True)
    return column, side


def spread_weights(column, side):
    y, xh, c = lax.axis_index("y"), lax.axis_index("xh"), lax.axis_index("c")
    send = lax.ppermute
    partner = send(column, ("xl", "c"), CROSS)
    low, high = jnp.where(c == 0, column, partner), jnp.where(c == 0, partner, column)
    here = jnp.concatenate([low, high], axis=1).reshape(HALF, CHUNK)
    across = send(here, ("xl", "xh", "c"), CROSS3)
    up_h, down_h = send(here, "y", shift(4, 1)), send(here, "y", shift(4, -1))
    up_a, down_a = send(across, "y", shift(4, 1)), send(across, "y", shift(4, -1))
    far_h, far_a = send(up_h, "y", shift(4, 1)), send(down_a, "y", shift(4, -1))
    pieces = [here, across, up_h, up_a, down_h, down_a, far_h, far_a]
    pieces = pieces + [send(p, "c", SWAP) for p in pieces]
    return pieces, [xh, side] + [jnp.mod(y - step, 4) for step in (0, 1, -1, 2)]


def body(
    patches,
    win_count,
    dest_perm,
    win_groups,
    norm_gain,
    qkv_weight,
    qkv_bias,
    proj_weight,
    proj_bias,
    merge_gain,
    owner,
):
    position = lax.axis_index(("xh", "z", "c"))
    counts, perm = win_count[0], dest_perm[0]
    column, side = gather_weights(qkv_weight, proj_weight)
    going = outgoing(
        position.astype(jnp.int32).reshape(1), counts, perm, patches.reshape(SRC_WIN, WIN, D)
    )
    pieces, placed = spread_weights(column, side)
    place = jnp.stack([position] + placed).astype(jnp.int32)
    arrived = lax.all_to_all(going, ("xh", "z", "c"), split_axis=0, concat_axis=0, tiled=True)
    packed = encode(
        place,
        counts,
        perm,
        win_groups.reshape(N_DEV * SRC_WIN),
        jnp.repeat(owner.reshape(1, MERGED), 4, axis=1),
        owner.reshape(MERGED, 1),
        norm_gain.reshape(1, D),
        qkv_bias.reshape(3, 1, D),
        proj_bias.reshape(1, D),
        merge_gain.reshape(1, D),
        arrived,
        pieces,
    )
    delivered = lax.all_to_all(packed, ("y", "xl"), split_axis=0, concat_axis=0, tiled=True)
    return delivered.reshape(1, N_SEC * CAP, COLS)


def solution(mesh):
    fine = Mesh(mesh.devices.reshape(4, 2, 2, 8, 2), ("y", "xl", "xh", "z", "c"))
    sec, dev = ("y", "xl"), ("xh", "z", "c")
    return jax.shard_map(
        body,
        mesh=fine,
        in_specs=(
            P(sec, dev, None),
            P(sec, None),
            P(sec, None),
            P(sec, None, None),
            P(),
            P(dev, None),
            P(),
            P(dev, None),
            P(),
            P(),
            P(sec, dev, None),
        ),
        out_specs=P(sec, dev, None),
        check_vma=False,
    )
```

time: 230 us -> 216 us (0.939)
  Pallas kernels: 33.2 us -> 23.4 us
  waiting for transfers between devices: 120 us -> 111 us
  starting transfers between devices: 26 us -> 32.5 us
    all_to_all x1, waiting for transfers between devices: 27.8 us -> 8.68 us  [body(): lax.all_to_all(going, ('xh', 'z', 'c'), split_axis=0, concat_axis=0, tile...]
    ppermute x16, waiting for transfers between devices: 76.6 us -> 94.9 us  [the longest x1 28.7 us: spread_weights(): across = send(here, ('xl', 'xh', 'c'), CROSS3)]
    all_to_all x1, waiting for transfers between devices: 16.1 us -> 7.39 us  [gather_weights(): lax.all_to_all(jnp.broadcast_to(own[None], (8, 40, CHUNK)), 'z', 0, 0, ti...]
    pallas_call x1, Pallas kernels: 29.7 us -> 21.6 us  [encode(): pl.pallas_call(encode_kernel, out_shape=jax.ShapeDtypeStruct((N_SEC * CAP...]
    all_to_all x1, starting transfers between devices: 5.06 us -> 12.7 us  [body(): lax.all_to_all(going, ('xh', 'z', 'c'), split_axis=0, concat_axis=0, tile...]
    unnamed x29 -> x32, local copies, waits for them, and re-layouts: 7.83 us -> 8.13 us
  transfers between devices with their start and end apart: 18 -> 18, of which waited for: 10 -> 10; matrix products, arithmetic and copies ran while one was open for 0% -> 0% of each run, Pallas kernels for 2% -> 1%
where the time goes in v3:
time: 216 us; the launch traced here: 214 us
  waiting for transfers between devices  111 us (51%)
  blocking collectives  36.3 us (17%)
  starting transfers between devices  32.5 us (15%)
  Pallas kernels  23.4 us (11%)
  local copies, waits for them, and re-layouts  9.42 us (4%)
    all_to_all x1, blocking collectives, body(): lax.all_to_all(packed, ('y', 'xl'), split_axis=0, concat_axis=0, tiled=True)  36.3 us
    ppermute x1, waiting for transfers between devices, spread_weights(): across = send(here, ('xl', 'xh', 'c'), CROSS3)  28.7 us
    ppermute x1, waiting for transfers between devices, spread_weights(): partner = send(column, ('xl', 'c'), CROSS)  27.9 us
    pallas_call x1, Pallas kernels, encode(): pl.pallas_call(encode_kernel, out_shape=jax.ShapeDtypeStruct((N_SEC * CAP...  21.6 us
    ppermute x1, waiting for transfers between devices, spread_weights(): send(up_h, 'y', shift(4, 1))  17.4 us
    ppermute x1, waiting for transfers between devices, spread_weights(): send(across, 'y', shift(4, -1))  16.8 us
    all_to_all x1, starting transfers between devices, body(): lax.all_to_all(going, ('xh', 'z', 'c'), split_axis=0, concat_axis=0, tile...  12.7 us
    all_to_all x1, waiting for transfers between devices, body(): lax.all_to_all(going, ('xh', 'z', 'c'), split_axis=0, concat_axis=0, tile...  8.68 us
  transfers between devices with their start and end apart: 18, of which 10 were waited for; matrix products, arithmetic and copies ran while one was open for 0% of the time, Pallas kernels for 1%

profile of v3, /device:TPU:4, one launch (start us, length us, event | category | flops | bytes accessed | tf_op | source)
XLA Modules:
  0.0 213.9 jit_solution(4082058213133015918)
XLA Ops:
  0.0 0.8 dynamic-slice_select_fusion
  1.6 8.5 %all-to-all-start.1 = ((bf16[8,40,640]{2,1,0:T(8,128)(2,1)}), bf16[8,40,640]{2,1,0:T(8,128)(2,1)S(1)}, u32[]{:S(2)}, u32[]{:S(2)}) async-start(bf16[8,40,640]{2,1,0:T(8,128)(2,1)} %broadcast_in_dim.13), calls=%async_computation.1 | async-start | bytes 819200 | tf_op jit(solution)/shard_map/all_to_all | solution.py:265
  10.1 2.1 copy-done.1
  13.5 1.8 outgoing.1
  15.4 2.4 %copy-done = bf16[32,64,1280]{2,1,0:T(8,128)(2,1)} copy-done((bf16[32,64,1280]{2,1,0:T(8,128)(2,1)}, bf16[32,64,1280]{2,1,0:T(8,128)(2,1)S(1)}, u32[]{:S(2)}) %copy-start) | copy-done | bytes 5242904
  17.7 7.4 %all-to-all-done.1 = bf16[8,40,640]{2,1,0:T(8,128)(2,1)S(1)} async-done(((bf16[8,40,640]{2,1,0:T(8,128)(2,1)}), bf16[8,40,640]{2,1,0:T(8,128)(2,1)S(1)}, u32[]{:S(2)}, u32[]{:S(2)}) %all-to-all-start.1) | async-done | bytes 409632 | tf_op jit(solution)/shard_map/all_to_all | solution.py:265
  25.1 12.7 %all-to-all-start = ((bf16[32,64,1280]{2,1,0:T(8,128)(2,1)}), bf16[32,64,1280]{2,1,0:T(8,128)(2,1)}, u32[]{:S(2)}, u32[]{:S(2)}) async-start(bf16[32,64,1280]{2,1,0:T(8,128)(2,1)} %copy-done), calls=%async_computation | async-start | bytes 10485760 | tf_op jit(solution)/shard_map/all_to_all | solution.py:305
  38.1 27.9 %collective-permute-done = bf16[8,40,640]{2,1,0:T(8,128)(2,1)S(1)} collective-permute-done((bf16[8,40,640]{2,1,0:T(8,128)(2,1)S(1)}, bf16[8,40,640]{2,1,0:T(8,128)(2,1)S(1)}, u32[]{:S(2)}, u32[]{:S(2)}) %collective-permute-start) | collective-permute-done | bytes 409632 | tf_op jit(solution)/shard_map/ppermute | solution.py:272
  66.2 1.3 collective-permute-start.1
  67.4 1.6 collective-permute-start.2
  69.0 1.7 collective-permute-start.4
  70.7 28.7 %collective-permute-done.1.rest_1_ = bf16[640,640]{1,0:T(8,128)(2,1)S(1)} collective-permute-done((bf16[640,640]{1,0:T(8,128)(2,1)S(1)}, bf16[640,640]{1,0:T(8,128)(2,1)S(1)}, u32[]{:S(2)}, u32[]{:S(2)}) %collective-permute-start.1) | collective-permute-done | bytes 819232 | tf_op jit(solution)/shard_map/ppermute | solution.py:275
  99.7 1.7 collective-permute-start.3
  101.4 1.2 collective-permute-start.6
  103.1 16.8 %collective-permute-done.5.rest_5_ = bf16[640,640]{1,0:T(8,128)(2,1)} collective-permute-done((bf16[640,640]{1,0:T(8,128)(2,1)S(1)}, bf16[640,640]{1,0:T(8,128)(2,1)}, u32[]{:S(2)}, u32[]{:S(2)}) %collective-permute-start.5) | collective-permute-done | bytes 819232 | tf_op jit(solution)/shard_map/ppermute | solution.py:277
  120.0 1.9 collective-permute-start.7
  122.2 17.4 %collective-permute-done.6.rest_6_ = bf16[640,640]{1,0:T(8,128)(2,1)} collective-permute-done((bf16[640,640]{1,0:T(8,128)(2,1)S(1)}, bf16[640,640]{1,0:T(8,128)(2,1)}, u32[]{:S(2)}, u32[]{:S(2)}) %collective-permute-start.6) | collective-permute-done | bytes 819232 | tf_op jit(solution)/shard_map/ppermute | solution.py:278
  142.1 1.4 collective-permute-done.11.rest_11_
  143.5 1.2 collective-permute-done.14.rest_14_
  144.7 1.2 collective-permute-done.15.rest_15_
  145.8 8.7 %all-to-all-done.arrived = bf16[32,64,1280]{2,1,0:T(8,128)(2,1)} async-done(((bf16[32,64,1280]{2,1,0:T(8,128)(2,1)}), bf16[32,64,1280]{2,1,0:T(8,128)(2,1)}, u32[]{:S(2)}, u32[]{:S(2)}) %all-to-all-start) | async-done | bytes 5242912 | tf_op jit(solution)/shard_map/all_to_all | solution.py:305
  154.5 21.6 %encode.1 = bf16[256,5120]{1,0:T(8,128)(2,1)} custom-call(s32[7]{0:T(128)S(1)} %stack.31.place, s32[32]{0:T(128)S(1)} %bitcast.22, s32[32]{0:T(128)S(1)} %bitcast.24, s32[768]{0:T(1024)S(1)} %reshape.41.groups, s32[1,512]{1,0:T(1,128)S(1)} %broadcast_in_dim.12.owner_row, s32[128,1]{1,0:T(8,128)S(1)} %copy.14.owner_column, f32[1,1280]{1,0:T(1,128)S(1)} %reshape.44.norm_gain, ...), custom_call_target="tpu_custom_call" | custom-call | tf_op jit(solution)/shard_map/encode/pallas_call | solution.py:225
  176.1 36.3 %all_to_all.19 = bf16[8,32,5120]{2,1,0:T(8,128)(2,1)S(1)} all-to-all(bf16[8,32,5120]{2,1,0:T(8,128)(2,1)} %bitcast.25), channel_id=1, replica_groups=mesh['y'=4,'xl'=2,'xh'=2,'z'=8,'c'=2] {'y','xl'}, dimensions={0} | all-to-all | bytes 5242880 | tf_op jit(solution)/shard_map/all_to_all | solution.py:320
  212.4 1.5 copy.16
  (60 shorter events, 5.9 us)
Async XLA Ops:
  1.6 23.5 %all-to-all-start.1 = ((bf16[8,40,640]{2,1,0:T(8,128)(2,1)}), bf16[8,40,640]{2,1,0:T(8,128)(2,1)S(1)}, u32[]{:S(2)}, u32[]{:S(2)}) async-start(bf16[8,40,640]{2,1,0:T(8,128)(2,1)} %broadcast_in_dim.13), calls=%async_computation.1 | async-start | bytes 819200 | tf_op jit(solution)/shard_map/all_to_all | solution.py:265
  25.1 129.4 %all-to-all-start = ((bf16[32,64,1280]{2,1,0:T(8,128)(2,1)}), bf16[32,64,1280]{2,1,0:T(8,128)(2,1)}, u32[]{:S(2)}, u32[]{:S(2)}) async-start(bf16[32,64,1280]{2,1,0:T(8,128)(2,1)} %copy-done), calls=%async_computation | async-start | bytes 10485760 | tf_op jit(solution)/shard_map/all_to_all | solution.py:305
  37.9 104.0 %copy-start.11 = (f32[1280]{0:T(1024)S(1)}, f32[1280]{0:T(1024)}, u32[]{:S(2)}) copy-start(f32[1280]{0:T(1024)} %param.15) | copy-start | bytes 15364
  37.9 104.0 %copy-start.9 = (f32[3840]{0:T(1024)S(1)}, f32[3840]{0:T(1024)}, u32[]{:S(2)}) copy-start(f32[3840]{0:T(1024)} %param.17) | copy-start | bytes 46084
  37.9 104.0 %copy-start.12 = (f32[1280]{0:T(1024)S(1)}, f32[1280]{0:T(1024)}, u32[]{:S(2)}) copy-start(f32[1280]{0:T(1024)} %param.19) | copy-start | bytes 15364
  37.9 104.0 %copy-start.13 = (f32[1280]{0:T(1024)S(1)}, f32[1280]{0:T(1024)}, u32[]{:S(2)}) copy-start(f32[1280]{0:T(1024)} %param.20) | copy-start | bytes 15364
  37.9 116.6 %copy-start.3 = (s32[1,32]{1,0:T(1,128)S(1)}, s32[1,32]{1,0:T(1,128)}, u32[]{:S(2)}) copy-start(s32[1,32]{1,0:T(1,128)} %param.12) | copy-start | bytes 388
  37.9 116.6 %copy-start.5 = (s32[1,32]{1,0:T(1,128)S(1)}, s32[1,32]{1,0:T(1,128)}, u32[]{:S(2)}) copy-start(s32[1,32]{1,0:T(1,128)} %param.13) | copy-start | bytes 388
  38.0 28.0 %collective-permute-start = (bf16[8,40,640]{2,1,0:T(8,128)(2,1)S(1)}, bf16[8,40,640]{2,1,0:T(8,128)(2,1)S(1)}, u32[]{:S(2)}, u32[]{:S(2)}) collective-permute-start(bf16[8,40,640]{2,1,0:T(8,128)(2,1)S(1)} %all-to-all-done.1), channel_id=1, source_target_pairs={{0,33},{1,32},{32,1},{33,0},{2,35},{3,34},{34,3},{35,2},{4,37},{5,... | collective-permute-start | bytes 1228808 | tf_op jit(solution)/shard_map/ppermute | solution.py:272
  66.2 33.2 %collective-permute-start.1 = (bf16[640,640]{1,0:T(8,128)(2,1)S(1)}, bf16[640,640]{1,0:T(8,128)(2,1)S(1)}, u32[]{:S(2)}, u32[]{:S(2)}) collective-permute-start(bf16[640,640]{1,0:T(8,128)(2,1)S(1)} %bitcast.16), channel_id=1, source_target_pairs={{0,49},{1,48},{16,33},{17,32},{32,17},{33,16},{48,1},{49,0},{2,51}... | collective-permute-start | bytes 2457608 | tf_op jit(solution)/shard_map/ppermute | solution.py:275
  67.4 34.0 %collective-permute-start.2 = (bf16[640,640]{1,0:T(8,128)(2,1)S(1)}, bf16[640,640]{1,0:T(8,128)(2,1)S(1)}, u32[]{:S(2)}, u32[]{:S(2)}) collective-permute-start(bf16[640,640]{1,0:T(8,128)(2,1)S(1)} %bitcast.17), channel_id=1, source_target_pairs={{0,64},{64,128},{128,192},{192,0},{1,65},{65,129},{129,193},{193,1... | collective-permute-start | bytes 2457608 | tf_op jit(solution)/shard_map/ppermute | solution.py:276
  69.0 33.6 %collective-permute-start.4 = (bf16[640,640]{1,0:T(8,128)(2,1)S(1)}, bf16[640,640]{1,0:T(8,128)(2,1)S(1)}, u32[]{:S(2)}, u32[]{:S(2)}) collective-permute-start(bf16[640,640]{1,0:T(8,128)(2,1)S(1)} %bitcast.18), channel_id=1, source_target_pairs={{0,192},{64,0},{128,64},{192,128},{1,193},{65,1},{129,65},{193,129... | collective-permute-start | bytes 2457608 | tf_op jit(solution)/shard_map/ppermute | solution.py:276
  70.7 32.0 %collective-permute-start.8 = (bf16[640,640]{1,0:T(8,128)(2,1)S(1)}, bf16[640,640]{1,0:T(8,128)(2,1)S(1)}, u32[]{:S(2)}, u32[]{:S(2)}) collective-permute-start(bf16[640,640]{1,0:T(8,128)(2,1)S(1)} %bitcast.19), channel_id=1, source_target_pairs={{0,1},{1,0},{2,3},{3,2},{4,5},{5,4},{6,7},{7,6},{8,9},{9,8},{10,11... | collective-permute-start | bytes 2457608 | tf_op jit(solution)/shard_map/ppermute | solution.py:280
  99.4 20.6 %collective-permute-start.5 = (bf16[640,640]{1,0:T(8,128)(2,1)S(1)}, bf16[640,640]{1,0:T(8,128)(2,1)}, u32[]{:S(2)}, u32[]{:S(2)}) collective-permute-start(bf16[640,640]{1,0:T(8,128)(2,1)S(1)} %collective-permute-done.1.rest_1_), channel_id=1, source_target_pairs={{0,192},{64,0},{128,64},{192,128},{1,193},{65,1},{129,65},{193,129... | collective-permute-start | bytes 2457608 | tf_op jit(solution)/shard_map/ppermute | solution.py:277
  99.7 22.4 %collective-permute-start.3 = (bf16[640,640]{1,0:T(8,128)(2,1)S(1)}, bf16[640,640]{1,0:T(8,128)(2,1)}, u32[]{:S(2)}, u32[]{:S(2)}) collective-permute-start(bf16[640,640]{1,0:T(8,128)(2,1)S(1)} %collective-permute-done.1.rest_1_), channel_id=1, source_target_pairs={{0,64},{64,128},{128,192},{192,0},{1,65},{65,129},{129,193},{193,1... | collective-permute-start | bytes 2457608 | tf_op jit(solution)/shard_map/ppermute | solution.py:277
  101.4 38.3 %collective-permute-start.6 = (bf16[640,640]{1,0:T(8,128)(2,1)S(1)}, bf16[640,640]{1,0:T(8,128)(2,1)}, u32[]{:S(2)}, u32[]{:S(2)}) collective-permute-start(bf16[640,640]{1,0:T(8,128)(2,1)S(1)} %collective-permute-done.2.rest_2_), channel_id=1, source_target_pairs={{0,64},{64,128},{128,192},{192,0},{1,65},{65,129},{129,193},{193,1... | collective-permute-start | bytes 2457608 | tf_op jit(solution)/shard_map/ppermute | solution.py:278
  102.6 37.1 %collective-permute-start.9 = (bf16[640,640]{1,0:T(8,128)(2,1)S(1)}, bf16[640,640]{1,0:T(8,128)(2,1)S(1)}, u32[]{:S(2)}, u32[]{:S(2)}) collective-permute-start(bf16[640,640]{1,0:T(8,128)(2,1)S(1)} %collective-permute-done.1.rest_1_), channel_id=1, source_target_pairs={{0,1},{1,0},{2,3},{3,2},{4,5},{5,4},{6,7},{7,6},{8,9},{9,8},{10,11... | collective-permute-start | bytes 2457608 | tf_op jit(solution)/shard_map/ppermute | solution.py:280
  102.7 37.5 %collective-permute-start.10 = (bf16[640,640]{1,0:T(8,128)(2,1)S(1)}, bf16[640,640]{1,0:T(8,128)(2,1)S(1)}, u32[]{:S(2)}, u32[]{:S(2)}) collective-permute-start(bf16[640,640]{1,0:T(8,128)(2,1)S(1)} %collective-permute-done.2.rest_2_), channel_id=1, source_target_pairs={{0,1},{1,0},{2,3},{3,2},{4,5},{5,4},{6,7},{7,6},{8,9},{9,8},{10,11... | collective-permute-start | bytes 2457608 | tf_op jit(solution)/shard_map/ppermute | solution.py:280
  120.0 20.7 %collective-permute-start.7 = (bf16[640,640]{1,0:T(8,128)(2,1)}, bf16[640,640]{1,0:T(8,128)(2,1)}, u32[]{:S(2)}, u32[]{:S(2)}) collective-permute-start(bf16[640,640]{1,0:T(8,128)(2,1)} %collective-permute-done.5.rest_5_), channel_id=1, source_target_pairs={{0,192},{64,0},{128,64},{192,128},{1,193},{65,1},{129,65},{193,129... | collective-permute-start | bytes 2457608 | tf_op jit(solution)/shard_map/ppermute | solution.py:278
  122.1 20.0 %collective-permute-start.12 = (bf16[640,640]{1,0:T(8,128)(2,1)S(1)}, bf16[640,640]{1,0:T(8,128)(2,1)}, u32[]{:S(2)}, u32[]{:S(2)}) collective-permute-start(bf16[640,640]{1,0:T(8,128)(2,1)S(1)} %collective-permute-done.4.rest_4_), channel_id=1, source_target_pairs={{0,1},{1,0},{2,3},{3,2},{4,5},{5,4},{6,7},{7,6},{8,9},{9,8},{10,11... | collective-permute-start | bytes 2457608 | tf_op jit(solution)/shard_map/ppermute | solution.py:280
  139.7 3.8 %collective-permute-start.13 = (bf16[640,640]{1,0:T(8,128)(2,1)}, bf16[640,640]{1,0:T(8,128)(2,1)}, u32[]{:S(2)}, u32[]{:S(2)}) collective-permute-start(bf16[640,640]{1,0:T(8,128)(2,1)} %collective-permute-done.5.rest_5_), channel_id=1, source_target_pairs={{0,1},{1,0},{2,3},{3,2},{4,5},{5,4},{6,7},{7,6},{8,9},{9,8},{10,11... | collective-permute-start | bytes 2457608 | tf_op jit(solution)/shard_map/ppermute | solution.py:280
  139.8 3.7 %collective-permute-start.11 = (bf16[640,640]{1,0:T(8,128)(2,1)}, bf16[640,640]{1,0:T(8,128)(2,1)}, u32[]{:S(2)}, u32[]{:S(2)}) collective-permute-start(bf16[640,640]{1,0:T(8,128)(2,1)} %collective-permute-done.3.rest_3_), channel_id=1, source_target_pairs={{0,1},{1,0},{2,3},{3,2},{4,5},{5,4},{6,7},{7,6},{8,9},{9,8},{10,11... | collective-permute-start | bytes 2457608 | tf_op jit(solution)/shard_map/ppermute | solution.py:280
  140.2 4.5 %collective-permute-start.14 = (bf16[640,640]{1,0:T(8,128)(2,1)}, bf16[640,640]{1,0:T(8,128)(2,1)}, u32[]{:S(2)}, u32[]{:S(2)}) collective-permute-start(bf16[640,640]{1,0:T(8,128)(2,1)} %collective-permute-done.6.rest_6_), channel_id=1, source_target_pairs={{0,1},{1,0},{2,3},{3,2},{4,5},{5,4},{6,7},{7,6},{8,9},{9,8},{10,11... | collective-permute-start | bytes 2457608 | tf_op jit(solution)/shard_map/ppermute | solution.py:280
  141.1 4.8 %collective-permute-start.15 = (bf16[640,640]{1,0:T(8,128)(2,1)}, bf16[640,640]{1,0:T(8,128)(2,1)}, u32[]{:S(2)}, u32[]{:S(2)}) collective-permute-start(bf16[640,640]{1,0:T(8,128)(2,1)} %collective-permute-done.7.rest_7_), channel_id=1, source_target_pairs={{0,1},{1,0},{2,3},{3,2},{4,5},{5,4},{6,7},{7,6},{8,9},{9,8},{10,11... | collective-permute-start | bytes 2457608 | tf_op jit(solution)/shard_map/ppermute | solution.py:280
  (9 other events, 252.3 us)

commit v4 on v3

--- a/solution.py
+++ b/solution.py
@@ -70,14 +70,14 @@
     return pl.pallas_call(
         outgoing_kernel,
         out_shape=jax.ShapeDtypeStruct((N_DEV, WIN, D), patches.dtype),
-        in_specs=[smem, smem, smem, pl.BlockSpec(memory_space=pl.ANY)],
-        out_specs=pl.BlockSpec(memory_space=pl.ANY),
+        in_specs=[smem, smem, smem, pl.BlockSpec(memory_space=pltpu.HBM)],
+        out_specs=pl.BlockSpec(memory_space=pltpu.HBM),
         scratch_shapes=[
             pltpu.VMEM((SRC_WIN, WIN, D), patches.dtype),
             pltpu.SemaphoreType.DMA((SRC_WIN,)),
             pltpu.SemaphoreType.DMA((SRC_WIN,)),
         ],
-        compiler_params=pltpu.CompilerParams(vmem_limit_bytes=16 * 1024 * 1024),
+        compiler_params=pltpu.CompilerParams(vmem_limit_bytes=60 * 1024 * 1024),
         name="outgoing",
     )(place, counts, perm, patches)
 
@@ -194,7 +194,7 @@
                 mixed[rows, at : at + 128] = parts[tile].astype(BF16)
         return carry
 
-    lax.fori_loop(0, DST_WIN, attend, 0)
+    lax.fori_loop(0, DST_WIN, attend, 0, unroll=True)
 
     encoded[...] = jnp.dot(mixed[...], weights[3], preferred_element_type=F32)
     for k in range(DST_WIN):
@@ -203,18 +203,21 @@
         mean = jnp.mean(values * values, axis=-1, keepdims=True)
         alive = lax.broadcasted_iota(jnp.int32, (WIN, 1), 0) < live[k]
         scale = jnp.where(alive, lax.rsqrt(mean + 1e-6), 0.0)
-        final[rows, :] = (values * scale * merge_gain[...]).astype(BF16)
-
-    lane = lax.broadcasted_iota(jnp.int32, (MERGED, ROWS), 1)
-    earlier = lax.broadcasted_iota(jnp.int32, (MERGED, ROWS), 0) < lax.shift_right_logical(lane, 2)
+        values = values * scale * merge_gain[...]
+        for t in range(D // 128):
+            final[t, rows, :] = values[:, t * 128 : t * 128 + 128]
+
+    at = lax.broadcasted_iota(jnp.int32, (MERGED, MERGED), 1)
+    earlier = lax.broadcasted_iota(jnp.int32, (MERGED, MERGED), 0) < at
     same = owner_column[...] == owner_row[...]
     rank = jnp.sum(jnp.where(same & earlier, 1, 0), axis=0, keepdims=True)
     places = owner_row[...] * CAP + rank
-    chosen = lax.broadcasted_iota(jnp.int32, (N_SEC * CAP, ROWS), 0) == places
-    turn = jnp.bitwise_and(lax.broadcasted_iota(jnp.int32, (N_SEC * CAP, ROWS), 1), 3)
+    chosen = lax.broadcasted_iota(jnp.int32, (N_SEC * CAP, MERGED), 0) == places
+    chosen = jnp.where(chosen, 1.0, 0.0).astype(BF16)
     for p in range(4):
-        pick = jnp.where(chosen & (turn == p), 1.0, 0.0).astype(BF16)
-        packed = jnp.dot(pick, final[...], preferred_element_type=F32)
+        merged = [final[t, pl.ds(p, MERGED, stride=4), :] for t in range(D // 128)]
+        merged = jnp.concatenate(merged, axis=1).astype(BF16)
+        packed = jnp.dot(chosen, merged, preferred_element_type=F32)
         out[:, p * D : (p + 1) * D] = packed.astype(BF16)
 
 
@@ -234,7 +237,7 @@
             pltpu.VMEM((3, ROWS, D), BF16),
             pltpu.VMEM((ROWS, D), BF16),
             pltpu.VMEM((ROWS, D), F32),
-            pltpu.VMEM((ROWS, D), BF16),
+            pltpu.VMEM((D // 128, ROWS, 128), F32),
             pltpu.SMEM((DST_WIN,), jnp.int32),
             pltpu.SMEM((DST_WIN,), jnp.int32),
             pltpu.SemaphoreType.DMA((4, 2, 2)),
@@ -308,7 +311,7 @@
         counts,
         perm,
         win_groups.reshape(N_DEV * SRC_WIN),
-        jnp.repeat(owner.reshape(1, MERGED), 4, axis=1),
+        owner.reshape(1, MERGED),
         owner.reshape(MERGED, 1),
         norm_gain.reshape(1, D),
         qkv_bias.reshape(3, 1, D),

time: 216 us -> 206 us (0.954)
  local copies, waits for them, and re-layouts: 9.42 us -> 3.48 us
  starting transfers between devices: 32.5 us -> 28.2 us
  Pallas kernels: 23.4 us -> 20 us
  blocking collectives: 36.3 us -> 38.6 us
    all_to_all x1, starting transfers between devices: 12.7 us -> 5.08 us  [body(): lax.all_to_all(going, ('xh', 'z', 'c'), split_axis=0, concat_axis=0, tile...]
    unnamed x32 -> x24, local copies, waits for them, and re-layouts: 8.13 us -> 2.38 us
    all_to_all x1, waiting for transfers between devices: 7.39 us -> 12.1 us  [gather_weights(): lax.all_to_all(jnp.broadcast_to(own[None], (8, 40, CHUNK)), 'z', 0, 0, ti...]
    pallas_call x1, Pallas kernels: 21.6 us -> 17.1 us  [encode(): pl.pallas_call(encode_kernel, out_shape=jax.ShapeDtypeStruct((N_SEC * CAP...]
    all_to_all x1, waiting for transfers between devices: 8.68 us -> 4.82 us  [body(): lax.all_to_all(going, ('xh', 'z', 'c'), split_axis=0, concat_axis=0, tile...]
    ppermute x1, starting transfers between devices: 0.31 us -> 3.01 us  [spread_weights(): send(across, 'y', shift(4, -1))]
    all_to_all x1, blocking collectives: 36.3 us -> 38.6 us  [body(): lax.all_to_all(packed, ('y', 'xl'), split_axis=0, concat_axis=0, tiled=True)]
where the time goes in v4:
time: 206 us; the launch traced here: 204 us
  waiting for transfers between devices  113 us (55%)
  blocking collectives  38.6 us (19%)
  starting transfers between devices  28.2 us (14%)
  Pallas kernels  20 us (10%)
  local copies, waits for them, and re-layouts  3.48 us (2%)
    all_to_all x1, blocking collectives, body(): lax.all_to_all(packed, ('y', 'xl'), split_axis=0, concat_axis=0, tiled=True)  38.6 us
    ppermute x1, waiting for transfers between devices, spread_weights(): across = send(here, ('xl', 'xh', 'c'), CROSS3)  28.8 us
    ppermute x1, waiting for transfers between devices, spread_weights(): partner = send(column, ('xl', 'c'), CROSS)  28.1 us
    ppermute x1, waiting for transfers between devices, spread_weights(): send(across, 'y', shift(4, -1))  17.5 us
    ppermute x1, waiting for transfers between devices, spread_weights(): send(up_h, 'y', shift(4, 1))  17.3 us
    pallas_call x1, Pallas kernels, encode(): pl.pallas_call(encode_kernel, out_shape=jax.ShapeDtypeStruct((N_SEC * CAP...  17.1 us
    all_to_all x1, waiting for transfers between devices, gather_weights(): lax.all_to_all(jnp.broadcast_to(own[None], (8, 40, CHUNK)), 'z', 0, 0, ti...  12.1 us
    all_to_all x1, starting transfers between devices, gather_weights(): lax.all_to_all(jnp.broadcast_to(own[None], (8, 40, CHUNK)), 'z', 0, 0, ti...  8.47 us
  transfers between devices with their start and end apart: 18, of which 10 were waited for; matrix products, arithmetic and copies ran while one was open for 0% of the time, Pallas kernels for 1%

profile of v4, /device:TPU:4, one launch (start us, length us, event | category | flops | bytes accessed | tf_op | source)
XLA Modules:
  0.0 204.1 jit_solution(11445998599830585104)
XLA Ops:
  0.0 0.8 dynamic-slice_select_fusion
  0.8 0.8 broadcast_in_dim.2
  1.6 8.5 %all-to-all-start.1 = ((bf16[8,40,640]{2,1,0:T(8,128)(2,1)}), bf16[8,40,640]{2,1,0:T(8,128)(2,1)S(1)}, u32[]{:S(2)}, u32[]{:S(2)}) async-start(bf16[8,40,640]{2,1,0:T(8,128)(2,1)} %broadcast_in_dim.2), calls=%async_computation.1 | async-start | bytes 819200 | tf_op jit(solution)/shard_map/all_to_all | solution.py:268
  10.1 2.9 %outgoing.1 = bf16[32,64,1280]{2,1,0:T(8,128)(2,1)} custom-call(s32[1]{0:T(128)} %bitcast.place, s32[32]{0:T(128)} %bitcast.20, s32[32]{0:T(128)} %bitcast.22, bf16[24,64,1280]{2,1,0:T(8,128)(2,1)} %bitcast.28), custom_call_target="tpu_custom_call" | custom-call | tf_op jit(solution)/shard_map/outgoing/pallas_call | solution.py:70
  13.0 12.1 %all-to-all-done.1 = bf16[8,40,640]{2,1,0:T(8,128)(2,1)S(1)} async-done(((bf16[8,40,640]{2,1,0:T(8,128)(2,1)}), bf16[8,40,640]{2,1,0:T(8,128)(2,1)S(1)}, u32[]{:S(2)}, u32[]{:S(2)}) %all-to-all-start.1) | async-done | bytes 409632 | tf_op jit(solution)/shard_map/all_to_all | solution.py:268
  25.1 5.1 %all-to-all-start = ((bf16[32,64,1280]{2,1,0:T(8,128)(2,1)}), bf16[32,64,1280]{2,1,0:T(8,128)(2,1)}, u32[]{:S(2)}, u32[]{:S(2)}) async-start(bf16[32,64,1280]{2,1,0:T(8,128)(2,1)} %outgoing.1), calls=%async_computation | async-start | bytes 10485760 | tf_op jit(solution)/shard_map/all_to_all | solution.py:308
  30.3 1.9 collective-permute-start
  32.3 28.1 %collective-permute-done = bf16[8,40,640]{2,1,0:T(8,128)(2,1)S(1)} collective-permute-done((bf16[8,40,640]{2,1,0:T(8,128)(2,1)S(1)}, bf16[8,40,640]{2,1,0:T(8,128)(2,1)S(1)}, u32[]{:S(2)}, u32[]{:S(2)}) %collective-permute-start) | collective-permute-done | bytes 409632 | tf_op jit(solution)/shard_map/ppermute | solution.py:275
  60.6 1.7 collective-permute-start.2
  62.2 1.7 collective-permute-start.4
  64.3 28.8 %collective-permute-done.1.rest_1_ = bf16[640,640]{1,0:T(8,128)(2,1)S(1)} collective-permute-done((bf16[640,640]{1,0:T(8,128)(2,1)S(1)}, bf16[640,640]{1,0:T(8,128)(2,1)S(1)}, u32[]{:S(2)}, u32[]{:S(2)}) %collective-permute-start.1) | collective-permute-done | bytes 819232 | tf_op jit(solution)/shard_map/ppermute | solution.py:278
  93.1 3.0 %collective-permute-start.5 = (bf16[640,640]{1,0:T(8,128)(2,1)S(1)}, bf16[640,640]{1,0:T(8,128)(2,1)}, u32[]{:S(2)}, u32[]{:S(2)}) collective-permute-start(bf16[640,640]{1,0:T(8,128)(2,1)S(1)} %collective-permute-done.1.rest_1_), channel_id=1, source_target_pairs={{0,192},{64,0},{128,64},{192,128},{1,193},{65,1},{129,65},{193,129... | collective-permute-start | bytes 2457608 | tf_op jit(solution)/shard_map/ppermute | solution.py:280
  96.1 0.6 collective-permute-start.6
  97.2 17.5 %collective-permute-done.5.rest_5_ = bf16[640,640]{1,0:T(8,128)(2,1)} collective-permute-done((bf16[640,640]{1,0:T(8,128)(2,1)S(1)}, bf16[640,640]{1,0:T(8,128)(2,1)}, u32[]{:S(2)}, u32[]{:S(2)}) %collective-permute-start.5) | collective-permute-done | bytes 819232 | tf_op jit(solution)/shard_map/ppermute | solution.py:280
  114.7 3.8 %collective-permute-start.7 = (bf16[640,640]{1,0:T(8,128)(2,1)}, bf16[640,640]{1,0:T(8,128)(2,1)}, u32[]{:S(2)}, u32[]{:S(2)}) collective-permute-start(bf16[640,640]{1,0:T(8,128)(2,1)} %collective-permute-done.5.rest_5_), channel_id=1, source_target_pairs={{0,192},{64,0},{128,64},{192,128},{1,193},{65,1},{129,65},{193,129... | collective-permute-start | bytes 2457608 | tf_op jit(solution)/shard_map/ppermute | solution.py:281
  118.6 17.3 %collective-permute-done.6.rest_6_ = bf16[640,640]{1,0:T(8,128)(2,1)} collective-permute-done((bf16[640,640]{1,0:T(8,128)(2,1)S(1)}, bf16[640,640]{1,0:T(8,128)(2,1)}, u32[]{:S(2)}, u32[]{:S(2)}) %collective-permute-start.6) | collective-permute-done | bytes 819232 | tf_op jit(solution)/shard_map/ppermute | solution.py:281
  136.8 0.6 copy-done.5
  138.1 1.6 collective-permute-done.11.rest_11_
  139.7 1.2 collective-permute-done.14.rest_14_
  140.9 1.2 collective-permute-done.15.rest_15_
  142.1 4.8 %all-to-all-done.arrived = bf16[32,64,1280]{2,1,0:T(8,128)(2,1)} async-done(((bf16[32,64,1280]{2,1,0:T(8,128)(2,1)}), bf16[32,64,1280]{2,1,0:T(8,128)(2,1)}, u32[]{:S(2)}, u32[]{:S(2)}) %all-to-all-start) | async-done | bytes 5242912 | tf_op jit(solution)/shard_map/all_to_all | solution.py:308
  146.9 17.1 %encode.1 = bf16[256,5120]{1,0:T(8,128)(2,1)} custom-call(s32[7]{0:T(128)S(1)} %stack.31.place, s32[32]{0:T(128)S(1)} %bitcast.21, s32[32]{0:T(128)S(1)} %bitcast.23, s32[768]{0:T(1024)S(1)} %reshape.35.groups, s32[1,128]{1,0:T(1,128)S(1)} %bitcast.25, s32[128,1]{1,0:T(8,128)S(1)} %copy.14.owner_column, f32[1,1280]{1,0:T(1,128)S(1)} %reshape.38.norm_gain, ...), custom_call_target="tpu_custom_call" | custom-call | tf_op jit(solution)/shard_map/encode/pallas_call | solution.py:228
  164.0 38.6 %all_to_all.19 = bf16[8,32,5120]{2,1,0:T(8,128)(2,1)S(1)} all-to-all(bf16[8,32,5120]{2,1,0:T(8,128)(2,1)} %bitcast.27), channel_id=1, replica_groups=mesh['y'=4,'xl'=2,'xh'=2,'z'=8,'c'=2] {'y','xl'}, dimensions={0} | all-to-all | bytes 5242880 | tf_op jit(solution)/shard_map/all_to_all | solution.py:323
  202.6 1.5 copy.16
  (50 shorter events, 2.9 us)
Async XLA Ops:
  1.6 23.5 %all-to-all-start.1 = ((bf16[8,40,640]{2,1,0:T(8,128)(2,1)}), bf16[8,40,640]{2,1,0:T(8,128)(2,1)S(1)}, u32[]{:S(2)}, u32[]{:S(2)}) async-start(bf16[8,40,640]{2,1,0:T(8,128)(2,1)} %broadcast_in_dim.2), calls=%async_computation.1 | async-start | bytes 819200 | tf_op jit(solution)/shard_map/all_to_all | solution.py:268
  25.1 121.8 %all-to-all-start = ((bf16[32,64,1280]{2,1,0:T(8,128)(2,1)}), bf16[32,64,1280]{2,1,0:T(8,128)(2,1)}, u32[]{:S(2)}, u32[]{:S(2)}) async-start(bf16[32,64,1280]{2,1,0:T(8,128)(2,1)} %outgoing.1), calls=%async_computation | async-start | bytes 10485760 | tf_op jit(solution)/shard_map/all_to_all | solution.py:308
  30.2 107.7 %copy-start.8 = (f32[1280]{0:T(1024)S(1)}, f32[1280]{0:T(1024)}, u32[]{:S(2)}) copy-start(f32[1280]{0:T(1024)} %param.15) | copy-start | bytes 15364
  30.3 107.7 %copy-start.6 = (f32[3840]{0:T(1024)S(1)}, f32[3840]{0:T(1024)}, u32[]{:S(2)}) copy-start(f32[3840]{0:T(1024)} %param.17) | copy-start | bytes 46084
  30.3 107.7 %copy-start.9 = (f32[1280]{0:T(1024)S(1)}, f32[1280]{0:T(1024)}, u32[]{:S(2)}) copy-start(f32[1280]{0:T(1024)} %param.19) | copy-start | bytes 15364
  30.3 107.7 %copy-start.10 = (f32[1280]{0:T(1024)S(1)}, f32[1280]{0:T(1024)}, u32[]{:S(2)}) copy-start(f32[1280]{0:T(1024)} %param.20) | copy-start | bytes 15364
  30.3 116.6 %copy-start = (s32[1,32]{1,0:T(1,128)S(1)}, s32[1,32]{1,0:T(1,128)}, u32[]{:S(2)}) copy-start(s32[1,32]{1,0:T(1,128)} %param.12) | copy-start | bytes 388
  30.3 116.6 %copy-start.1 = (s32[1,32]{1,0:T(1,128)S(1)}, s32[1,32]{1,0:T(1,128)}, u32[]{:S(2)}) copy-start(s32[1,32]{1,0:T(1,128)} %param.13) | copy-start | bytes 388
  30.3 30.0 %collective-permute-start = (bf16[8,40,640]{2,1,0:T(8,128)(2,1)S(1)}, bf16[8,40,640]{2,1,0:T(8,128)(2,1)S(1)}, u32[]{:S(2)}, u32[]{:S(2)}) collective-permute-start(bf16[8,40,640]{2,1,0:T(8,128)(2,1)S(1)} %all-to-all-done.1), channel_id=1, source_target_pairs={{0,33},{1,32},{32,1},{33,0},{2,35},{3,34},{34,3},{35,2},{4,37},{5,... | collective-permute-start | bytes 1228808 | tf_op jit(solution)/shard_map/ppermute | solution.py:275
  60.5 32.6 %collective-permute-start.1 = (bf16[640,640]{1,0:T(8,128)(2,1)S(1)}, bf16[640,640]{1,0:T(8,128)(2,1)S(1)}, u32[]{:S(2)}, u32[]{:S(2)}) collective-permute-start(bf16[640,640]{1,0:T(8,128)(2,1)S(1)} %bitcast.15), channel_id=1, source_target_pairs={{0,49},{1,48},{16,33},{17,32},{32,17},{33,16},{48,1},{49,0},{2,51}... | collective-permute-start | bytes 2457608 | tf_op jit(solution)/shard_map/ppermute | solution.py:278
  60.6 35.5 %collective-permute-start.2 = (bf16[640,640]{1,0:T(8,128)(2,1)S(1)}, bf16[640,640]{1,0:T(8,128)(2,1)S(1)}, u32[]{:S(2)}, u32[]{:S(2)}) collective-permute-start(bf16[640,640]{1,0:T(8,128)(2,1)S(1)} %bitcast.16), channel_id=1, source_target_pairs={{0,64},{64,128},{128,192},{192,0},{1,65},{65,129},{129,193},{193,1... | collective-permute-start | bytes 2457608 | tf_op jit(solution)/shard_map/ppermute | solution.py:279
  62.2 34.5 %collective-permute-start.4 = (bf16[640,640]{1,0:T(8,128)(2,1)S(1)}, bf16[640,640]{1,0:T(8,128)(2,1)S(1)}, u32[]{:S(2)}, u32[]{:S(2)}) collective-permute-start(bf16[640,640]{1,0:T(8,128)(2,1)S(1)} %bitcast.17), channel_id=1, source_target_pairs={{0,192},{64,0},{128,64},{192,128},{1,193},{65,1},{129,65},{193,129... | collective-permute-start | bytes 2457608 | tf_op jit(solution)/shard_map/ppermute | solution.py:279
  63.9 33.1 %collective-permute-start.8 = (bf16[640,640]{1,0:T(8,128)(2,1)S(1)}, bf16[640,640]{1,0:T(8,128)(2,1)S(1)}, u32[]{:S(2)}, u32[]{:S(2)}) collective-permute-start(bf16[640,640]{1,0:T(8,128)(2,1)S(1)} %bitcast.18), channel_id=1, source_target_pairs={{0,1},{1,0},{2,3},{3,2},{4,5},{5,4},{6,7},{7,6},{8,9},{9,8},{10,11... | collective-permute-start | bytes 2457608 | tf_op jit(solution)/shard_map/ppermute | solution.py:283
  93.1 21.6 %collective-permute-start.5 = (bf16[640,640]{1,0:T(8,128)(2,1)S(1)}, bf16[640,640]{1,0:T(8,128)(2,1)}, u32[]{:S(2)}, u32[]{:S(2)}) collective-permute-start(bf16[640,640]{1,0:T(8,128)(2,1)S(1)} %collective-permute-done.1.rest_1_), channel_id=1, source_target_pairs={{0,192},{64,0},{128,64},{192,128},{1,193},{65,1},{129,65},{193,129... | collective-permute-start | bytes 2457608 | tf_op jit(solution)/shard_map/ppermute | solution.py:280
  96.1 22.4 %collective-permute-start.3 = (bf16[640,640]{1,0:T(8,128)(2,1)S(1)}, bf16[640,640]{1,0:T(8,128)(2,1)}, u32[]{:S(2)}, u32[]{:S(2)}) collective-permute-start(bf16[640,640]{1,0:T(8,128)(2,1)S(1)} %collective-permute-done.1.rest_1_), channel_id=1, source_target_pairs={{0,64},{64,128},{128,192},{192,0},{1,65},{65,129},{129,193},{193,1... | collective-permute-start | bytes 2457608 | tf_op jit(solution)/shard_map/ppermute | solution.py:280
  96.1 39.8 %collective-permute-start.6 = (bf16[640,640]{1,0:T(8,128)(2,1)S(1)}, bf16[640,640]{1,0:T(8,128)(2,1)}, u32[]{:S(2)}, u32[]{:S(2)}) collective-permute-start(bf16[640,640]{1,0:T(8,128)(2,1)S(1)} %collective-permute-done.2.rest_2_), channel_id=1, source_target_pairs={{0,64},{64,128},{128,192},{192,0},{1,65},{65,129},{129,193},{193,1... | collective-permute-start | bytes 2457608 | tf_op jit(solution)/shard_map/ppermute | solution.py:281
  96.7 39.2 %collective-permute-start.9 = (bf16[640,640]{1,0:T(8,128)(2,1)S(1)}, bf16[640,640]{1,0:T(8,128)(2,1)S(1)}, u32[]{:S(2)}, u32[]{:S(2)}) collective-permute-start(bf16[640,640]{1,0:T(8,128)(2,1)S(1)} %collective-permute-done.1.rest_1_), channel_id=1, source_target_pairs={{0,1},{1,0},{2,3},{3,2},{4,5},{5,4},{6,7},{7,6},{8,9},{9,8},{10,11... | collective-permute-start | bytes 2457608 | tf_op jit(solution)/shard_map/ppermute | solution.py:283
  97.0 39.4 %collective-permute-start.10 = (bf16[640,640]{1,0:T(8,128)(2,1)S(1)}, bf16[640,640]{1,0:T(8,128)(2,1)S(1)}, u32[]{:S(2)}, u32[]{:S(2)}) collective-permute-start(bf16[640,640]{1,0:T(8,128)(2,1)S(1)} %collective-permute-done.2.rest_2_), channel_id=1, source_target_pairs={{0,1},{1,0},{2,3},{3,2},{4,5},{5,4},{6,7},{7,6},{8,9},{9,8},{10,11... | collective-permute-start | bytes 2457608 | tf_op jit(solution)/shard_map/ppermute | solution.py:283
  114.7 22.1 %collective-permute-start.7 = (bf16[640,640]{1,0:T(8,128)(2,1)}, bf16[640,640]{1,0:T(8,128)(2,1)}, u32[]{:S(2)}, u32[]{:S(2)}) collective-permute-start(bf16[640,640]{1,0:T(8,128)(2,1)} %collective-permute-done.5.rest_5_), channel_id=1, source_target_pairs={{0,192},{64,0},{128,64},{192,128},{1,193},{65,1},{129,65},{193,129... | collective-permute-start | bytes 2457608 | tf_op jit(solution)/shard_map/ppermute | solution.py:281
  118.5 19.6 %collective-permute-start.12 = (bf16[640,640]{1,0:T(8,128)(2,1)S(1)}, bf16[640,640]{1,0:T(8,128)(2,1)}, u32[]{:S(2)}, u32[]{:S(2)}) collective-permute-start(bf16[640,640]{1,0:T(8,128)(2,1)S(1)} %collective-permute-done.4.rest_4_), channel_id=1, source_target_pairs={{0,1},{1,0},{2,3},{3,2},{4,5},{5,4},{6,7},{7,6},{8,9},{9,8},{10,11... | collective-permute-start | bytes 2457608 | tf_op jit(solution)/shard_map/ppermute | solution.py:283
  135.9 3.8 %collective-permute-start.13 = (bf16[640,640]{1,0:T(8,128)(2,1)}, bf16[640,640]{1,0:T(8,128)(2,1)}, u32[]{:S(2)}, u32[]{:S(2)}) collective-permute-start(bf16[640,640]{1,0:T(8,128)(2,1)} %collective-permute-done.5.rest_5_), channel_id=1, source_target_pairs={{0,1},{1,0},{2,3},{3,2},{4,5},{5,4},{6,7},{7,6},{8,9},{9,8},{10,11... | collective-permute-start | bytes 2457608 | tf_op jit(solution)/shard_map/ppermute | solution.py:283
  135.9 3.8 %collective-permute-start.11 = (bf16[640,640]{1,0:T(8,128)(2,1)}, bf16[640,640]{1,0:T(8,128)(2,1)}, u32[]{:S(2)}, u32[]{:S(2)}) collective-permute-start(bf16[640,640]{1,0:T(8,128)(2,1)} %collective-permute-done.3.rest_3_), channel_id=1, source_target_pairs={{0,1},{1,0},{2,3},{3,2},{4,5},{5,4},{6,7},{7,6},{8,9},{9,8},{10,11... | collective-permute-start | bytes 2457608 | tf_op jit(solution)/shard_map/ppermute | solution.py:283
  136.4 4.5 %collective-permute-start.14 = (bf16[640,640]{1,0:T(8,128)(2,1)}, bf16[640,640]{1,0:T(8,128)(2,1)}, u32[]{:S(2)}, u32[]{:S(2)}) collective-permute-start(bf16[640,640]{1,0:T(8,128)(2,1)} %collective-permute-done.6.rest_6_), channel_id=1, source_target_pairs={{0,1},{1,0},{2,3},{3,2},{4,5},{5,4},{6,7},{7,6},{8,9},{9,8},{10,11... | collective-permute-start | bytes 2457608 | tf_op jit(solution)/shard_map/ppermute | solution.py:283
  137.4 4.7 %collective-permute-start.15 = (bf16[640,640]{1,0:T(8,128)(2,1)}, bf16[640,640]{1,0:T(8,128)(2,1)}, u32[]{:S(2)}, u32[]{:S(2)}) collective-permute-start(bf16[640,640]{1,0:T(8,128)(2,1)} %collective-permute-done.7.rest_7_), channel_id=1, source_target_pairs={{0,1},{1,0},{2,3},{3,2},{4,5},{5,4},{6,7},{7,6},{8,9},{9,8},{10,11... | collective-permute-start | bytes 2457608 | tf_op jit(solution)/shard_map/ppermute | solution.py:283
  (5 other events, 256.2 us)

commit v5 on v4

--- a/solution.py
+++ b/solution.py
@@ -22,6 +22,8 @@
 COLS = 4 * D
 CHUNK = 640
 HALF = 640
+PART = 320
+PIECES = 9
 EXP2_SCALE = HD ** (-0.5) * math.log2(math.e)
 VMEM_LIMIT = 48 * 1024 * 1024
 
@@ -29,7 +31,7 @@
 BF16 = jnp.bfloat16
 
 
-def outgoing_kernel(place, counts, perm, patches, out, staged, in_sem, out_sem):
+def outgoing_kernel(place, counts, perm, groups, patches, out, table, staged, in_sem, out_sem):
     pos = place[0]
     mine = counts[pos]
 
@@ -58,6 +60,25 @@
             load(i).wait()
             save(i).start()
 
+    def find(r, found):
+        return jnp.where(perm[r] == pos, r, found)
+
+    residue = lax.fori_loop(0, N_DEV, find, jnp.int32(0))
+
+    def locate(d, before):
+        count = counts[d]
+        within = jnp.bitwise_and(residue - before, N_DEV - 1)
+
+        @pl.when(within < count)
+        def _():
+            slot = lax.shift_right_logical(before + within, 5)
+            table[slot] = d
+            table[DST_WIN + slot] = 4 * groups[d * SRC_WIN + within]
+
+        return before + count
+
+    lax.fori_loop(0, N_DEV, locate, jnp.int32(0))
+
     for i in range(SRC_WIN):
 
         @pl.when(i < mine)
@@ -65,13 +86,16 @@
             save(i).wait()
 
 
-def outgoing(place, counts, perm, patches):
+def outgoing(place, counts, perm, groups, patches):
     smem = pl.BlockSpec(memory_space=pltpu.SMEM)
     return pl.pallas_call(
         outgoing_kernel,
-        out_shape=jax.ShapeDtypeStruct((N_DEV, WIN, D), patches.dtype),
-        in_specs=[smem, smem, smem, pl.BlockSpec(memory_space=pltpu.HBM)],
-        out_specs=pl.BlockSpec(memory_space=pltpu.HBM),
+        out_shape=(
+            jax.ShapeDtypeStruct((N_DEV, WIN, D), patches.dtype),
+            jax.ShapeDtypeStruct((2 * DST_WIN,), jnp.int32),
+        ),
+        in_specs=[smem, smem, smem, smem, pl.BlockSpec(memory_space=pltpu.HBM)],
+        out_specs=(pl.BlockSpec(memory_space=pltpu.HBM), smem),
         scratch_shapes=[
             pltpu.VMEM((SRC_WIN, WIN, D), patches.dtype),
             pltpu.SemaphoreType.DMA((SRC_WIN,)),
@@ -79,14 +103,12 @@
         ],
         compiler_params=pltpu.CompilerParams(vmem_limit_bytes=60 * 1024 * 1024),
         name="outgoing",
-    )(place, counts, perm, patches)
+    )(place, counts, perm, groups, patches)
 
 
 def encode_kernel(
     place,
-    counts,
-    perm,
-    groups,
+    table,
     owner_row,
     owner_column,
     norm_gain,
@@ -96,50 +118,35 @@
     arrived,
     *rest,
 ):
-    pieces = rest[:16]
-    out, weights, windows, normed, triple, mixed, encoded, final, source, live, wsem, xsem = rest[16:]
-    pos, here, side = place[0], place[1], place[2]
-
-    def find(r, found):
-        return jnp.where(perm[r] == pos, r, found)
-
-    residue = lax.fori_loop(0, N_DEV, find, jnp.int32(0))
-
-    def locate(d, begin):
-        count = counts[d]
-        within = jnp.bitwise_and(residue - begin, N_DEV - 1)
-
-        @pl.when(within < count)
-        def _():
-            slot = lax.shift_right_logical(begin + within, 5)
-            source[slot] = d
-            live[slot] = 4 * groups[d * SRC_WIN + within]
-
-        return begin + count
-
-    lax.fori_loop(0, N_DEV, locate, jnp.int32(0))
+    pieces = rest[: 2 * PIECES]
+    out, weights, windows, normed, triple, mixed, encoded, final, wsem, xsem = rest[2 * PIECES :]
+    here, side = place[0], place[1]
 
     def window_copy(k):
         return pltpu.make_async_copy(
-            arrived.at[source[k]], windows.at[pl.ds(k * WIN, WIN)], xsem.at[k]
+            arrived.at[table[k]], windows.at[pl.ds(k * WIN, WIN)], xsem.at[k]
         )
 
-    def weight_copy(n, core, across):
-        row = jnp.bitwise_xor(here, across) * HALF
+    def weight_copy(core, piece):
+        n, across = min(piece // 2, 3), min(piece % 2 + piece // 8, 1)
+        rows = PART if piece >= 7 else HALF
+        row = jnp.bitwise_xor(here, across) * HALF + (PART if piece == 8 else 0)
         column = jnp.bitwise_xor(side, core) * CHUNK
         to = weights.at[
-            place[3 + n],
-            pl.ds(pl.multiple_of(row, HALF), HALF),
+            place[2 + n],
+            pl.ds(pl.multiple_of(row, PART), rows),
             pl.ds(pl.multiple_of(column, CHUNK), CHUNK),
         ]
-        return pltpu.make_async_copy(pieces[8 * core + 2 * n + across], to, wsem.at[n, core, across])
+        return pltpu.make_async_copy(pieces[PIECES * core + piece], to, wsem.at[core, piece])
+
+    def block_copies(n):
+        return [weight_copy(core, p) for core in range(2) for p in ((2 * n, 2 * n + 1) if n < 3 else (6, 7, 8))]
 
     for k in range(DST_WIN):
         window_copy(k).start()
     for n in range(4):
-        for core in range(2):
-            for across in range(2):
-                weight_copy(n, core, across).start()
+        for copy in block_copies(n):
+            copy.start()
     for k in range(DST_WIN):
         window_copy(k).wait()
         rows = pl.ds(k * WIN, WIN)
@@ -148,10 +155,9 @@
         normed[rows, :] = (values * lax.rsqrt(mean + 1e-6) * norm_gain[...]).astype(BF16)
 
     for n in range(4):
-        block = place[3 + n]
-        for core in range(2):
-            for across in range(2):
-                weight_copy(n, core, across).wait()
+        block = place[2 + n]
+        for copy in block_copies(n):
+            copy.wait()
 
         @pl.when(block < 3)
         def _(block=block):
@@ -160,7 +166,7 @@
 
     def attend(w, carry):
         rows = pl.ds(pl.multiple_of(w * WIN, WIN), WIN)
-        dead = lax.broadcasted_iota(jnp.int32, (WIN, 2 * WIN), 0) >= live[w]
+        dead = lax.broadcasted_iota(jnp.int32, (WIN, 2 * WIN), 0) >= table[DST_WIN + w]
         zero = jnp.zeros((), BF16)
         for half in range(2):
             parts = [None] * (CHUNK // 128)
@@ -201,7 +207,7 @@
         rows = pl.ds(k * WIN, WIN)
         values = windows[rows, :].astype(F32) + encoded[rows, :] + proj_bias[...]
         mean = jnp.mean(values * values, axis=-1, keepdims=True)
-        alive = lax.broadcasted_iota(jnp.int32, (WIN, 1), 0) < live[k]
+        alive = lax.broadcasted_iota(jnp.int32, (WIN, 1), 0) < table[DST_WIN + k]
         scale = jnp.where(alive, lax.rsqrt(mean + 1e-6), 0.0)
         values = values * scale * merge_gain[...]
         for t in range(D // 128):
@@ -221,14 +227,14 @@
         out[:, p * D : (p + 1) * D] = packed.astype(BF16)
 
 
-def encode(place, counts, perm, groups, owner_row, owner_column, gain, qb, pb, mg, arrived, pieces):
+def encode(place, table, owner_row, owner_column, gain, qb, pb, mg, arrived, pieces):
     smem = pl.BlockSpec(memory_space=pltpu.SMEM)
     vmem = pl.BlockSpec(memory_space=pltpu.VMEM)
     hbm = pl.BlockSpec(memory_space=pl.ANY)
     return pl.pallas_call(
         encode_kernel,
         out_shape=jax.ShapeDtypeStruct((N_SEC * CAP, COLS), BF16),
-        in_specs=[smem] * 4 + [vmem] * 6 + [hbm] * 17,
+        in_specs=[smem] * 2 + [vmem] * 6 + [hbm] * (1 + 2 * PIECES),
         out_specs=vmem,
         scratch_shapes=[
             pltpu.VMEM((4, D, D), BF16),
@@ -238,14 +244,12 @@
             pltpu.VMEM((ROWS, D), BF16),
             pltpu.VMEM((ROWS, D), F32),
             pltpu.VMEM((D // 128, ROWS, 128), F32),
-            pltpu.SMEM((DST_WIN,), jnp.int32),
-            pltpu.SMEM((DST_WIN,), jnp.int32),
-            pltpu.SemaphoreType.DMA((4, 2, 2)),
+            pltpu.SemaphoreType.DMA((2, PIECES)),
             pltpu.SemaphoreType.DMA((DST_WIN,)),
         ],
         compiler_params=pltpu.CompilerParams(vmem_limit_bytes=VMEM_LIMIT),
         name="encode",
-    )(place, counts, perm, groups, owner_row, owner_column, gain, qb, pb, mg, arrived, *pieces)
+    )(place, table, owner_row, owner_column, gain, qb, pb, mg, arrived, *pieces)
 
 
 def shift(n, k):
@@ -278,8 +282,9 @@
     across = send(here, ("xl", "xh", "c"), CROSS3)
     up_h, down_h = send(here, "y", shift(4, 1)), send(here, "y", shift(4, -1))
     up_a, down_a = send(across, "y", shift(4, 1)), send(across, "y", shift(4, -1))
-    far_h, far_a = send(up_h, "y", shift(4, 1)), send(down_a, "y", shift(4, -1))
-    pieces = [here, across, up_h, up_a, down_h, down_a, far_h, far_a]
+    far_h = send(up_h, "y", shift(4, 1))
+    far_low, far_high = send(up_a[:PART], "y", shift(4, 1)), send(down_a[PART:], "y", shift(4, -1))
+    pieces = [here, across, up_h, up_a, down_h, down_a, far_h, far_low, far_high]
     pieces = pieces + [send(p, "c", SWAP) for p in pieces]
     return pieces, [xh, side] + [jnp.mod(y - step, 4) for step in (0, 1, -1, 2)]
 
@@ -300,17 +305,19 @@
     position = lax.axis_index(("xh", "z", "c"))
     counts, perm = win_count[0], dest_perm[0]
     column, side = gather_weights(qkv_weight, proj_weight)
-    going = outgoing(
-        position.astype(jnp.int32).reshape(1), counts, perm, patches.reshape(SRC_WIN, WIN, D)
+    going, table = outgoing(
+        position.astype(jnp.int32).reshape(1),
+        counts,
+        perm,
+        win_groups.reshape(N_DEV * SRC_WIN),
+        patches.reshape(SRC_WIN, WIN, D),
     )
     pieces, placed = spread_weights(column, side)
-    place = jnp.stack([position] + placed).astype(jnp.int32)
+    place = jnp.stack(placed).astype(jnp.int32)
     arrived = lax.all_to_all(going, ("xh", "z", "c"), split_axis=0, concat_axis=0, tiled=True)
     packed = encode(
         place,
-        counts,
-        perm,
-        win_groups.reshape(N_DEV * SRC_WIN),
+        table,
         owner.reshape(1, MERGED),
         owner.reshape(MERGED, 1),
         norm_gain.reshape(1, D),

time: 206 us -> 211 us (1.024)
  the two profiles are of different devices: /device:TPU:4 before, /device:TPU:128 now
where the time goes in v5:
time: 211 us
  waiting for transfers between devices  112 us (53%)
  blocking collectives  37.7 us (18%)
  starting transfers between devices  31.9 us (15%)
  Pallas kernels  21.6 us (10%)
  local copies, waits for them, and re-layouts  6.24 us (3%)
    all_to_all x1, blocking collectives, body(): lax.all_to_all(packed, ('y', 'xl'), split_axis=0, concat_axis=0, tiled=True)  37.7 us
    ppermute x1, waiting for transfers between devices, spread_weights(): across = send(here, ('xl', 'xh', 'c'), CROSS3)  32.1 us
    ppermute x1, waiting for transfers between devices, spread_weights(): partner = send(column, ('xl', 'c'), CROSS)  31.3 us
    ppermute x1, waiting for transfers between devices, spread_weights(): send(across, 'y', shift(4, 1))  18.4 us
    pallas_call x1, Pallas kernels, encode(): pl.pallas_call(encode_kernel, out_shape=jax.ShapeDtypeStruct((N_SEC * CAP...  16.5 us
    ppermute x1, waiting for transfers between devices, spread_weights(): far_h = send(up_h, 'y', shift(4, 1))  15.2 us
    all_to_all x1, starting transfers between devices, body(): lax.all_to_all(going, ('xh', 'z', 'c'), split_axis=0, concat_axis=0, tile...  9.89 us
    all_to_all x1, starting transfers between devices, gather_weights(): lax.all_to_all(jnp.broadcast_to(own[None], (8, 40, CHUNK)), 'z', 0, 0, ti...  7.21 us
  transfers between devices with their start and end apart: 20, of which 8 were waited for; matrix products, arithmetic and copies ran while one was open for 1% of the time, Pallas kernels for 2%

profile of v5, /device:TPU:128, one launch (start us, length us, event | category | flops | bytes accessed | tf_op | source)
XLA Modules:
  0.0 210.5 jit_solution(7882591476311460672)
XLA Ops:
  1.6 7.2 %all-to-all-start.1 = ((bf16[8,40,640]{2,1,0:T(8,128)(2,1)}), bf16[8,40,640]{2,1,0:T(8,128)(2,1)S(1)}, u32[]{:S(2)}, u32[]{:S(2)}) async-start(bf16[8,40,640]{2,1,0:T(8,128)(2,1)} %broadcast_in_dim.2), calls=%async_computation.1 | async-start | bytes 819200 | tf_op jit(solution)/shard_map/all_to_all | solution.py:272
  10.3 5.1 %outgoing.1 = (bf16[32,64,1280]{2,1,0:T(8,128)(2,1)}, s32[16]{0:T(128)}) custom-call(s32[1]{0:T(128)} %bitcast.6.place, s32[32]{0:T(128)} %bitcast.25, s32[32]{0:T(128)} %bitcast.26, s32[768]{0:T(1024)} %reshape.38.groups, bf16[24,64,1280]{2,1,0:T(8,128)(2,1)} %bitcast.24), custom_call_target="tpu_custom_call" | custom-call | tf_op jit(solution)/shard_map/outgoing/pallas_call | solution.py:91
  15.4 3.1 %all-to-all-done.1 = bf16[8,40,640]{2,1,0:T(8,128)(2,1)S(1)} async-done(((bf16[8,40,640]{2,1,0:T(8,128)(2,1)}), bf16[8,40,640]{2,1,0:T(8,128)(2,1)S(1)}, u32[]{:S(2)}, u32[]{:S(2)}) %all-to-all-start.1) | async-done | bytes 409632 | tf_op jit(solution)/shard_map/all_to_all | solution.py:272
  18.5 9.9 %all-to-all-start = ((bf16[32,64,1280]{2,1,0:T(8,128)(2,1)}), bf16[32,64,1280]{2,1,0:T(8,128)(2,1)}, u32[]{:S(2)}, u32[]{:S(2)}) async-start(bf16[32,64,1280]{2,1,0:T(8,128)(2,1)} %get-tuple-element.8), calls=%async_computation | async-start | bytes 10485760 | tf_op jit(solution)/shard_map/all_to_all | solution.py:317
  28.5 1.3 collective-permute-start
  29.8 31.3 %collective-permute-done = bf16[8,40,640]{2,1,0:T(8,128)(2,1)S(1)} collective-permute-done((bf16[8,40,640]{2,1,0:T(8,128)(2,1)S(1)}, bf16[8,40,640]{2,1,0:T(8,128)(2,1)S(1)}, u32[]{:S(2)}, u32[]{:S(2)}) %collective-permute-start) | collective-permute-done | bytes 409632 | tf_op jit(solution)/shard_map/ppermute | solution.py:279
  61.2 2.4 %collective-permute-start.1 = (bf16[640,640]{1,0:T(8,128)(2,1)S(1)}, bf16[640,640]{1,0:T(8,128)(2,1)S(1)}, u32[]{:S(2)}, u32[]{:S(2)}) collective-permute-start(bf16[640,640]{1,0:T(8,128)(2,1)S(1)} %bitcast.15), channel_id=1, source_target_pairs={{0,49},{1,48},{16,33},{17,32},{32,17},{33,16},{48,1},{49,0},{2,51}... | collective-permute-start | bytes 2457608 | tf_op jit(solution)/shard_map/ppermute | solution.py:282
  63.7 1.6 collective-permute-start.2
  65.2 1.7 collective-permute-start.4
  66.9 32.1 %collective-permute-done.1.rest_1_ = bf16[640,640]{1,0:T(8,128)(2,1)S(1)} collective-permute-done((bf16[640,640]{1,0:T(8,128)(2,1)S(1)}, bf16[640,640]{1,0:T(8,128)(2,1)S(1)}, u32[]{:S(2)}, u32[]{:S(2)}) %collective-permute-start.1) | collective-permute-done | bytes 819232 | tf_op jit(solution)/shard_map/ppermute | solution.py:282
  99.0 1.6 collective-permute-start.3
  100.6 1.7 collective-permute-start.5
  102.9 18.4 %collective-permute-done.3.rest_3_ = bf16[640,640]{1,0:T(8,128)(2,1)S(1)} collective-permute-done((bf16[640,640]{1,0:T(8,128)(2,1)S(1)}, bf16[640,640]{1,0:T(8,128)(2,1)S(1)}, u32[]{:S(2)}, u32[]{:S(2)}) %collective-permute-start.3) | collective-permute-done | bytes 819232 | tf_op jit(solution)/shard_map/ppermute | solution.py:284
  121.8 1.0 slice.9
  122.9 0.9 collective-permute-start.7
  123.8 15.2 %collective-permute-done.6.rest_6_ = bf16[640,640]{1,0:T(8,128)(2,1)} collective-permute-done((bf16[640,640]{1,0:T(8,128)(2,1)S(1)}, bf16[640,640]{1,0:T(8,128)(2,1)}, u32[]{:S(2)}, u32[]{:S(2)}) %collective-permute-start.6) | collective-permute-done | bytes 819232 | tf_op jit(solution)/shard_map/ppermute | solution.py:285
  139.7 1.9 collective-permute-start.8
  141.5 5.7 %collective-permute-done.7.rest_7_ = bf16[320,640]{1,0:T(8,128)(2,1)} collective-permute-done((bf16[320,640]{1,0:T(8,128)(2,1)S(1)}, bf16[320,640]{1,0:T(8,128)(2,1)}, u32[]{:S(2)}, u32[]{:S(2)}) %collective-permute-start.7) | collective-permute-done | bytes 409632 | tf_op jit(solution)/shard_map/ppermute | solution.py:286
  147.3 4.3 %collective-permute-done.8.rest_8_ = bf16[320,640]{1,0:T(8,128)(2,1)} collective-permute-done((bf16[320,640]{1,0:T(8,128)(2,1)S(1)}, bf16[320,640]{1,0:T(8,128)(2,1)}, u32[]{:S(2)}, u32[]{:S(2)}) %collective-permute-start.8) | collective-permute-done | bytes 409632 | tf_op jit(solution)/shard_map/ppermute | solution.py:286
  152.0 1.7 collective-permute-done.17.rest_17_
  153.7 1.1 copy-done.1
  154.9 16.5 %encode.1 = bf16[256,5120]{1,0:T(8,128)(2,1)} custom-call(s32[6]{0:T(128)S(1)} %stack.27.place, s32[16]{0:T(128)S(1)} %copy-done.3, s32[1,128]{1,0:T(1,128)S(1)} %bitcast.21, s32[128,1]{1,0:T(8,128)S(1)} %copy.14.owner_column, f32[1,1280]{1,0:T(1,128)S(1)} %reshape.42.norm_gain, f32[3,1,1280]{2,1,0:T(1,128)S(1)} %reshape.43.qkv_bias, ...), custom_call_target="tpu_custom_call" | custom-call | tf_op jit(solution)/shard_map/encode/pallas_call | solution.py:234
  171.4 37.7 %all_to_all.19 = bf16[8,32,5120]{2,1,0:T(8,128)(2,1)S(1)} all-to-all(bf16[8,32,5120]{2,1,0:T(8,128)(2,1)} %bitcast.22), channel_id=1, replica_groups=mesh['y'=4,'xl'=2,'xh'=2,'z'=8,'c'=2] {'y','xl'}, dimensions={0} | all-to-all | bytes 5242880 | tf_op jit(solution)/shard_map/all_to_all | solution.py:330
  209.1 1.5 copy.16
  (58 shorter events, 5.4 us)
Async XLA Ops:
  1.6 16.9 %all-to-all-start.1 = ((bf16[8,40,640]{2,1,0:T(8,128)(2,1)}), bf16[8,40,640]{2,1,0:T(8,128)(2,1)S(1)}, u32[]{:S(2)}, u32[]{:S(2)}) async-start(bf16[8,40,640]{2,1,0:T(8,128)(2,1)} %broadcast_in_dim.2), calls=%async_computation.1 | async-start | bytes 819200 | tf_op jit(solution)/shard_map/all_to_all | solution.py:272
  18.5 135.2 %all-to-all-start = ((bf16[32,64,1280]{2,1,0:T(8,128)(2,1)}), bf16[32,64,1280]{2,1,0:T(8,128)(2,1)}, u32[]{:S(2)}, u32[]{:S(2)}) async-start(bf16[32,64,1280]{2,1,0:T(8,128)(2,1)} %get-tuple-element.8), calls=%async_computation | async-start | bytes 10485760 | tf_op jit(solution)/shard_map/all_to_all | solution.py:317
  28.4 123.3 %copy-start.8 = (f32[3840]{0:T(1024)S(1)}, f32[3840]{0:T(1024)}, u32[]{:S(2)}) copy-start(f32[3840]{0:T(1024)} %param.17) | copy-start | bytes 46084
  28.4 123.4 %copy-start.10 = (f32[1280]{0:T(1024)S(1)}, f32[1280]{0:T(1024)}, u32[]{:S(2)}) copy-start(f32[1280]{0:T(1024)} %param.19) | copy-start | bytes 15364
  28.5 123.4 %copy-start.11 = (f32[1280]{0:T(1024)S(1)}, f32[1280]{0:T(1024)}, u32[]{:S(2)}) copy-start(f32[1280]{0:T(1024)} %param.20) | copy-start | bytes 15364
  28.5 125.3 %copy-start.3 = (s32[16]{0:T(128)S(1)}, s32[16]{0:T(128)}, u32[]{:S(2)}) copy-start(s32[16]{0:T(128)} %get-tuple-element.7.table) | copy-start | bytes 196
  28.5 32.6 %collective-permute-start = (bf16[8,40,640]{2,1,0:T(8,128)(2,1)S(1)}, bf16[8,40,640]{2,1,0:T(8,128)(2,1)S(1)}, u32[]{:S(2)}, u32[]{:S(2)}) collective-permute-start(bf16[8,40,640]{2,1,0:T(8,128)(2,1)S(1)} %all-to-all-done.1), channel_id=1, source_target_pairs={{0,33},{1,32},{32,1},{33,0},{2,35},{3,34},{34,3},{35,2},{4,37},{5,... | collective-permute-start | bytes 1228808 | tf_op jit(solution)/shard_map/ppermute | solution.py:279
  61.2 37.8 %collective-permute-start.1 = (bf16[640,640]{1,0:T(8,128)(2,1)S(1)}, bf16[640,640]{1,0:T(8,128)(2,1)S(1)}, u32[]{:S(2)}, u32[]{:S(2)}) collective-permute-start(bf16[640,640]{1,0:T(8,128)(2,1)S(1)} %bitcast.15), channel_id=1, source_target_pairs={{0,49},{1,48},{16,33},{17,32},{32,17},{33,16},{48,1},{49,0},{2,51}... | collective-permute-start | bytes 2457608 | tf_op jit(solution)/shard_map/ppermute | solution.py:282
  63.7 38.6 %collective-permute-start.2 = (bf16[640,640]{1,0:T(8,128)(2,1)S(1)}, bf16[640,640]{1,0:T(8,128)(2,1)S(1)}, u32[]{:S(2)}, u32[]{:S(2)}) collective-permute-start(bf16[640,640]{1,0:T(8,128)(2,1)S(1)} %bitcast.16), channel_id=1, source_target_pairs={{0,64},{64,128},{128,192},{192,0},{1,65},{65,129},{129,193},{193,1... | collective-permute-start | bytes 2457608 | tf_op jit(solution)/shard_map/ppermute | solution.py:283
  65.2 37.4 %collective-permute-start.4 = (bf16[640,640]{1,0:T(8,128)(2,1)S(1)}, bf16[640,640]{1,0:T(8,128)(2,1)S(1)}, u32[]{:S(2)}, u32[]{:S(2)}) collective-permute-start(bf16[640,640]{1,0:T(8,128)(2,1)S(1)} %bitcast.17), channel_id=1, source_target_pairs={{0,192},{64,0},{128,64},{192,128},{1,193},{65,1},{129,65},{193,129... | collective-permute-start | bytes 2457608 | tf_op jit(solution)/shard_map/ppermute | solution.py:283
  99.0 22.3 %collective-permute-start.3 = (bf16[640,640]{1,0:T(8,128)(2,1)S(1)}, bf16[640,640]{1,0:T(8,128)(2,1)S(1)}, u32[]{:S(2)}, u32[]{:S(2)}) collective-permute-start(bf16[640,640]{1,0:T(8,128)(2,1)S(1)} %collective-permute-done.1.rest_1_), channel_id=1, source_target_pairs={{0,64},{64,128},{128,192},{192,0},{1,65},{65,129},{129,193},{193,1... | collective-permute-start | bytes 2457608 | tf_op jit(solution)/shard_map/ppermute | solution.py:284
  100.6 20.7 %collective-permute-start.5 = (bf16[640,640]{1,0:T(8,128)(2,1)S(1)}, bf16[640,640]{1,0:T(8,128)(2,1)}, u32[]{:S(2)}, u32[]{:S(2)}) collective-permute-start(bf16[640,640]{1,0:T(8,128)(2,1)S(1)} %collective-permute-done.1.rest_1_), channel_id=1, source_target_pairs={{0,192},{64,0},{128,64},{192,128},{1,193},{65,1},{129,65},{193,129... | collective-permute-start | bytes 2457608 | tf_op jit(solution)/shard_map/ppermute | solution.py:284
  102.3 20.6 %collective-permute-start.9 = (bf16[640,640]{1,0:T(8,128)(2,1)S(1)}, bf16[640,640]{1,0:T(8,128)(2,1)S(1)}, u32[]{:S(2)}, u32[]{:S(2)}) collective-permute-start(bf16[640,640]{1,0:T(8,128)(2,1)S(1)} %bitcast.18), channel_id=1, source_target_pairs={{0,1},{1,0},{2,3},{3,2},{4,5},{5,4},{6,7},{7,6},{8,9},{9,8},{10,11... | collective-permute-start | bytes 2457608 | tf_op jit(solution)/shard_map/ppermute | solution.py:288
  102.3 36.7 %collective-permute-start.6 = (bf16[640,640]{1,0:T(8,128)(2,1)S(1)}, bf16[640,640]{1,0:T(8,128)(2,1)}, u32[]{:S(2)}, u32[]{:S(2)}) collective-permute-start(bf16[640,640]{1,0:T(8,128)(2,1)S(1)} %collective-permute-done.2.rest_2_), channel_id=1, source_target_pairs={{0,64},{64,128},{128,192},{192,0},{1,65},{65,129},{129,193},{193,1... | collective-permute-start | bytes 2457608 | tf_op jit(solution)/shard_map/ppermute | solution.py:285
  102.7 36.3 %collective-permute-start.10 = (bf16[640,640]{1,0:T(8,128)(2,1)S(1)}, bf16[640,640]{1,0:T(8,128)(2,1)S(1)}, u32[]{:S(2)}, u32[]{:S(2)}) collective-permute-start(bf16[640,640]{1,0:T(8,128)(2,1)S(1)} %collective-permute-done.1.rest_1_), channel_id=1, source_target_pairs={{0,1},{1,0},{2,3},{3,2},{4,5},{5,4},{6,7},{7,6},{8,9},{9,8},{10,11... | collective-permute-start | bytes 2457608 | tf_op jit(solution)/shard_map/ppermute | solution.py:288
  121.3 18.2 %collective-permute-start.11 = (bf16[640,640]{1,0:T(8,128)(2,1)S(1)}, bf16[640,640]{1,0:T(8,128)(2,1)S(1)}, u32[]{:S(2)}, u32[]{:S(2)}) collective-permute-start(bf16[640,640]{1,0:T(8,128)(2,1)S(1)} %collective-permute-done.2.rest_2_), channel_id=1, source_target_pairs={{0,1},{1,0},{2,3},{3,2},{4,5},{5,4},{6,7},{7,6},{8,9},{9,8},{10,11... | collective-permute-start | bytes 2457608 | tf_op jit(solution)/shard_map/ppermute | solution.py:288
  121.3 18.4 %collective-permute-start.13 = (bf16[640,640]{1,0:T(8,128)(2,1)S(1)}, bf16[640,640]{1,0:T(8,128)(2,1)S(1)}, u32[]{:S(2)}, u32[]{:S(2)}) collective-permute-start(bf16[640,640]{1,0:T(8,128)(2,1)S(1)} %collective-permute-done.4.rest_4_), channel_id=1, source_target_pairs={{0,1},{1,0},{2,3},{3,2},{4,5},{5,4},{6,7},{7,6},{8,9},{9,8},{10,11... | collective-permute-start | bytes 2457608 | tf_op jit(solution)/shard_map/ppermute | solution.py:288
  122.9 24.4 %collective-permute-start.7 = (bf16[320,640]{1,0:T(8,128)(2,1)S(1)}, bf16[320,640]{1,0:T(8,128)(2,1)}, u32[]{:S(2)}, u32[]{:S(2)}) collective-permute-start(bf16[320,640]{1,0:T(8,128)(2,1)S(1)} %slice.8), channel_id=1, source_target_pairs={{0,64},{64,128},{128,192},{192,0},{1,65},{65,129},{129,193},{193,1... | collective-permute-start | bytes 1228808 | tf_op jit(solution)/shard_map/ppermute | solution.py:286
  138.9 13.0 %collective-permute-start.12 = (bf16[640,640]{1,0:T(8,128)(2,1)S(1)}, bf16[640,640]{1,0:T(8,128)(2,1)}, u32[]{:S(2)}, u32[]{:S(2)}) collective-permute-start(bf16[640,640]{1,0:T(8,128)(2,1)S(1)} %collective-permute-done.3.rest_3_), channel_id=1, source_target_pairs={{0,1},{1,0},{2,3},{3,2},{4,5},{5,4},{6,7},{7,6},{8,9},{9,8},{10,11... | collective-permute-start | bytes 2457608 | tf_op jit(solution)/shard_map/ppermute | solution.py:288
  139.0 13.0 %collective-permute-start.14 = (bf16[640,640]{1,0:T(8,128)(2,1)}, bf16[640,640]{1,0:T(8,128)(2,1)}, u32[]{:S(2)}, u32[]{:S(2)}) collective-permute-start(bf16[640,640]{1,0:T(8,128)(2,1)} %collective-permute-done.5.rest_5_), channel_id=1, source_target_pairs={{0,1},{1,0},{2,3},{3,2},{4,5},{5,4},{6,7},{7,6},{8,9},{9,8},{10,11... | collective-permute-start | bytes 2457608 | tf_op jit(solution)/shard_map/ppermute | solution.py:288
  139.5 12.5 %collective-permute-start.15 = (bf16[640,640]{1,0:T(8,128)(2,1)}, bf16[640,640]{1,0:T(8,128)(2,1)}, u32[]{:S(2)}, u32[]{:S(2)}) collective-permute-start(bf16[640,640]{1,0:T(8,128)(2,1)} %collective-permute-done.6.rest_6_), channel_id=1, source_target_pairs={{0,1},{1,0},{2,3},{3,2},{4,5},{5,4},{6,7},{7,6},{8,9},{9,8},{10,11... | collective-permute-start | bytes 2457608 | tf_op jit(solution)/shard_map/ppermute | solution.py:288
  139.7 12.0 %collective-permute-start.8 = (bf16[320,640]{1,0:T(8,128)(2,1)S(1)}, bf16[320,640]{1,0:T(8,128)(2,1)}, u32[]{:S(2)}, u32[]{:S(2)}) collective-permute-start(bf16[320,640]{1,0:T(8,128)(2,1)S(1)} %slice.9), channel_id=1, source_target_pairs={{0,192},{64,0},{128,64},{192,128},{1,193},{65,1},{129,65},{193,129... | collective-permute-start | bytes 1228808 | tf_op jit(solution)/shard_map/ppermute | solution.py:286
  147.3 4.7 %collective-permute-start.16 = (bf16[320,640]{1,0:T(8,128)(2,1)}, bf16[320,640]{1,0:T(8,128)(2,1)}, u32[]{:S(2)}, u32[]{:S(2)}) collective-permute-start(bf16[320,640]{1,0:T(8,128)(2,1)} %collective-permute-done.7.rest_7_), channel_id=1, source_target_pairs={{0,1},{1,0},{2,3},{3,2},{4,5},{5,4},{6,7},{7,6},{8,9},{9,8},{10,11... | collective-permute-start | bytes 1228808 | tf_op jit(solution)/shard_map/ppermute | solution.py:288
  151.6 2.1 collective-permute-start.17
  (8 other events, 319.4 us)

commit v6 on v5

--- a/solution.py
+++ b/solution.py
@@ -22,8 +22,6 @@
 COLS = 4 * D
 CHUNK = 640
 HALF = 640
-PART = 320
-PIECES = 9
 EXP2_SCALE = HD ** (-0.5) * math.log2(math.e)
 VMEM_LIMIT = 48 * 1024 * 1024
 
@@ -118,8 +116,8 @@
     arrived,
     *rest,
 ):
-    pieces = rest[: 2 * PIECES]
-    out, weights, windows, normed, triple, mixed, encoded, final, wsem, xsem = rest[2 * PIECES :]
+    pieces = rest[:16]
+    out, weights, windows, normed, triple, mixed, encoded, final, wsem, xsem = rest[16:]
     here, side = place[0], place[1]
 
     def window_copy(k):
@@ -127,26 +125,22 @@
             arrived.at[table[k]], windows.at[pl.ds(k * WIN, WIN)], xsem.at[k]
         )
 
-    def weight_copy(core, piece):
-        n, across = min(piece // 2, 3), min(piece % 2 + piece // 8, 1)
-        rows = PART if piece >= 7 else HALF
-        row = jnp.bitwise_xor(here, across) * HALF + (PART if piece == 8 else 0)
+    def weight_copy(n, core, across):
+        row = jnp.bitwise_xor(here, across) * HALF
         column = jnp.bitwise_xor(side, core) * CHUNK
         to = weights.at[
             place[2 + n],
-            pl.ds(pl.multiple_of(row, PART), rows),
+            pl.ds(pl.multiple_of(row, HALF), HALF),
             pl.ds(pl.multiple_of(column, CHUNK), CHUNK),
         ]
-        return pltpu.make_async_copy(pieces[PIECES * core + piece], to, wsem.at[core, piece])
-
-    def block_copies(n):
-        return [weight_copy(core, p) for core in range(2) for p in ((2 * n, 2 * n + 1) if n < 3 else (6, 7, 8))]
+        return pltpu.make_async_copy(pieces[8 * core + 2 * n + across], to, wsem.at[n, core, across])
 
     for k in range(DST_WIN):
         window_copy(k).start()
     for n in range(4):
-        for copy in block_copies(n):
-            copy.start()
+        for core in range(2):
+            for across in range(2):
+                weight_copy(n, core, across).start()
     for k in range(DST_WIN):
         window_copy(k).wait()
         rows = pl.ds(k * WIN, WIN)
@@ -156,8 +150,9 @@
 
     for n in range(4):
         block = place[2 + n]
-        for copy in block_copies(n):
-            copy.wait()
+        for core in range(2):
+            for across in range(2):
+                weight_copy(n, core, across).wait()
 
         @pl.when(block < 3)
         def _(block=block):
@@ -234,7 +229,7 @@
     return pl.pallas_call(
         encode_kernel,
         out_shape=jax.ShapeDtypeStruct((N_SEC * CAP, COLS), BF16),
-        in_specs=[smem] * 2 + [vmem] * 6 + [hbm] * (1 + 2 * PIECES),
+        in_specs=[smem] * 2 + [vmem] * 6 + [hbm] * 17,
         out_specs=vmem,
         scratch_shapes=[
             pltpu.VMEM((4, D, D), BF16),
@@ -244,7 +239,7 @@
             pltpu.VMEM((ROWS, D), BF16),
             pltpu.VMEM((ROWS, D), F32),
             pltpu.VMEM((D // 128, ROWS, 128), F32),
-            pltpu.SemaphoreType.DMA((2, PIECES)),
+            pltpu.SemaphoreType.DMA((4, 2, 2)),
             pltpu.SemaphoreType.DMA((DST_WIN,)),
         ],
         compiler_params=pltpu.CompilerParams(vmem_limit_bytes=VMEM_LIMIT),
@@ -277,14 +272,18 @@
     y, xh, c = lax.axis_index("y"), lax.axis_index("xh"), lax.axis_index("c")
     send = lax.ppermute
     partner = send(column, ("xl", "c"), CROSS)
-    low, high = jnp.where(c == 0, column, partner), jnp.where(c == 0, partner, column)
-    here = jnp.concatenate([low, high], axis=1).reshape(HALF, CHUNK)
-    across = send(here, ("xl", "xh", "c"), CROSS3)
+    across_column = send(column, ("xl", "xh", "c"), CROSS3)
+    across_partner = send(partner, ("xl", "xh", "c"), CROSS3)
+
+    def joined(even, odd):
+        low, high = jnp.where(c == 0, even, odd), jnp.where(c == 0, odd, even)
+        return jnp.concatenate([low, high], axis=1).reshape(HALF, CHUNK)
+
+    here, across = joined(column, partner), joined(across_partner, across_column)
     up_h, down_h = send(here, "y", shift(4, 1)), send(here, "y", shift(4, -1))
     up_a, down_a = send(across, "y", shift(4, 1)), send(across, "y", shift(4, -1))
-    far_h = send(up_h, "y", shift(4, 1))
-    far_low, far_high = send(up_a[:PART], "y", shift(4, 1)), send(down_a[PART:], "y", shift(4, -1))
-    pieces = [here, across, up_h, up_a, down_h, down_a, far_h, far_low, far_high]
+    far_h, far_a = send(up_h, "y", shift(4, 1)), send(down_a, "y", shift(4, -1))
+    pieces = [here, across, up_h, up_a, down_h, down_a, far_h, far_a]
     pieces = pieces + [send(p, "c", SWAP) for p in pieces]
     return pieces, [xh, side] + [jnp.mod(y - step, 4) for step in (0, 1, -1, 2)]
 

time: 211 us -> 205 us (0.972)
  the two profiles are of different devices: /device:TPU:128 before, /device:TPU:4 now
where the time goes in v6:
time: 205 us; the launch traced here: 203 us
  waiting for transfers between devices  109 us (53%)
  blocking collectives  38.6 us (19%)
  starting transfers between devices  27.9 us (14%)
  Pallas kernels  20 us (10%)
  local copies, waits for them, and re-layouts  4.01 us (2%)
  other arithmetic  3.24 us (2%)
    all_to_all x1, blocking collectives, body(): lax.all_to_all(packed, ('y', 'xl'), split_axis=0, concat_axis=0, tiled=True)  38.6 us
    ppermute x1, waiting for transfers between devices, spread_weights(): partner = send(column, ('xl', 'c'), CROSS)  28.3 us
    all_to_all x1, waiting for transfers between devices, body(): lax.all_to_all(going, ('xh', 'z', 'c'), split_axis=0, concat_axis=0, tile...  21.7 us
    pallas_call x1, Pallas kernels, encode(): pl.pallas_call(encode_kernel, out_shape=jax.ShapeDtypeStruct((N_SEC * CAP...  16.3 us
    ppermute x1, waiting for transfers between devices, spread_weights(): send(across, 'y', shift(4, -1))  15.6 us
    ppermute x1, waiting for transfers between devices, spread_weights(): send(up_h, 'y', shift(4, 1))  14 us
    all_to_all x1, waiting for transfers between devices, gather_weights(): lax.all_to_all(jnp.broadcast_to(own[None], (8, 40, CHUNK)), 'z', 0, 0, ti...  9.89 us
    ppermute x1, waiting for transfers between devices, spread_weights(): across_partner = send(partner, ('xl', 'xh', 'c'), CROSS3)  9.41 us
  transfers between devices with their start and end apart: 19, of which 11 were waited for; matrix products, arithmetic and copies ran while one was open for 2% of the time, Pallas kernels for 2%

profile of v6, /device:TPU:4, one launch (start us, length us, event | category | flops | bytes accessed | tf_op | source)
XLA Modules:
  0.0 203.3 jit_solution(14674833234075874889)
XLA Ops:
  0.0 0.8 dynamic-slice_select_fusion
  1.6 8.5 %all-to-all-start.1 = ((bf16[8,40,640]{2,1,0:T(8,128)(2,1)}), bf16[8,40,640]{2,1,0:T(8,128)(2,1)S(1)}, u32[]{:S(2)}, u32[]{:S(2)}) async-start(bf16[8,40,640]{2,1,0:T(8,128)(2,1)} %broadcast_in_dim.2), calls=%async_computation.1 | async-start | bytes 819200 | tf_op jit(solution)/shard_map/all_to_all | solution.py:267
  11.6 3.7 %outgoing.1 = (bf16[32,64,1280]{2,1,0:T(8,128)(2,1)}, s32[16]{0:T(128)}) custom-call(s32[1]{0:T(128)} %bitcast.6.place, s32[32]{0:T(128)} %bitcast.29, s32[32]{0:T(128)} %bitcast.30, s32[768]{0:T(1024)} %reshape.41.groups, bf16[24,64,1280]{2,1,0:T(8,128)(2,1)} %bitcast.28), custom_call_target="tpu_custom_call" | custom-call | tf_op jit(solution)/shard_map/outgoing/pallas_call | solution.py:89
  15.2 9.9 %all-to-all-done.1 = bf16[8,40,640]{2,1,0:T(8,128)(2,1)S(1)} async-done(((bf16[8,40,640]{2,1,0:T(8,128)(2,1)}), bf16[8,40,640]{2,1,0:T(8,128)(2,1)S(1)}, u32[]{:S(2)}, u32[]{:S(2)}) %all-to-all-start.1) | async-done | bytes 409632 | tf_op jit(solution)/shard_map/all_to_all | solution.py:267
  25.1 5.1 %all-to-all-start = ((bf16[32,64,1280]{2,1,0:T(8,128)(2,1)}), bf16[32,64,1280]{2,1,0:T(8,128)(2,1)}, u32[]{:S(2)}, u32[]{:S(2)}) async-start(bf16[32,64,1280]{2,1,0:T(8,128)(2,1)} %get-tuple-element.8), calls=%async_computation | async-start | bytes 10485760 | tf_op jit(solution)/shard_map/all_to_all | solution.py:316
  30.2 1.9 collective-permute-start
  32.2 28.3 %collective-permute-done = bf16[8,40,640]{2,1,0:T(8,128)(2,1)} collective-permute-done((bf16[8,40,640]{2,1,0:T(8,128)(2,1)S(1)}, bf16[8,40,640]{2,1,0:T(8,128)(2,1)}, u32[]{:S(2)}, u32[]{:S(2)}) %collective-permute-start) | collective-permute-done | bytes 409632 | tf_op jit(solution)/shard_map/ppermute | solution.py:274
  60.5 1.1 broadcast_select_fusion.3
  61.8 1.7 collective-permute-start.3
  63.4 1.7 collective-permute-start.5
  65.4 9.4 %collective-permute-done.1 = bf16[8,40,640]{2,1,0:T(8,128)(2,1)} collective-permute-done((bf16[8,40,640]{2,1,0:T(8,128)(2,1)}, bf16[8,40,640]{2,1,0:T(8,128)(2,1)}, u32[]{:S(2)}, u32[]{:S(2)}) %collective-permute-start.1) | collective-permute-done | bytes 409632 | tf_op jit(solution)/shard_map/ppermute | solution.py:276
  74.8 1.1 broadcast_select_fusion.1
  76.0 3.1 %collective-permute-start.6 = (bf16[640,640]{1,0:T(8,128)(2,1)S(1)}, bf16[640,640]{1,0:T(8,128)(2,1)}, u32[]{:S(2)}, u32[]{:S(2)}) collective-permute-start(bf16[640,640]{1,0:T(8,128)(2,1)S(1)} %bitcast.20), channel_id=1, source_target_pairs={{0,192},{64,0},{128,64},{192,128},{1,193},{65,1},{129,65},{193,129... | collective-permute-start | bytes 2457608 | tf_op jit(solution)/shard_map/ppermute | solution.py:284
  79.1 5.1 %collective-permute-done.3.rest_2_ = bf16[640,640]{1,0:T(8,128)(2,1)S(1)} collective-permute-done((bf16[640,640]{1,0:T(8,128)(2,1)S(1)}, bf16[640,640]{1,0:T(8,128)(2,1)S(1)}, u32[]{:S(2)}, u32[]{:S(2)}) %collective-permute-start.3) | collective-permute-done | bytes 819232 | tf_op jit(solution)/shard_map/ppermute | solution.py:283
  84.5 1.6 collective-permute-start.7
  86.1 15.6 %collective-permute-done.6.rest_5_ = bf16[640,640]{1,0:T(8,128)(2,1)} collective-permute-done((bf16[640,640]{1,0:T(8,128)(2,1)S(1)}, bf16[640,640]{1,0:T(8,128)(2,1)}, u32[]{:S(2)}, u32[]{:S(2)}) %collective-permute-start.6) | collective-permute-done | bytes 819232 | tf_op jit(solution)/shard_map/ppermute | solution.py:284
  101.7 3.0 %collective-permute-start.8 = (bf16[640,640]{1,0:T(8,128)(2,1)}, bf16[640,640]{1,0:T(8,128)(2,1)}, u32[]{:S(2)}, u32[]{:S(2)}) collective-permute-start(bf16[640,640]{1,0:T(8,128)(2,1)} %collective-permute-done.6.rest_5_), channel_id=1, source_target_pairs={{0,192},{64,0},{128,64},{192,128},{1,193},{65,1},{129,65},{193,129... | collective-permute-start | bytes 2457608 | tf_op jit(solution)/shard_map/ppermute | solution.py:285
  105.2 14.0 %collective-permute-done.7.rest_6_ = bf16[640,640]{1,0:T(8,128)(2,1)} collective-permute-done((bf16[640,640]{1,0:T(8,128)(2,1)S(1)}, bf16[640,640]{1,0:T(8,128)(2,1)}, u32[]{:S(2)}, u32[]{:S(2)}) %collective-permute-start.7) | collective-permute-done | bytes 819232 | tf_op jit(solution)/shard_map/ppermute | solution.py:285
  119.8 2.7 %collective-permute-done.8.rest_7_ = bf16[640,640]{1,0:T(8,128)(2,1)} collective-permute-done((bf16[640,640]{1,0:T(8,128)(2,1)}, bf16[640,640]{1,0:T(8,128)(2,1)}, u32[]{:S(2)}, u32[]{:S(2)}) %collective-permute-start.8) | collective-permute-done | bytes 819232 | tf_op jit(solution)/shard_map/ppermute | solution.py:285
  123.1 2.1 %collective-permute-done.16.rest_15_ = bf16[640,640]{1,0:T(8,128)(2,1)} collective-permute-done((bf16[640,640]{1,0:T(8,128)(2,1)}, bf16[640,640]{1,0:T(8,128)(2,1)}, u32[]{:S(2)}, u32[]{:S(2)}) %collective-permute-start.16) | collective-permute-done | bytes 819232 | tf_op jit(solution)/shard_map/ppermute | solution.py:287
  125.2 21.7 %all-to-all-done.arrived = bf16[32,64,1280]{2,1,0:T(8,128)(2,1)} async-done(((bf16[32,64,1280]{2,1,0:T(8,128)(2,1)}), bf16[32,64,1280]{2,1,0:T(8,128)(2,1)}, u32[]{:S(2)}, u32[]{:S(2)}) %all-to-all-start) | async-done | bytes 5242912 | tf_op jit(solution)/shard_map/all_to_all | solution.py:316
  146.9 16.3 %encode.1 = bf16[256,5120]{1,0:T(8,128)(2,1)} custom-call(s32[6]{0:T(128)S(1)} %stack.27.place, s32[16]{0:T(128)S(1)} %copy-done.1, s32[1,128]{1,0:T(1,128)S(1)} %bitcast.25, s32[128,1]{1,0:T(8,128)S(1)} %copy.14.owner_column, f32[1,1280]{1,0:T(1,128)S(1)} %reshape.45.norm_gain, f32[3,1,1280]{2,1,0:T(1,128)S(1)} %reshape.46.qkv_bias, ...), custom_call_target="tpu_custom_call" | custom-call | tf_op jit(solution)/shard_map/encode/pallas_call | solution.py:229
  163.2 38.6 %all_to_all.19 = bf16[8,32,5120]{2,1,0:T(8,128)(2,1)S(1)} all-to-all(bf16[8,32,5120]{2,1,0:T(8,128)(2,1)} %bitcast.26), channel_id=1, replica_groups=mesh['y'=4,'xl'=2,'xh'=2,'z'=8,'c'=2] {'y','xl'}, dimensions={0} | all-to-all | bytes 5242880 | tf_op jit(solution)/shard_map/all_to_all | solution.py:329
  201.8 1.5 copy.16
  (50 shorter events, 4.6 us)
Async XLA Ops:
  1.6 23.5 %all-to-all-start.1 = ((bf16[8,40,640]{2,1,0:T(8,128)(2,1)}), bf16[8,40,640]{2,1,0:T(8,128)(2,1)S(1)}, u32[]{:S(2)}, u32[]{:S(2)}) async-start(bf16[8,40,640]{2,1,0:T(8,128)(2,1)} %broadcast_in_dim.2), calls=%async_computation.1 | async-start | bytes 819200 | tf_op jit(solution)/shard_map/all_to_all | solution.py:267
  25.1 121.8 %all-to-all-start = ((bf16[32,64,1280]{2,1,0:T(8,128)(2,1)}), bf16[32,64,1280]{2,1,0:T(8,128)(2,1)}, u32[]{:S(2)}, u32[]{:S(2)}) async-start(bf16[32,64,1280]{2,1,0:T(8,128)(2,1)} %get-tuple-element.8), calls=%async_computation | async-start | bytes 10485760 | tf_op jit(solution)/shard_map/all_to_all | solution.py:316
  30.2 30.3 %collective-permute-start = (bf16[8,40,640]{2,1,0:T(8,128)(2,1)S(1)}, bf16[8,40,640]{2,1,0:T(8,128)(2,1)}, u32[]{:S(2)}, u32[]{:S(2)}) collective-permute-start(bf16[8,40,640]{2,1,0:T(8,128)(2,1)S(1)} %all-to-all-done.1), channel_id=1, source_target_pairs={{0,33},{1,32},{32,1},{33,0},{2,35},{3,34},{34,3},{35,2},{4,37},{5,... | collective-permute-start | bytes 1228808 | tf_op jit(solution)/shard_map/ppermute | solution.py:274
  32.2 33.2 %collective-permute-start.2 = (bf16[8,40,640]{2,1,0:T(8,128)(2,1)S(1)}, bf16[8,40,640]{2,1,0:T(8,128)(2,1)S(1)}, u32[]{:S(2)}, u32[]{:S(2)}) collective-permute-start(bf16[8,40,640]{2,1,0:T(8,128)(2,1)S(1)} %all-to-all-done.1), channel_id=1, source_target_pairs={{0,49},{1,48},{16,33},{17,32},{32,17},{33,16},{48,1},{49,0},{2,51}... | collective-permute-start | bytes 1228808 | tf_op jit(solution)/shard_map/ppermute | solution.py:275
  60.5 14.3 %collective-permute-start.1 = (bf16[8,40,640]{2,1,0:T(8,128)(2,1)}, bf16[8,40,640]{2,1,0:T(8,128)(2,1)}, u32[]{:S(2)}, u32[]{:S(2)}) collective-permute-start(bf16[8,40,640]{2,1,0:T(8,128)(2,1)} %collective-permute-done), channel_id=1, source_target_pairs={{0,49},{1,48},{16,33},{17,32},{32,17},{33,16},{48,1},{49,0},{2,51}... | collective-permute-start | bytes 1228808 | tf_op jit(solution)/shard_map/ppermute | solution.py:276
  61.6 61.0 %copy-start.6 = (f32[1280]{0:T(1024)S(1)}, f32[1280]{0:T(1024)}, u32[]{:S(2)}) copy-start(f32[1280]{0:T(1024)} %param.15) | copy-start | bytes 15364
  61.7 61.0 %copy-start.5 = (f32[3840]{0:T(1024)S(1)}, f32[3840]{0:T(1024)}, u32[]{:S(2)}) copy-start(f32[3840]{0:T(1024)} %param.17) | copy-start | bytes 46084
  61.7 61.0 %copy-start.7 = (f32[1280]{0:T(1024)S(1)}, f32[1280]{0:T(1024)}, u32[]{:S(2)}) copy-start(f32[1280]{0:T(1024)} %param.19) | copy-start | bytes 15364
  61.7 61.0 %copy-start.8 = (f32[1280]{0:T(1024)S(1)}, f32[1280]{0:T(1024)}, u32[]{:S(2)}) copy-start(f32[1280]{0:T(1024)} %param.20) | copy-start | bytes 15364
  61.7 85.2 %copy-start.1 = (s32[16]{0:T(128)S(1)}, s32[16]{0:T(128)}, u32[]{:S(2)}) copy-start(s32[16]{0:T(128)} %get-tuple-element.7.table) | copy-start | bytes 196
  61.8 22.4 %collective-permute-start.3 = (bf16[640,640]{1,0:T(8,128)(2,1)S(1)}, bf16[640,640]{1,0:T(8,128)(2,1)S(1)}, u32[]{:S(2)}, u32[]{:S(2)}) collective-permute-start(bf16[640,640]{1,0:T(8,128)(2,1)S(1)} %bitcast.16), channel_id=1, source_target_pairs={{0,64},{64,128},{128,192},{192,0},{1,65},{65,129},{129,193},{193,1... | collective-permute-start | bytes 2457608 | tf_op jit(solution)/shard_map/ppermute | solution.py:283
  63.4 21.0 %collective-permute-start.5 = (bf16[640,640]{1,0:T(8,128)(2,1)S(1)}, bf16[640,640]{1,0:T(8,128)(2,1)S(1)}, u32[]{:S(2)}, u32[]{:S(2)}) collective-permute-start(bf16[640,640]{1,0:T(8,128)(2,1)S(1)} %bitcast.17), channel_id=1, source_target_pairs={{0,192},{64,0},{128,64},{192,128},{1,193},{65,1},{129,65},{193,129... | collective-permute-start | bytes 2457608 | tf_op jit(solution)/shard_map/ppermute | solution.py:283
  65.1 21.0 %collective-permute-start.9 = (bf16[640,640]{1,0:T(8,128)(2,1)S(1)}, bf16[640,640]{1,0:T(8,128)(2,1)S(1)}, u32[]{:S(2)}, u32[]{:S(2)}) collective-permute-start(bf16[640,640]{1,0:T(8,128)(2,1)S(1)} %bitcast.18), channel_id=1, source_target_pairs={{0,1},{1,0},{2,3},{3,2},{4,5},{5,4},{6,7},{7,6},{8,9},{9,8},{10,11... | collective-permute-start | bytes 2457608 | tf_op jit(solution)/shard_map/ppermute | solution.py:287
  76.0 25.7 %collective-permute-start.6 = (bf16[640,640]{1,0:T(8,128)(2,1)S(1)}, bf16[640,640]{1,0:T(8,128)(2,1)}, u32[]{:S(2)}, u32[]{:S(2)}) collective-permute-start(bf16[640,640]{1,0:T(8,128)(2,1)S(1)} %bitcast.20), channel_id=1, source_target_pairs={{0,192},{64,0},{128,64},{192,128},{1,193},{65,1},{129,65},{193,129... | collective-permute-start | bytes 2457608 | tf_op jit(solution)/shard_map/ppermute | solution.py:284
  79.1 25.6 %collective-permute-start.4 = (bf16[640,640]{1,0:T(8,128)(2,1)S(1)}, bf16[640,640]{1,0:T(8,128)(2,1)}, u32[]{:S(2)}, u32[]{:S(2)}) collective-permute-start(bf16[640,640]{1,0:T(8,128)(2,1)S(1)} %bitcast.21), channel_id=1, source_target_pairs={{0,64},{64,128},{128,192},{192,0},{1,65},{65,129},{129,193},{193,1... | collective-permute-start | bytes 2457608 | tf_op jit(solution)/shard_map/ppermute | solution.py:284
  84.2 20.5 %collective-permute-start.10 = (bf16[640,640]{1,0:T(8,128)(2,1)S(1)}, bf16[640,640]{1,0:T(8,128)(2,1)S(1)}, u32[]{:S(2)}, u32[]{:S(2)}) collective-permute-start(bf16[640,640]{1,0:T(8,128)(2,1)S(1)} %bitcast.22), channel_id=1, source_target_pairs={{0,1},{1,0},{2,3},{3,2},{4,5},{5,4},{6,7},{7,6},{8,9},{9,8},{10,11... | collective-permute-start | bytes 2457608 | tf_op jit(solution)/shard_map/ppermute | solution.py:287
  84.5 34.7 %collective-permute-start.7 = (bf16[640,640]{1,0:T(8,128)(2,1)S(1)}, bf16[640,640]{1,0:T(8,128)(2,1)}, u32[]{:S(2)}, u32[]{:S(2)}) collective-permute-start(bf16[640,640]{1,0:T(8,128)(2,1)S(1)} %collective-permute-done.3.rest_2_), channel_id=1, source_target_pairs={{0,64},{64,128},{128,192},{192,0},{1,65},{65,129},{129,193},{193,1... | collective-permute-start | bytes 2457608 | tf_op jit(solution)/shard_map/ppermute | solution.py:285
  86.1 33.2 %collective-permute-start.11 = (bf16[640,640]{1,0:T(8,128)(2,1)S(1)}, bf16[640,640]{1,0:T(8,128)(2,1)S(1)}, u32[]{:S(2)}, u32[]{:S(2)}) collective-permute-start(bf16[640,640]{1,0:T(8,128)(2,1)S(1)} %collective-permute-done.3.rest_2_), channel_id=1, source_target_pairs={{0,1},{1,0},{2,3},{3,2},{4,5},{5,4},{6,7},{7,6},{8,9},{9,8},{10,11... | collective-permute-start | bytes 2457608 | tf_op jit(solution)/shard_map/ppermute | solution.py:287
  101.7 20.8 %collective-permute-start.8 = (bf16[640,640]{1,0:T(8,128)(2,1)}, bf16[640,640]{1,0:T(8,128)(2,1)}, u32[]{:S(2)}, u32[]{:S(2)}) collective-permute-start(bf16[640,640]{1,0:T(8,128)(2,1)} %collective-permute-done.6.rest_5_), channel_id=1, source_target_pairs={{0,192},{64,0},{128,64},{192,128},{1,193},{65,1},{129,65},{193,129... | collective-permute-start | bytes 2457608 | tf_op jit(solution)/shard_map/ppermute | solution.py:285
  104.7 18.1 %collective-permute-start.13 = (bf16[640,640]{1,0:T(8,128)(2,1)S(1)}, bf16[640,640]{1,0:T(8,128)(2,1)}, u32[]{:S(2)}, u32[]{:S(2)}) collective-permute-start(bf16[640,640]{1,0:T(8,128)(2,1)S(1)} %collective-permute-done.5.rest_4_), channel_id=1, source_target_pairs={{0,1},{1,0},{2,3},{3,2},{4,5},{5,4},{6,7},{7,6},{8,9},{9,8},{10,11... | collective-permute-start | bytes 2457608 | tf_op jit(solution)/shard_map/ppermute | solution.py:287
  104.7 18.1 %collective-permute-start.14 = (bf16[640,640]{1,0:T(8,128)(2,1)}, bf16[640,640]{1,0:T(8,128)(2,1)}, u32[]{:S(2)}, u32[]{:S(2)}) collective-permute-start(bf16[640,640]{1,0:T(8,128)(2,1)} %collective-permute-done.6.rest_5_), channel_id=1, source_target_pairs={{0,1},{1,0},{2,3},{3,2},{4,5},{5,4},{6,7},{7,6},{8,9},{9,8},{10,11... | collective-permute-start | bytes 2457608 | tf_op jit(solution)/shard_map/ppermute | solution.py:287
  119.2 3.6 %collective-permute-start.12 = (bf16[640,640]{1,0:T(8,128)(2,1)}, bf16[640,640]{1,0:T(8,128)(2,1)}, u32[]{:S(2)}, u32[]{:S(2)}) collective-permute-start(bf16[640,640]{1,0:T(8,128)(2,1)} %collective-permute-done.4.rest_3_), channel_id=1, source_target_pairs={{0,1},{1,0},{2,3},{3,2},{4,5},{5,4},{6,7},{7,6},{8,9},{9,8},{10,11... | collective-permute-start | bytes 2457608 | tf_op jit(solution)/shard_map/ppermute | solution.py:287
  119.2 3.8 %collective-permute-start.15 = (bf16[640,640]{1,0:T(8,128)(2,1)}, bf16[640,640]{1,0:T(8,128)(2,1)}, u32[]{:S(2)}, u32[]{:S(2)}) collective-permute-start(bf16[640,640]{1,0:T(8,128)(2,1)} %collective-permute-done.7.rest_6_), channel_id=1, source_target_pairs={{0,1},{1,0},{2,3},{3,2},{4,5},{5,4},{6,7},{7,6},{8,9},{9,8},{10,11... | collective-permute-start | bytes 2457608 | tf_op jit(solution)/shard_map/ppermute | solution.py:287
  122.5 2.7 %collective-permute-start.16 = (bf16[640,640]{1,0:T(8,128)(2,1)}, bf16[640,640]{1,0:T(8,128)(2,1)}, u32[]{:S(2)}, u32[]{:S(2)}) collective-permute-start(bf16[640,640]{1,0:T(8,128)(2,1)} %collective-permute-done.8.rest_7_), channel_id=1, source_target_pairs={{0,1},{1,0},{2,3},{3,2},{4,5},{5,4},{6,7},{7,6},{8,9},{9,8},{10,11... | collective-permute-start | bytes 2457608 | tf_op jit(solution)/shard_map/ppermute | solution.py:287
  (4 other events, 112.4 us)

commit v7 on v6

--- a/solution.py
+++ b/solution.py
@@ -117,7 +117,7 @@
     *rest,
 ):
     pieces = rest[:16]
-    out, weights, windows, normed, triple, mixed, encoded, final, wsem, xsem = rest[16:]
+    packed_rows, out, psem, weights, windows, normed, triple, mixed, encoded, final, wsem, xsem = rest[16:]
     here, side = place[0], place[1]
 
     def window_copy(k):
@@ -197,16 +197,18 @@
 
     lax.fori_loop(0, DST_WIN, attend, 0, unroll=True)
 
-    encoded[...] = jnp.dot(mixed[...], weights[3], preferred_element_type=F32)
-    for k in range(DST_WIN):
-        rows = pl.ds(k * WIN, WIN)
-        values = windows[rows, :].astype(F32) + encoded[rows, :] + proj_bias[...]
-        mean = jnp.mean(values * values, axis=-1, keepdims=True)
-        alive = lax.broadcasted_iota(jnp.int32, (WIN, 1), 0) < table[DST_WIN + k]
-        scale = jnp.where(alive, lax.rsqrt(mean + 1e-6), 0.0)
-        values = values * scale * merge_gain[...]
-        for t in range(D // 128):
-            final[t, rows, :] = values[:, t * 128 : t * 128 + 128]
+    for half in range(2):
+        part = pl.ds(half * (ROWS // 2), ROWS // 2)
+        encoded[part, :] = jnp.dot(mixed[part, :], weights[3], preferred_element_type=F32)
+        for k in range(half * (DST_WIN // 2), (half + 1) * (DST_WIN // 2)):
+            rows = pl.ds(k * WIN, WIN)
+            values = windows[rows, :].astype(F32) + encoded[rows, :] + proj_bias[...]
+            mean = jnp.mean(values * values, axis=-1, keepdims=True)
+            alive = lax.broadcasted_iota(jnp.int32, (WIN, 1), 0) < table[DST_WIN + k]
+            scale = jnp.where(alive, lax.rsqrt(mean + 1e-6), 0.0)
+            values = values * scale * merge_gain[...]
+            for t in range(D // 128):
+                final[t, rows, :] = values[:, t * 128 : t * 128 + 128]
 
     at = lax.broadcasted_iota(jnp.int32, (MERGED, MERGED), 1)
     earlier = lax.broadcasted_iota(jnp.int32, (MERGED, MERGED), 0) < at
@@ -215,11 +217,19 @@
     places = owner_row[...] * CAP + rank
     chosen = lax.broadcasted_iota(jnp.int32, (N_SEC * CAP, MERGED), 0) == places
     chosen = jnp.where(chosen, 1.0, 0.0).astype(BF16)
+
+    def leave(p):
+        cols = pl.ds(p * D, D)
+        return pltpu.make_async_copy(out.at[:, cols], packed_rows.at[:, cols], psem.at[p])
+
     for p in range(4):
         merged = [final[t, pl.ds(p, MERGED, stride=4), :] for t in range(D // 128)]
         merged = jnp.concatenate(merged, axis=1).astype(BF16)
         packed = jnp.dot(chosen, merged, preferred_element_type=F32)
         out[:, p * D : (p + 1) * D] = packed.astype(BF16)
+        leave(p).start()
+    for p in range(4):
+        leave(p).wait()
 
 
 def encode(place, table, owner_row, owner_column, gain, qb, pb, mg, arrived, pieces):
@@ -230,8 +240,10 @@
         encode_kernel,
         out_shape=jax.ShapeDtypeStruct((N_SEC * CAP, COLS), BF16),
         in_specs=[smem] * 2 + [vmem] * 6 + [hbm] * 17,
-        out_specs=vmem,
+        out_specs=pl.BlockSpec(memory_space=pltpu.HBM),
         scratch_shapes=[
+            pltpu.VMEM((N_SEC * CAP, COLS), BF16),
+            pltpu.SemaphoreType.DMA((4,)),
             pltpu.VMEM((4, D, D), BF16),
             pltpu.VMEM((ROWS, D), BF16),
             pltpu.VMEM((ROWS, D), BF16),

time: 205 us -> 204 us (level)
  no operation moved by 1% of the time
where the time goes in v7:
time: 204 us; the launch traced here: 202 us
  waiting for transfers between devices  109 us (53%)
  blocking collectives  38.6 us (19%)
  starting transfers between devices  27.9 us (14%)
  Pallas kernels  19.2 us (9%)
  local copies, waits for them, and re-layouts  4.01 us (2%)
  other arithmetic  3.24 us (2%)
    all_to_all x1, blocking collectives, body(): lax.all_to_all(packed, ('y', 'xl'), split_axis=0, concat_axis=0, tiled=True)  38.6 us
    ppermute x1, waiting for transfers between devices, spread_weights(): partner = send(column, ('xl', 'c'), CROSS)  28.3 us
    all_to_all x1, waiting for transfers between devices, body(): lax.all_to_all(going, ('xh', 'z', 'c'), split_axis=0, concat_axis=0, tile...  21.7 us
    ppermute x1, waiting for transfers between devices, spread_weights(): send(across, 'y', shift(4, -1))  15.6 us
    pallas_call x1, Pallas kernels, encode(): pl.pallas_call(encode_kernel, out_shape=jax.ShapeDtypeStruct((N_SEC * CAP...  15.3 us
    ppermute x1, waiting for transfers between devices, spread_weights(): send(up_h, 'y', shift(4, 1))  14 us
    all_to_all x1, waiting for transfers between devices, gather_weights(): lax.all_to_all(jnp.broadcast_to(own[None], (8, 40, CHUNK)), 'z', 0, 0, ti...  9.72 us
    ppermute x1, waiting for transfers between devices, spread_weights(): across_partner = send(partner, ('xl', 'xh', 'c'), CROSS3)  9.41 us
  transfers between devices with their start and end apart: 19, of which 11 were waited for; matrix products, arithmetic and copies ran while one was open for 2% of the time, Pallas kernels for 2%

profile of v7, /device:TPU:4, one launch (start us, length us, event | category | flops | bytes accessed | tf_op | source)
XLA Modules:
  0.0 202.4 jit_solution(16840089281304048287)
XLA Ops:
  0.0 0.8 dynamic-slice_select_fusion
  1.6 8.5 %all-to-all-start.1 = ((bf16[8,40,640]{2,1,0:T(8,128)(2,1)}), bf16[8,40,640]{2,1,0:T(8,128)(2,1)S(1)}, u32[]{:S(2)}, u32[]{:S(2)}) async-start(bf16[8,40,640]{2,1,0:T(8,128)(2,1)} %broadcast_in_dim.2), calls=%async_computation.1 | async-start | bytes 819200 | tf_op jit(solution)/shard_map/all_to_all | solution.py:279
  11.6 3.9 %outgoing.1 = (bf16[32,64,1280]{2,1,0:T(8,128)(2,1)}, s32[16]{0:T(128)}) custom-call(s32[1]{0:T(128)} %bitcast.6.place, s32[32]{0:T(128)} %bitcast.29, s32[32]{0:T(128)} %bitcast.30, s32[768]{0:T(1024)} %reshape.41.groups, bf16[24,64,1280]{2,1,0:T(8,128)(2,1)} %bitcast.28), custom_call_target="tpu_custom_call" | custom-call | tf_op jit(solution)/shard_map/outgoing/pallas_call | solution.py:89
  15.4 9.7 %all-to-all-done.1 = bf16[8,40,640]{2,1,0:T(8,128)(2,1)S(1)} async-done(((bf16[8,40,640]{2,1,0:T(8,128)(2,1)}), bf16[8,40,640]{2,1,0:T(8,128)(2,1)S(1)}, u32[]{:S(2)}, u32[]{:S(2)}) %all-to-all-start.1) | async-done | bytes 409632 | tf_op jit(solution)/shard_map/all_to_all | solution.py:279
  25.1 5.1 %all-to-all-start = ((bf16[32,64,1280]{2,1,0:T(8,128)(2,1)}), bf16[32,64,1280]{2,1,0:T(8,128)(2,1)}, u32[]{:S(2)}, u32[]{:S(2)}) async-start(bf16[32,64,1280]{2,1,0:T(8,128)(2,1)} %get-tuple-element.8), calls=%async_computation | async-start | bytes 10485760 | tf_op jit(solution)/shard_map/all_to_all | solution.py:328
  30.2 1.9 collective-permute-start
  32.2 28.3 %collective-permute-done = bf16[8,40,640]{2,1,0:T(8,128)(2,1)} collective-permute-done((bf16[8,40,640]{2,1,0:T(8,128)(2,1)S(1)}, bf16[8,40,640]{2,1,0:T(8,128)(2,1)}, u32[]{:S(2)}, u32[]{:S(2)}) %collective-permute-start) | collective-permute-done | bytes 409632 | tf_op jit(solution)/shard_map/ppermute | solution.py:286
  60.5 1.1 broadcast_select_fusion.3
  61.8 1.7 collective-permute-start.3
  63.4 1.7 collective-permute-start.5
  65.4 9.4 %collective-permute-done.1 = bf16[8,40,640]{2,1,0:T(8,128)(2,1)} collective-permute-done((bf16[8,40,640]{2,1,0:T(8,128)(2,1)}, bf16[8,40,640]{2,1,0:T(8,128)(2,1)}, u32[]{:S(2)}, u32[]{:S(2)}) %collective-permute-start.1) | collective-permute-done | bytes 409632 | tf_op jit(solution)/shard_map/ppermute | solution.py:288
  74.8 1.1 broadcast_select_fusion.1
  76.0 3.1 %collective-permute-start.6 = (bf16[640,640]{1,0:T(8,128)(2,1)S(1)}, bf16[640,640]{1,0:T(8,128)(2,1)}, u32[]{:S(2)}, u32[]{:S(2)}) collective-permute-start(bf16[640,640]{1,0:T(8,128)(2,1)S(1)} %bitcast.20), channel_id=1, source_target_pairs={{0,192},{64,0},{128,64},{192,128},{1,193},{65,1},{129,65},{193,129... | collective-permute-start | bytes 2457608 | tf_op jit(solution)/shard_map/ppermute | solution.py:296
  79.1 5.1 %collective-permute-done.3.rest_2_ = bf16[640,640]{1,0:T(8,128)(2,1)S(1)} collective-permute-done((bf16[640,640]{1,0:T(8,128)(2,1)S(1)}, bf16[640,640]{1,0:T(8,128)(2,1)S(1)}, u32[]{:S(2)}, u32[]{:S(2)}) %collective-permute-start.3) | collective-permute-done | bytes 819232 | tf_op jit(solution)/shard_map/ppermute | solution.py:295
  84.5 1.6 collective-permute-start.7
  86.1 15.6 %collective-permute-done.6.rest_5_ = bf16[640,640]{1,0:T(8,128)(2,1)} collective-permute-done((bf16[640,640]{1,0:T(8,128)(2,1)S(1)}, bf16[640,640]{1,0:T(8,128)(2,1)}, u32[]{:S(2)}, u32[]{:S(2)}) %collective-permute-start.6) | collective-permute-done | bytes 819232 | tf_op jit(solution)/shard_map/ppermute | solution.py:296
  101.7 3.0 %collective-permute-start.8 = (bf16[640,640]{1,0:T(8,128)(2,1)}, bf16[640,640]{1,0:T(8,128)(2,1)}, u32[]{:S(2)}, u32[]{:S(2)}) collective-permute-start(bf16[640,640]{1,0:T(8,128)(2,1)} %collective-permute-done.6.rest_5_), channel_id=1, source_target_pairs={{0,192},{64,0},{128,64},{192,128},{1,193},{65,1},{129,65},{193,129... | collective-permute-start | bytes 2457608 | tf_op jit(solution)/shard_map/ppermute | solution.py:297
  105.2 14.0 %collective-permute-done.7.rest_6_ = bf16[640,640]{1,0:T(8,128)(2,1)} collective-permute-done((bf16[640,640]{1,0:T(8,128)(2,1)S(1)}, bf16[640,640]{1,0:T(8,128)(2,1)}, u32[]{:S(2)}, u32[]{:S(2)}) %collective-permute-start.7) | collective-permute-done | bytes 819232 | tf_op jit(solution)/shard_map/ppermute | solution.py:297
  119.8 2.7 %collective-permute-done.8.rest_7_ = bf16[640,640]{1,0:T(8,128)(2,1)} collective-permute-done((bf16[640,640]{1,0:T(8,128)(2,1)}, bf16[640,640]{1,0:T(8,128)(2,1)}, u32[]{:S(2)}, u32[]{:S(2)}) %collective-permute-start.8) | collective-permute-done | bytes 819232 | tf_op jit(solution)/shard_map/ppermute | solution.py:297
  123.1 2.1 %collective-permute-done.16.rest_15_ = bf16[640,640]{1,0:T(8,128)(2,1)} collective-permute-done((bf16[640,640]{1,0:T(8,128)(2,1)}, bf16[640,640]{1,0:T(8,128)(2,1)}, u32[]{:S(2)}, u32[]{:S(2)}) %collective-permute-start.16) | collective-permute-done | bytes 819232 | tf_op jit(solution)/shard_map/ppermute | solution.py:299
  125.2 21.7 %all-to-all-done.arrived = bf16[32,64,1280]{2,1,0:T(8,128)(2,1)} async-done(((bf16[32,64,1280]{2,1,0:T(8,128)(2,1)}), bf16[32,64,1280]{2,1,0:T(8,128)(2,1)}, u32[]{:S(2)}, u32[]{:S(2)}) %all-to-all-start) | async-done | bytes 5242912 | tf_op jit(solution)/shard_map/all_to_all | solution.py:328
  146.9 15.3 %encode.1 = bf16[256,5120]{1,0:T(8,128)(2,1)} custom-call(s32[6]{0:T(128)S(1)} %stack.27.place, s32[16]{0:T(128)S(1)} %copy-done.1, s32[1,128]{1,0:T(1,128)S(1)} %bitcast.25, s32[128,1]{1,0:T(8,128)S(1)} %copy.14.owner_column, f32[1,1280]{1,0:T(1,128)S(1)} %reshape.45.norm_gain, f32[3,1,1280]{2,1,0:T(1,128)S(1)} %reshape.46.qkv_bias, ...), custom_call_target="tpu_custom_call" | custom-call | tf_op jit(solution)/shard_map/encode/pallas_call | solution.py:239
  162.3 38.6 %all_to_all.19 = bf16[8,32,5120]{2,1,0:T(8,128)(2,1)S(1)} all-to-all(bf16[8,32,5120]{2,1,0:T(8,128)(2,1)} %bitcast.26), channel_id=1, replica_groups=mesh['y'=4,'xl'=2,'xh'=2,'z'=8,'c'=2] {'y','xl'}, dimensions={0} | all-to-all | bytes 5242880 | tf_op jit(solution)/shard_map/all_to_all | solution.py:341
  200.9 1.5 copy.16
  (50 shorter events, 4.6 us)
Async XLA Ops:
  1.6 23.5 %all-to-all-start.1 = ((bf16[8,40,640]{2,1,0:T(8,128)(2,1)}), bf16[8,40,640]{2,1,0:T(8,128)(2,1)S(1)}, u32[]{:S(2)}, u32[]{:S(2)}) async-start(bf16[8,40,640]{2,1,0:T(8,128)(2,1)} %broadcast_in_dim.2), calls=%async_computation.1 | async-start | bytes 819200 | tf_op jit(solution)/shard_map/all_to_all | solution.py:279
  25.1 121.8 %all-to-all-start = ((bf16[32,64,1280]{2,1,0:T(8,128)(2,1)}), bf16[32,64,1280]{2,1,0:T(8,128)(2,1)}, u32[]{:S(2)}, u32[]{:S(2)}) async-start(bf16[32,64,1280]{2,1,0:T(8,128)(2,1)} %get-tuple-element.8), calls=%async_computation | async-start | bytes 10485760 | tf_op jit(solution)/shard_map/all_to_all | solution.py:328
  30.2 30.3 %collective-permute-start = (bf16[8,40,640]{2,1,0:T(8,128)(2,1)S(1)}, bf16[8,40,640]{2,1,0:T(8,128)(2,1)}, u32[]{:S(2)}, u32[]{:S(2)}) collective-permute-start(bf16[8,40,640]{2,1,0:T(8,128)(2,1)S(1)} %all-to-all-done.1), channel_id=1, source_target_pairs={{0,33},{1,32},{32,1},{33,0},{2,35},{3,34},{34,3},{35,2},{4,37},{5,... | collective-permute-start | bytes 1228808 | tf_op jit(solution)/shard_map/ppermute | solution.py:286
  32.2 33.2 %collective-permute-start.2 = (bf16[8,40,640]{2,1,0:T(8,128)(2,1)S(1)}, bf16[8,40,640]{2,1,0:T(8,128)(2,1)S(1)}, u32[]{:S(2)}, u32[]{:S(2)}) collective-permute-start(bf16[8,40,640]{2,1,0:T(8,128)(2,1)S(1)} %all-to-all-done.1), channel_id=1, source_target_pairs={{0,49},{1,48},{16,33},{17,32},{32,17},{33,16},{48,1},{49,0},{2,51}... | collective-permute-start | bytes 1228808 | tf_op jit(solution)/shard_map/ppermute | solution.py:287
  60.5 14.3 %collective-permute-start.1 = (bf16[8,40,640]{2,1,0:T(8,128)(2,1)}, bf16[8,40,640]{2,1,0:T(8,128)(2,1)}, u32[]{:S(2)}, u32[]{:S(2)}) collective-permute-start(bf16[8,40,640]{2,1,0:T(8,128)(2,1)} %collective-permute-done), channel_id=1, source_target_pairs={{0,49},{1,48},{16,33},{17,32},{32,17},{33,16},{48,1},{49,0},{2,51}... | collective-permute-start | bytes 1228808 | tf_op jit(solution)/shard_map/ppermute | solution.py:288
  61.6 61.0 %copy-start.6 = (f32[1280]{0:T(1024)S(1)}, f32[1280]{0:T(1024)}, u32[]{:S(2)}) copy-start(f32[1280]{0:T(1024)} %param.15) | copy-start | bytes 15364
  61.7 61.0 %copy-start.5 = (f32[3840]{0:T(1024)S(1)}, f32[3840]{0:T(1024)}, u32[]{:S(2)}) copy-start(f32[3840]{0:T(1024)} %param.17) | copy-start | bytes 46084
  61.7 61.0 %copy-start.7 = (f32[1280]{0:T(1024)S(1)}, f32[1280]{0:T(1024)}, u32[]{:S(2)}) copy-start(f32[1280]{0:T(1024)} %param.19) | copy-start | bytes 15364
  61.7 61.0 %copy-start.8 = (f32[1280]{0:T(1024)S(1)}, f32[1280]{0:T(1024)}, u32[]{:S(2)}) copy-start(f32[1280]{0:T(1024)} %param.20) | copy-start | bytes 15364
  61.7 85.2 %copy-start.1 = (s32[16]{0:T(128)S(1)}, s32[16]{0:T(128)}, u32[]{:S(2)}) copy-start(s32[16]{0:T(128)} %get-tuple-element.7.table) | copy-start | bytes 196
  61.8 22.4 %collective-permute-start.3 = (bf16[640,640]{1,0:T(8,128)(2,1)S(1)}, bf16[640,640]{1,0:T(8,128)(2,1)S(1)}, u32[]{:S(2)}, u32[]{:S(2)}) collective-permute-start(bf16[640,640]{1,0:T(8,128)(2,1)S(1)} %bitcast.16), channel_id=1, source_target_pairs={{0,64},{64,128},{128,192},{192,0},{1,65},{65,129},{129,193},{193,1... | collective-permute-start | bytes 2457608 | tf_op jit(solution)/shard_map/ppermute | solution.py:295
  63.4 21.0 %collective-permute-start.5 = (bf16[640,640]{1,0:T(8,128)(2,1)S(1)}, bf16[640,640]{1,0:T(8,128)(2,1)S(1)}, u32[]{:S(2)}, u32[]{:S(2)}) collective-permute-start(bf16[640,640]{1,0:T(8,128)(2,1)S(1)} %bitcast.17), channel_id=1, source_target_pairs={{0,192},{64,0},{128,64},{192,128},{1,193},{65,1},{129,65},{193,129... | collective-permute-start | bytes 2457608 | tf_op jit(solution)/shard_map/ppermute | solution.py:295
  65.1 21.0 %collective-permute-start.9 = (bf16[640,640]{1,0:T(8,128)(2,1)S(1)}, bf16[640,640]{1,0:T(8,128)(2,1)S(1)}, u32[]{:S(2)}, u32[]{:S(2)}) collective-permute-start(bf16[640,640]{1,0:T(8,128)(2,1)S(1)} %bitcast.18), channel_id=1, source_target_pairs={{0,1},{1,0},{2,3},{3,2},{4,5},{5,4},{6,7},{7,6},{8,9},{9,8},{10,11... | collective-permute-start | bytes 2457608 | tf_op jit(solution)/shard_map/ppermute | solution.py:299
  76.0 25.7 %collective-permute-start.6 = (bf16[640,640]{1,0:T(8,128)(2,1)S(1)}, bf16[640,640]{1,0:T(8,128)(2,1)}, u32[]{:S(2)}, u32[]{:S(2)}) collective-permute-start(bf16[640,640]{1,0:T(8,128)(2,1)S(1)} %bitcast.20), channel_id=1, source_target_pairs={{0,192},{64,0},{128,64},{192,128},{1,193},{65,1},{129,65},{193,129... | collective-permute-start | bytes 2457608 | tf_op jit(solution)/shard_map/ppermute | solution.py:296
  79.1 25.6 %collective-permute-start.4 = (bf16[640,640]{1,0:T(8,128)(2,1)S(1)}, bf16[640,640]{1,0:T(8,128)(2,1)}, u32[]{:S(2)}, u32[]{:S(2)}) collective-permute-start(bf16[640,640]{1,0:T(8,128)(2,1)S(1)} %bitcast.21), channel_id=1, source_target_pairs={{0,64},{64,128},{128,192},{192,0},{1,65},{65,129},{129,193},{193,1... | collective-permute-start | bytes 2457608 | tf_op jit(solution)/shard_map/ppermute | solution.py:296
  84.2 20.5 %collective-permute-start.10 = (bf16[640,640]{1,0:T(8,128)(2,1)S(1)}, bf16[640,640]{1,0:T(8,128)(2,1)S(1)}, u32[]{:S(2)}, u32[]{:S(2)}) collective-permute-start(bf16[640,640]{1,0:T(8,128)(2,1)S(1)} %bitcast.22), channel_id=1, source_target_pairs={{0,1},{1,0},{2,3},{3,2},{4,5},{5,4},{6,7},{7,6},{8,9},{9,8},{10,11... | collective-permute-start | bytes 2457608 | tf_op jit(solution)/shard_map/ppermute | solution.py:299
  84.5 34.7 %collective-permute-start.7 = (bf16[640,640]{1,0:T(8,128)(2,1)S(1)}, bf16[640,640]{1,0:T(8,128)(2,1)}, u32[]{:S(2)}, u32[]{:S(2)}) collective-permute-start(bf16[640,640]{1,0:T(8,128)(2,1)S(1)} %collective-permute-done.3.rest_2_), channel_id=1, source_target_pairs={{0,64},{64,128},{128,192},{192,0},{1,65},{65,129},{129,193},{193,1... | collective-permute-start | bytes 2457608 | tf_op jit(solution)/shard_map/ppermute | solution.py:297
  86.1 33.2 %collective-permute-start.11 = (bf16[640,640]{1,0:T(8,128)(2,1)S(1)}, bf16[640,640]{1,0:T(8,128)(2,1)S(1)}, u32[]{:S(2)}, u32[]{:S(2)}) collective-permute-start(bf16[640,640]{1,0:T(8,128)(2,1)S(1)} %collective-permute-done.3.rest_2_), channel_id=1, source_target_pairs={{0,1},{1,0},{2,3},{3,2},{4,5},{5,4},{6,7},{7,6},{8,9},{9,8},{10,11... | collective-permute-start | bytes 2457608 | tf_op jit(solution)/shard_map/ppermute | solution.py:299
  101.7 20.8 %collective-permute-start.8 = (bf16[640,640]{1,0:T(8,128)(2,1)}, bf16[640,640]{1,0:T(8,128)(2,1)}, u32[]{:S(2)}, u32[]{:S(2)}) collective-permute-start(bf16[640,640]{1,0:T(8,128)(2,1)} %collective-permute-done.6.rest_5_), channel_id=1, source_target_pairs={{0,192},{64,0},{128,64},{192,128},{1,193},{65,1},{129,65},{193,129... | collective-permute-start | bytes 2457608 | tf_op jit(solution)/shard_map/ppermute | solution.py:297
  104.7 18.1 %collective-permute-start.13 = (bf16[640,640]{1,0:T(8,128)(2,1)S(1)}, bf16[640,640]{1,0:T(8,128)(2,1)}, u32[]{:S(2)}, u32[]{:S(2)}) collective-permute-start(bf16[640,640]{1,0:T(8,128)(2,1)S(1)} %collective-permute-done.5.rest_4_), channel_id=1, source_target_pairs={{0,1},{1,0},{2,3},{3,2},{4,5},{5,4},{6,7},{7,6},{8,9},{9,8},{10,11... | collective-permute-start | bytes 2457608 | tf_op jit(solution)/shard_map/ppermute | solution.py:299
  104.7 18.1 %collective-permute-start.14 = (bf16[640,640]{1,0:T(8,128)(2,1)}, bf16[640,640]{1,0:T(8,128)(2,1)}, u32[]{:S(2)}, u32[]{:S(2)}) collective-permute-start(bf16[640,640]{1,0:T(8,128)(2,1)} %collective-permute-done.6.rest_5_), channel_id=1, source_target_pairs={{0,1},{1,0},{2,3},{3,2},{4,5},{5,4},{6,7},{7,6},{8,9},{9,8},{10,11... | collective-permute-start | bytes 2457608 | tf_op jit(solution)/shard_map/ppermute | solution.py:299
  119.2 3.6 %collective-permute-start.12 = (bf16[640,640]{1,0:T(8,128)(2,1)}, bf16[640,640]{1,0:T(8,128)(2,1)}, u32[]{:S(2)}, u32[]{:S(2)}) collective-permute-start(bf16[640,640]{1,0:T(8,128)(2,1)} %collective-permute-done.4.rest_3_), channel_id=1, source_target_pairs={{0,1},{1,0},{2,3},{3,2},{4,5},{5,4},{6,7},{7,6},{8,9},{9,8},{10,11... | collective-permute-start | bytes 2457608 | tf_op jit(solution)/shard_map/ppermute | solution.py:299
  119.2 3.8 %collective-permute-start.15 = (bf16[640,640]{1,0:T(8,128)(2,1)}, bf16[640,640]{1,0:T(8,128)(2,1)}, u32[]{:S(2)}, u32[]{:S(2)}) collective-permute-start(bf16[640,640]{1,0:T(8,128)(2,1)} %collective-permute-done.7.rest_6_), channel_id=1, source_target_pairs={{0,1},{1,0},{2,3},{3,2},{4,5},{5,4},{6,7},{7,6},{8,9},{9,8},{10,11... | collective-permute-start | bytes 2457608 | tf_op jit(solution)/shard_map/ppermute | solution.py:299
  122.5 2.7 %collective-permute-start.16 = (bf16[640,640]{1,0:T(8,128)(2,1)}, bf16[640,640]{1,0:T(8,128)(2,1)}, u32[]{:S(2)}, u32[]{:S(2)}) collective-permute-start(bf16[640,640]{1,0:T(8,128)(2,1)} %collective-permute-done.8.rest_7_), channel_id=1, source_target_pairs={{0,1},{1,0},{2,3},{3,2},{4,5},{5,4},{6,7},{7,6},{8,9},{9,8},{10,11... | collective-permute-start | bytes 2457608 | tf_op jit(solution)/shard_map/ppermute | solution.py:299
  (4 other events, 112.4 us)

commit v8 on v7

--- a/solution.py
+++ b/solution.py
@@ -29,6 +29,11 @@
 BF16 = jnp.bfloat16
 
 
+def slot_of(device):
+    xh, z = lax.shift_right_logical(device, 4), jnp.bitwise_and(lax.shift_right_logical(device, 1), 7)
+    return 4 * z + 2 * xh + jnp.bitwise_and(device, 1)
+
+
 def outgoing_kernel(place, counts, perm, groups, patches, out, table, staged, in_sem, out_sem):
     pos = place[0]
     mine = counts[pos]
@@ -48,7 +53,7 @@
     begin = lax.fori_loop(0, N_DEV, add, jnp.int32(0))
 
     def save(i):
-        slot = perm[jnp.bitwise_and(begin + i, N_DEV - 1)]
+        slot = slot_of(perm[jnp.bitwise_and(begin + i, N_DEV - 1)])
         return pltpu.make_async_copy(staged.at[i], out.at[slot], out_sem.at[i])
 
     for i in range(SRC_WIN):
@@ -70,7 +75,7 @@
         @pl.when(within < count)
         def _():
             slot = lax.shift_right_logical(before + within, 5)
-            table[slot] = d
+            table[slot] = slot_of(d)
             table[DST_WIN + slot] = 4 * groups[d * SRC_WIN + within]
 
         return before + count
@@ -325,7 +330,7 @@
     )
     pieces, placed = spread_weights(column, side)
     place = jnp.stack(placed).astype(jnp.int32)
-    arrived = lax.all_to_all(going, ("xh", "z", "c"), split_axis=0, concat_axis=0, tiled=True)
+    arrived = lax.all_to_all(going, ("z", "xh", "c"), split_axis=0, concat_axis=0, tiled=True)
     packed = encode(
         place,
         table,

time: 204 us -> 205 us (level)
  starting transfers between devices: 27.9 us -> 36.3 us
  waiting for transfers between devices: 109 us -> 103 us
    ppermute x1, starting transfers between devices: 0.01 us -> 8.52 us  [spread_weights(): across_partner = send(partner, ('xl', 'xh', 'c'), CROSS3)]
    all_to_all x1, waiting for transfers between devices: 21.7 us -> 18.4 us  [body(): lax.all_to_all(going, ('z', 'xh', 'c'), split_axis=0, concat_axis=0, tile...]
    ppermute x1, waiting for transfers between devices: 2.69 us -> 0.53 us  [spread_weights(): send(down_a, 'y', shift(4, -1))]
  transfers between devices with their start and end apart: 19 -> 19, of which waited for: 11 -> 12; matrix products, arithmetic and copies ran while one was open for 2% -> 2% of each run, Pallas kernels for 2% -> 2%
where the time goes in v8:
time: 205 us; the launch traced here: 204 us
  waiting for transfers between devices  103 us (50%)
  blocking collectives  38.2 us (19%)
  starting transfers between devices  36.3 us (18%)
  Pallas kernels  18.9 us (9%)
  local copies, waits for them, and re-layouts  4.01 us (2%)
  other arithmetic  3.24 us (2%)
    all_to_all x1, blocking collectives, body(): lax.all_to_all(packed, ('y', 'xl'), split_axis=0, concat_axis=0, tiled=True)  38.2 us
    ppermute x1, waiting for transfers between devices, spread_weights(): partner = send(column, ('xl', 'c'), CROSS)  26.3 us
    all_to_all x1, waiting for transfers between devices, body(): lax.all_to_all(going, ('z', 'xh', 'c'), split_axis=0, concat_axis=0, tile...  18.4 us
    pallas_call x1, Pallas kernels, encode(): pl.pallas_call(encode_kernel, out_shape=jax.ShapeDtypeStruct((N_SEC * CAP...  15.3 us
    ppermute x1, waiting for transfers between devices, spread_weights(): send(up_h, 'y', shift(4, 1))  15 us
    ppermute x1, waiting for transfers between devices, spread_weights(): send(across, 'y', shift(4, -1))  14.5 us
    ppermute x1, waiting for transfers between devices, spread_weights(): across_partner = send(partner, ('xl', 'xh', 'c'), CROSS3)  11.2 us
    all_to_all x1, waiting for transfers between devices, gather_weights(): lax.all_to_all(jnp.broadcast_to(own[None], (8, 40, CHUNK)), 'z', 0, 0, ti...  10 us
  transfers between devices with their start and end apart: 19, of which 12 were waited for; matrix products, arithmetic and copies ran while one was open for 2% of the time, Pallas kernels for 2%

profile of v8, /device:TPU:4, one launch (start us, length us, event | category | flops | bytes accessed | tf_op | source)
XLA Modules:
  0.0 204.2 jit_solution(14348769667057000583)
XLA Ops:
  1.6 8.5 %all-to-all-start.1 = ((bf16[8,40,640]{2,1,0:T(8,128)(2,1)}), bf16[8,40,640]{2,1,0:T(8,128)(2,1)S(1)}, u32[]{:S(2)}, u32[]{:S(2)}) async-start(bf16[8,40,640]{2,1,0:T(8,128)(2,1)} %broadcast_in_dim.2), calls=%async_computation.1 | async-start | bytes 819200 | tf_op jit(solution)/shard_map/all_to_all | solution.py:284
  11.6 3.6 %outgoing.1 = (bf16[32,64,1280]{2,1,0:T(8,128)(2,1)}, s32[16]{0:T(128)}) custom-call(s32[1]{0:T(128)} %bitcast.6.place, s32[32]{0:T(128)} %bitcast.29, s32[32]{0:T(128)} %bitcast.30, s32[768]{0:T(1024)} %reshape.41.groups, bf16[24,64,1280]{2,1,0:T(8,128)(2,1)} %bitcast.28), custom_call_target="tpu_custom_call" | custom-call | tf_op jit(solution)/shard_map/outgoing/pallas_call | solution.py:94
  15.1 10.0 %all-to-all-done.1 = bf16[8,40,640]{2,1,0:T(8,128)(2,1)S(1)} async-done(((bf16[8,40,640]{2,1,0:T(8,128)(2,1)}), bf16[8,40,640]{2,1,0:T(8,128)(2,1)S(1)}, u32[]{:S(2)}, u32[]{:S(2)}) %all-to-all-start.1) | async-done | bytes 409632 | tf_op jit(solution)/shard_map/all_to_all | solution.py:284
  25.1 5.0 %all-to-all-start = ((bf16[32,64,1280]{2,1,0:T(8,128)(2,1)}), bf16[32,64,1280]{2,1,0:T(8,128)(2,1)}, u32[]{:S(2)}, u32[]{:S(2)}) async-start(bf16[32,64,1280]{2,1,0:T(8,128)(2,1)} %get-tuple-element.8), calls=%async_computation | async-start | bytes 10485760 | tf_op jit(solution)/shard_map/all_to_all | solution.py:333
  30.2 1.9 collective-permute-start
  32.1 26.3 %collective-permute-done = bf16[8,40,640]{2,1,0:T(8,128)(2,1)} collective-permute-done((bf16[8,40,640]{2,1,0:T(8,128)(2,1)S(1)}, bf16[8,40,640]{2,1,0:T(8,128)(2,1)}, u32[]{:S(2)}, u32[]{:S(2)}) %collective-permute-start) | collective-permute-done | bytes 409632 | tf_op jit(solution)/shard_map/ppermute | solution.py:291
  58.4 8.5 %collective-permute-start.1 = (bf16[8,40,640]{2,1,0:T(8,128)(2,1)}, bf16[8,40,640]{2,1,0:T(8,128)(2,1)}, u32[]{:S(2)}, u32[]{:S(2)}) collective-permute-start(bf16[8,40,640]{2,1,0:T(8,128)(2,1)} %collective-permute-done), channel_id=1, source_target_pairs={{0,49},{1,48},{16,33},{17,32},{32,17},{33,16},{48,1},{49,0},{2,51}... | collective-permute-start | bytes 1228808 | tf_op jit(solution)/shard_map/ppermute | solution.py:293
  66.9 1.1 broadcast_select_fusion.3
  68.2 1.7 collective-permute-start.3
  69.9 1.7 collective-permute-start.5
  71.5 11.2 %collective-permute-done.1 = bf16[8,40,640]{2,1,0:T(8,128)(2,1)} collective-permute-done((bf16[8,40,640]{2,1,0:T(8,128)(2,1)}, bf16[8,40,640]{2,1,0:T(8,128)(2,1)}, u32[]{:S(2)}, u32[]{:S(2)}) %collective-permute-start.1) | collective-permute-done | bytes 409632 | tf_op jit(solution)/shard_map/ppermute | solution.py:293
  83.9 3.1 %collective-permute-start.6 = (bf16[640,640]{1,0:T(8,128)(2,1)S(1)}, bf16[640,640]{1,0:T(8,128)(2,1)}, u32[]{:S(2)}, u32[]{:S(2)}) collective-permute-start(bf16[640,640]{1,0:T(8,128)(2,1)S(1)} %bitcast.20), channel_id=1, source_target_pairs={{0,192},{64,0},{128,64},{192,128},{1,193},{65,1},{129,65},{193,129... | collective-permute-start | bytes 2457608 | tf_op jit(solution)/shard_map/ppermute | solution.py:301
  87.0 2.5 %collective-permute-done.3.rest_2_ = bf16[640,640]{1,0:T(8,128)(2,1)S(1)} collective-permute-done((bf16[640,640]{1,0:T(8,128)(2,1)S(1)}, bf16[640,640]{1,0:T(8,128)(2,1)S(1)}, u32[]{:S(2)}, u32[]{:S(2)}) %collective-permute-start.3) | collective-permute-done | bytes 819232 | tf_op jit(solution)/shard_map/ppermute | solution.py:300
  89.5 1.6 collective-permute-done.5.rest_4_
  91.1 1.6 collective-permute-start.7
  92.6 14.5 %collective-permute-done.6.rest_5_ = bf16[640,640]{1,0:T(8,128)(2,1)} collective-permute-done((bf16[640,640]{1,0:T(8,128)(2,1)S(1)}, bf16[640,640]{1,0:T(8,128)(2,1)}, u32[]{:S(2)}, u32[]{:S(2)}) %collective-permute-start.6) | collective-permute-done | bytes 819232 | tf_op jit(solution)/shard_map/ppermute | solution.py:301
  107.2 3.0 %collective-permute-start.8 = (bf16[640,640]{1,0:T(8,128)(2,1)}, bf16[640,640]{1,0:T(8,128)(2,1)}, u32[]{:S(2)}, u32[]{:S(2)}) collective-permute-start(bf16[640,640]{1,0:T(8,128)(2,1)} %collective-permute-done.6.rest_5_), channel_id=1, source_target_pairs={{0,192},{64,0},{128,64},{192,128},{1,193},{65,1},{129,65},{193,129... | collective-permute-start | bytes 2457608 | tf_op jit(solution)/shard_map/ppermute | solution.py:302
  110.7 15.0 %collective-permute-done.7.rest_6_ = bf16[640,640]{1,0:T(8,128)(2,1)} collective-permute-done((bf16[640,640]{1,0:T(8,128)(2,1)S(1)}, bf16[640,640]{1,0:T(8,128)(2,1)}, u32[]{:S(2)}, u32[]{:S(2)}) %collective-permute-start.7) | collective-permute-done | bytes 819232 | tf_op jit(solution)/shard_map/ppermute | solution.py:302
  128.4 1.2 collective-permute-done.15.rest_14_
  129.6 1.2 collective-permute-done.16.rest_15_
  130.8 18.4 %all-to-all-done.arrived = bf16[32,64,1280]{2,1,0:T(8,128)(2,1)} async-done(((bf16[32,64,1280]{2,1,0:T(8,128)(2,1)}), bf16[32,64,1280]{2,1,0:T(8,128)(2,1)}, u32[]{:S(2)}, u32[]{:S(2)}) %all-to-all-start) | async-done | bytes 5242912 | tf_op jit(solution)/shard_map/all_to_all | solution.py:333
  149.1 15.3 %encode.1 = bf16[256,5120]{1,0:T(8,128)(2,1)} custom-call(s32[6]{0:T(128)S(1)} %stack.27.place, s32[16]{0:T(128)S(1)} %copy-done.1, s32[1,128]{1,0:T(1,128)S(1)} %bitcast.25, s32[128,1]{1,0:T(8,128)S(1)} %copy.14.owner_column, f32[1,1280]{1,0:T(1,128)S(1)} %reshape.45.norm_gain, f32[3,1,1280]{2,1,0:T(1,128)S(1)} %reshape.46.qkv_bias, ...), custom_call_target="tpu_custom_call" | custom-call | tf_op jit(solution)/shard_map/encode/pallas_call | solution.py:244
  164.5 38.2 %all_to_all.19 = bf16[8,32,5120]{2,1,0:T(8,128)(2,1)S(1)} all-to-all(bf16[8,32,5120]{2,1,0:T(8,128)(2,1)} %bitcast.26), channel_id=1, replica_groups=mesh['y'=4,'xl'=2,'xh'=2,'z'=8,'c'=2] {'y','xl'}, dimensions={0} | all-to-all | bytes 5242880 | tf_op jit(solution)/shard_map/all_to_all | solution.py:346
  202.7 1.5 copy.16
  (50 shorter events, 7.5 us)
Async XLA Ops:
  1.6 23.5 %all-to-all-start.1 = ((bf16[8,40,640]{2,1,0:T(8,128)(2,1)}), bf16[8,40,640]{2,1,0:T(8,128)(2,1)S(1)}, u32[]{:S(2)}, u32[]{:S(2)}) async-start(bf16[8,40,640]{2,1,0:T(8,128)(2,1)} %broadcast_in_dim.2), calls=%async_computation.1 | async-start | bytes 819200 | tf_op jit(solution)/shard_map/all_to_all | solution.py:284
  25.1 124.0 %all-to-all-start = ((bf16[32,64,1280]{2,1,0:T(8,128)(2,1)}), bf16[32,64,1280]{2,1,0:T(8,128)(2,1)}, u32[]{:S(2)}, u32[]{:S(2)}) async-start(bf16[32,64,1280]{2,1,0:T(8,128)(2,1)} %get-tuple-element.8), calls=%async_computation | async-start | bytes 10485760 | tf_op jit(solution)/shard_map/all_to_all | solution.py:333
  30.2 28.3 %collective-permute-start = (bf16[8,40,640]{2,1,0:T(8,128)(2,1)S(1)}, bf16[8,40,640]{2,1,0:T(8,128)(2,1)}, u32[]{:S(2)}, u32[]{:S(2)}) collective-permute-start(bf16[8,40,640]{2,1,0:T(8,128)(2,1)S(1)} %all-to-all-done.1), channel_id=1, source_target_pairs={{0,33},{1,32},{32,1},{33,0},{2,35},{3,34},{34,3},{35,2},{4,37},{5,... | collective-permute-start | bytes 1228808 | tf_op jit(solution)/shard_map/ppermute | solution.py:291
  32.1 39.5 %collective-permute-start.2 = (bf16[8,40,640]{2,1,0:T(8,128)(2,1)S(1)}, bf16[8,40,640]{2,1,0:T(8,128)(2,1)S(1)}, u32[]{:S(2)}, u32[]{:S(2)}) collective-permute-start(bf16[8,40,640]{2,1,0:T(8,128)(2,1)S(1)} %all-to-all-done.1), channel_id=1, source_target_pairs={{0,49},{1,48},{16,33},{17,32},{32,17},{33,16},{48,1},{49,0},{2,51}... | collective-permute-start | bytes 1228808 | tf_op jit(solution)/shard_map/ppermute | solution.py:292
  58.4 24.3 %collective-permute-start.1 = (bf16[8,40,640]{2,1,0:T(8,128)(2,1)}, bf16[8,40,640]{2,1,0:T(8,128)(2,1)}, u32[]{:S(2)}, u32[]{:S(2)}) collective-permute-start(bf16[8,40,640]{2,1,0:T(8,128)(2,1)} %collective-permute-done), channel_id=1, source_target_pairs={{0,49},{1,48},{16,33},{17,32},{32,17},{33,16},{48,1},{49,0},{2,51}... | collective-permute-start | bytes 1228808 | tf_op jit(solution)/shard_map/ppermute | solution.py:293
  68.1 59.2 %copy-start.6 = (f32[1280]{0:T(1024)S(1)}, f32[1280]{0:T(1024)}, u32[]{:S(2)}) copy-start(f32[1280]{0:T(1024)} %param.15) | copy-start | bytes 15364
  68.1 59.2 %copy-start.5 = (f32[3840]{0:T(1024)S(1)}, f32[3840]{0:T(1024)}, u32[]{:S(2)}) copy-start(f32[3840]{0:T(1024)} %param.17) | copy-start | bytes 46084
  68.1 59.2 %copy-start.7 = (f32[1280]{0:T(1024)S(1)}, f32[1280]{0:T(1024)}, u32[]{:S(2)}) copy-start(f32[1280]{0:T(1024)} %param.19) | copy-start | bytes 15364
  68.1 59.3 %copy-start.8 = (f32[1280]{0:T(1024)S(1)}, f32[1280]{0:T(1024)}, u32[]{:S(2)}) copy-start(f32[1280]{0:T(1024)} %param.20) | copy-start | bytes 15364
  68.1 81.0 %copy-start.1 = (s32[16]{0:T(128)S(1)}, s32[16]{0:T(128)}, u32[]{:S(2)}) copy-start(s32[16]{0:T(128)} %get-tuple-element.7.table) | copy-start | bytes 196
  68.2 21.2 %collective-permute-start.3 = (bf16[640,640]{1,0:T(8,128)(2,1)S(1)}, bf16[640,640]{1,0:T(8,128)(2,1)S(1)}, u32[]{:S(2)}, u32[]{:S(2)}) collective-permute-start(bf16[640,640]{1,0:T(8,128)(2,1)S(1)} %bitcast.16), channel_id=1, source_target_pairs={{0,64},{64,128},{128,192},{192,0},{1,65},{65,129},{129,193},{193,1... | collective-permute-start | bytes 2457608 | tf_op jit(solution)/shard_map/ppermute | solution.py:300
  69.9 21.2 %collective-permute-start.5 = (bf16[640,640]{1,0:T(8,128)(2,1)S(1)}, bf16[640,640]{1,0:T(8,128)(2,1)S(1)}, u32[]{:S(2)}, u32[]{:S(2)}) collective-permute-start(bf16[640,640]{1,0:T(8,128)(2,1)S(1)} %bitcast.17), channel_id=1, source_target_pairs={{0,192},{64,0},{128,64},{192,128},{1,193},{65,1},{129,65},{193,129... | collective-permute-start | bytes 2457608 | tf_op jit(solution)/shard_map/ppermute | solution.py:300
  71.5 21.1 %collective-permute-start.9 = (bf16[640,640]{1,0:T(8,128)(2,1)S(1)}, bf16[640,640]{1,0:T(8,128)(2,1)S(1)}, u32[]{:S(2)}, u32[]{:S(2)}) collective-permute-start(bf16[640,640]{1,0:T(8,128)(2,1)S(1)} %bitcast.18), channel_id=1, source_target_pairs={{0,1},{1,0},{2,3},{3,2},{4,5},{5,4},{6,7},{7,6},{8,9},{9,8},{10,11... | collective-permute-start | bytes 2457608 | tf_op jit(solution)/shard_map/ppermute | solution.py:304
  83.9 23.3 %collective-permute-start.6 = (bf16[640,640]{1,0:T(8,128)(2,1)S(1)}, bf16[640,640]{1,0:T(8,128)(2,1)}, u32[]{:S(2)}, u32[]{:S(2)}) collective-permute-start(bf16[640,640]{1,0:T(8,128)(2,1)S(1)} %bitcast.20), channel_id=1, source_target_pairs={{0,192},{64,0},{128,64},{192,128},{1,193},{65,1},{129,65},{193,129... | collective-permute-start | bytes 2457608 | tf_op jit(solution)/shard_map/ppermute | solution.py:301
  87.0 23.2 %collective-permute-start.4 = (bf16[640,640]{1,0:T(8,128)(2,1)S(1)}, bf16[640,640]{1,0:T(8,128)(2,1)}, u32[]{:S(2)}, u32[]{:S(2)}) collective-permute-start(bf16[640,640]{1,0:T(8,128)(2,1)S(1)} %bitcast.21), channel_id=1, source_target_pairs={{0,64},{64,128},{128,192},{192,0},{1,65},{65,129},{129,193},{193,1... | collective-permute-start | bytes 2457608 | tf_op jit(solution)/shard_map/ppermute | solution.py:301
  89.5 20.7 %collective-permute-start.10 = (bf16[640,640]{1,0:T(8,128)(2,1)S(1)}, bf16[640,640]{1,0:T(8,128)(2,1)S(1)}, u32[]{:S(2)}, u32[]{:S(2)}) collective-permute-start(bf16[640,640]{1,0:T(8,128)(2,1)S(1)} %bitcast.22), channel_id=1, source_target_pairs={{0,1},{1,0},{2,3},{3,2},{4,5},{5,4},{6,7},{7,6},{8,9},{9,8},{10,11... | collective-permute-start | bytes 2457608 | tf_op jit(solution)/shard_map/ppermute | solution.py:304
  91.1 34.7 %collective-permute-start.7 = (bf16[640,640]{1,0:T(8,128)(2,1)S(1)}, bf16[640,640]{1,0:T(8,128)(2,1)}, u32[]{:S(2)}, u32[]{:S(2)}) collective-permute-start(bf16[640,640]{1,0:T(8,128)(2,1)S(1)} %collective-permute-done.3.rest_2_), channel_id=1, source_target_pairs={{0,64},{64,128},{128,192},{192,0},{1,65},{65,129},{129,193},{193,1... | collective-permute-start | bytes 2457608 | tf_op jit(solution)/shard_map/ppermute | solution.py:302
  92.6 33.1 %collective-permute-start.11 = (bf16[640,640]{1,0:T(8,128)(2,1)S(1)}, bf16[640,640]{1,0:T(8,128)(2,1)S(1)}, u32[]{:S(2)}, u32[]{:S(2)}) collective-permute-start(bf16[640,640]{1,0:T(8,128)(2,1)S(1)} %collective-permute-done.3.rest_2_), channel_id=1, source_target_pairs={{0,1},{1,0},{2,3},{3,2},{4,5},{5,4},{6,7},{7,6},{8,9},{9,8},{10,11... | collective-permute-start | bytes 2457608 | tf_op jit(solution)/shard_map/ppermute | solution.py:304
  107.2 19.7 %collective-permute-start.8 = (bf16[640,640]{1,0:T(8,128)(2,1)}, bf16[640,640]{1,0:T(8,128)(2,1)}, u32[]{:S(2)}, u32[]{:S(2)}) collective-permute-start(bf16[640,640]{1,0:T(8,128)(2,1)} %collective-permute-done.6.rest_5_), channel_id=1, source_target_pairs={{0,192},{64,0},{128,64},{192,128},{1,193},{65,1},{129,65},{193,129... | collective-permute-start | bytes 2457608 | tf_op jit(solution)/shard_map/ppermute | solution.py:302
  110.2 17.3 %collective-permute-start.13 = (bf16[640,640]{1,0:T(8,128)(2,1)S(1)}, bf16[640,640]{1,0:T(8,128)(2,1)}, u32[]{:S(2)}, u32[]{:S(2)}) collective-permute-start(bf16[640,640]{1,0:T(8,128)(2,1)S(1)} %collective-permute-done.5.rest_4_), channel_id=1, source_target_pairs={{0,1},{1,0},{2,3},{3,2},{4,5},{5,4},{6,7},{7,6},{8,9},{9,8},{10,11... | collective-permute-start | bytes 2457608 | tf_op jit(solution)/shard_map/ppermute | solution.py:304
  110.2 18.2 %collective-permute-start.14 = (bf16[640,640]{1,0:T(8,128)(2,1)}, bf16[640,640]{1,0:T(8,128)(2,1)}, u32[]{:S(2)}, u32[]{:S(2)}) collective-permute-start(bf16[640,640]{1,0:T(8,128)(2,1)} %collective-permute-done.6.rest_5_), channel_id=1, source_target_pairs={{0,1},{1,0},{2,3},{3,2},{4,5},{5,4},{6,7},{7,6},{8,9},{9,8},{10,11... | collective-permute-start | bytes 2457608 | tf_op jit(solution)/shard_map/ppermute | solution.py:304
  125.7 2.7 %collective-permute-start.12 = (bf16[640,640]{1,0:T(8,128)(2,1)}, bf16[640,640]{1,0:T(8,128)(2,1)}, u32[]{:S(2)}, u32[]{:S(2)}) collective-permute-start(bf16[640,640]{1,0:T(8,128)(2,1)} %collective-permute-done.4.rest_3_), channel_id=1, source_target_pairs={{0,1},{1,0},{2,3},{3,2},{4,5},{5,4},{6,7},{7,6},{8,9},{9,8},{10,11... | collective-permute-start | bytes 2457608 | tf_op jit(solution)/shard_map/ppermute | solution.py:304
  125.8 3.8 %collective-permute-start.15 = (bf16[640,640]{1,0:T(8,128)(2,1)}, bf16[640,640]{1,0:T(8,128)(2,1)}, u32[]{:S(2)}, u32[]{:S(2)}) collective-permute-start(bf16[640,640]{1,0:T(8,128)(2,1)} %collective-permute-done.7.rest_6_), channel_id=1, source_target_pairs={{0,1},{1,0},{2,3},{3,2},{4,5},{5,4},{6,7},{7,6},{8,9},{9,8},{10,11... | collective-permute-start | bytes 2457608 | tf_op jit(solution)/shard_map/ppermute | solution.py:304
  126.9 3.9 %collective-permute-start.16 = (bf16[640,640]{1,0:T(8,128)(2,1)}, bf16[640,640]{1,0:T(8,128)(2,1)}, u32[]{:S(2)}, u32[]{:S(2)}) collective-permute-start(bf16[640,640]{1,0:T(8,128)(2,1)} %collective-permute-done.8.rest_7_), channel_id=1, source_target_pairs={{0,1},{1,0},{2,3},{3,2},{4,5},{5,4},{6,7},{7,6},{8,9},{9,8},{10,11... | collective-permute-start | bytes 2457608 | tf_op jit(solution)/shard_map/ppermute | solution.py:304
  (4 other events, 109.5 us)
